TPU v7x, 32 devices: a whole 2x2x4 slice. The times are simulated.
32 devices in a mesh: dp: 8 (over y, x, core), fsdp: 4 (over z).
Axes of the slice: x: 2, y: 2, z: 4, core: 2. Of those that a mesh axis runs over, the one named last changes fastest.
Arguments:
- tokens: bfloat16 [46400, 1024], P(('dp', 'fsdp')), may hold values from -6 to 6
- output_grad: bfloat16 [46400, 1024], P(('dp', 'fsdp')), may hold values from -6 to 6
- group_member: int32 [8], P('dp'), may hold values from 0 to 1, as said below
- image_counts: int32 [2], replicated, may hold values from 64 to 4095
- position_source: int32 [145, 4], replicated, may hold values from 0 to 49
- position_table: bfloat16 [50, 1024], P(None, 'fsdp'), may hold values from -3 to 3
- first_gain: bfloat16 [1024], P('fsdp'), may hold values from 0.5 to 1.5
- first_shift: bfloat16 [1024], P('fsdp'), may hold values from -1 to 1
- input_proj: bfloat16 [1024, 3072], P('fsdp'), may hold values from -0.1875 to 0.1875
- query_bias: bfloat16 [1024], P('fsdp'), may hold values from -1 to 1
- value_bias: bfloat16 [1024], P('fsdp'), may hold values from -1 to 1
- output_proj: bfloat16 [1024, 1024], P('fsdp'), may hold values from -0.75 to 0.75
- output_bias: bfloat16 [1024], P('fsdp'), may hold values from -1 to 1
- second_gain: bfloat16 [1024], P('fsdp'), may hold values from 0.5 to 1.5
- second_shift: bfloat16 [1024], P('fsdp'), may hold values from -1 to 1
- hidden_weight: bfloat16 [1024, 4096], P('fsdp'), may hold values from -0.1875 to 0.1875
- hidden_bias: bfloat16 [4096], P('fsdp'), may hold values from -1 to 1
- return_weight: bfloat16 [4096, 1024], P('fsdp'), may hold values from -0.09375 to 0.09375
- return_bias: bfloat16 [1024], P('fsdp'), may hold values from -1 to 1
Outputs:
- block_out: bfloat16 [46400, 1024], P(('dp', 'fsdp'))
- tokens_grad: bfloat16 [46400, 1024], P(('dp', 'fsdp'))
- table_grad: float32 [50, 1024], P(None, 'fsdp')
- first_gain_grad: float32 [1024], P('fsdp')
- first_shift_grad: float32 [1024], P('fsdp')
- input_proj_grad: float32 [1024, 3072], P('fsdp')
- query_bias_grad: float32 [1024], P('fsdp')
- value_bias_grad: float32 [1024], P('fsdp')
- output_proj_grad: float32 [1024, 1024], P('fsdp')
- output_bias_grad: float32 [1024], P('fsdp')
- second_gain_grad: float32 [1024], P('fsdp')
- second_shift_grad: float32 [1024], P('fsdp')
- hidden_weight_grad: float32 [1024, 4096], P('fsdp')
- hidden_bias_grad: float32 [4096], P('fsdp')
- return_weight_grad: float32 [4096, 1024], P('fsdp')
- return_bias_grad: float32 [1024], P('fsdp')
Inputs may be any that keep to these rules, and one draw needn't show every extreme that they name: `group_member`: exactly 3 entries are 1, the others 0.
All inputs are finite; a program needn't handle non-finite values.
Results may differ from a plain program's by a relative error of at most 0.02.
Values may be sent and summed in bfloat16 or wider, within the bound.
No kernel may reach another device: no remote copies, remote signals or barrier semaphores. Data moves between devices by JAX's collectives and lax.ppermute only.
A program may use at most 320 MiB of HBM per device.

v0:
```python
from functools import partial
import math

import jax
import jax.numpy as jnp
from jax import lax
from jax.sharding import PartitionSpec as P

D = 1024
HEADS = 16
HEAD_DIM = 64
SG = 7
LG = 12
SMALL_LEN = 50
LARGE_LEN = 145
ROWS = 1450


EPS = 1e-06


def shortened(value):
    return jax.tree.map(lambda a: a.astype(jnp.bfloat16) if a.dtype == jnp.float32 else a, value)


def grid_fraction(index):
    scaled = jnp.maximum((2 * index + 1) * SG - LG, 0)
    lower = scaled // (2 * LG)
    return (scaled - 2 * LG * lower).astype(jnp.float32) / (2.0 * LG)


def interp_table(position_source):
    position = jnp.arange(LARGE_LEN, dtype=jnp.int32)
    patch = jnp.maximum(position - 1, 0)
    frac_row = grid_fraction(patch // LG)
    frac_col = grid_fraction(patch % LG)
    weights = jnp.stack(
        [
            (1.0 - frac_row) * (1.0 - frac_col),
            (1.0 - frac_row) * frac_col,
            frac_row * (1.0 - frac_col),
            frac_row * frac_col,
        ],
        axis=1,
    )
    class_row = (jnp.arange(4, dtype=jnp.int32) == 0).astype(jnp.float32)
    weights = jnp.where((position == 0)[:, None], class_row[None, :], weights)
    onehot = (
        position_source[:, :, None] == jnp.arange(SMALL_LEN, dtype=jnp.int32)[None, None, :]
    ).astype(jnp.float32)
    return jnp.sum(weights[:, :, None] * onehot, axis=1)


def layer_norm(values, gain, shift):
    average = jnp.mean(values, axis=-1, keepdims=True)
    centred = values - average
    variance = jnp.mean(centred * centred, axis=-1, keepdims=True)
    inv_std = lax.rsqrt(variance + EPS)
    normed = centred * inv_std
    return (normed * gain + shift, normed, inv_std)


def norm_back(grad_norm, normed, inv_std, gain):
    scaled = grad_norm * gain
    inner = (
        scaled
        - jnp.mean(scaled, axis=-1, keepdims=True)
        - normed * jnp.mean(scaled * normed, axis=-1, keepdims=True)
    )
    return (inv_std * inner, jnp.sum(grad_norm * normed, axis=0), jnp.sum(grad_norm, axis=0))


def image_scores(query_low, keys_low, length):
    images = ROWS // length
    query_img = query_low.reshape(images, length, HEADS, HEAD_DIM)
    keys_img = keys_low.reshape(images, length, HEADS, HEAD_DIM)
    logits = jnp.einsum("nqhd,nkhd->nhqk", query_img, keys_img, preferred_element_type=jnp.float32)
    return (logits / math.sqrt(HEAD_DIM), query_img, keys_img)


def attend_forward(query_low, keys_low, values_low, length):
    images = ROWS // length
    scores, _, _ = image_scores(query_low, keys_low, length)
    highest = jnp.max(scores, axis=-1, keepdims=True)
    log_total = highest + jnp.log(jnp.sum(jnp.exp(scores - highest), axis=-1, keepdims=True))
    probs = jnp.exp(scores - log_total)
    values_img = values_low.reshape(images, length, HEADS, HEAD_DIM)
    attended = jnp.einsum(
        "nhqk,nkhd->nqhd",
        probs.astype(jnp.bfloat16),
        values_img,
        preferred_element_type=jnp.float32,
    )
    lse_rows = jnp.transpose(log_total[..., 0], (0, 2, 1)).reshape(ROWS, HEADS)
    return (attended.reshape(ROWS, D).astype(jnp.bfloat16), lse_rows)


def attend_backward(query_low, keys_low, values_low, lse_rows, grad_att_low, length):
    images = ROWS // length
    scores, query_img, keys_img = image_scores(query_low, keys_low, length)
    log_total = jnp.transpose(lse_rows.reshape(images, length, HEADS), (0, 2, 1))[..., None]
    probs = jnp.exp(scores - log_total)
    values_img = values_low.reshape(images, length, HEADS, HEAD_DIM)
    grad_img = grad_att_low.reshape(images, length, HEADS, HEAD_DIM)
    grad_values = jnp.einsum(
        "nhqk,nqhd->nkhd", probs.astype(jnp.bfloat16), grad_img, preferred_element_type=jnp.float32
    )
    grad_probs = jnp.einsum(
        "nqhd,nkhd->nhqk", grad_img, values_img, preferred_element_type=jnp.float32
    )
    grad_scores = probs * (grad_probs - jnp.sum(grad_probs * probs, axis=-1, keepdims=True))
    grad_scores_low = grad_scores.astype(jnp.bfloat16)
    grad_query = jnp.einsum(
        "nhqk,nkhd->nqhd", grad_scores_low, keys_img, preferred_element_type=jnp.float32
    ) / math.sqrt(HEAD_DIM)
    grad_keys = jnp.einsum(
        "nhqk,nqhd->nkhd", grad_scores_low, query_img, preferred_element_type=jnp.float32
    ) / math.sqrt(HEAD_DIM)
    return (
        grad_query.reshape(ROWS, D).astype(jnp.bfloat16),
        grad_keys.reshape(ROWS, D).astype(jnp.bfloat16),
        grad_values.reshape(ROWS, D).astype(jnp.bfloat16),
    )


def per_device(
    tokens,
    output_grad,
    group_member,
    image_counts,
    position_source,
    position_table,
    first_gain,
    first_shift,
    input_proj,
    query_bias,
    value_bias,
    output_proj,
    output_bias,
    second_gain,
    second_shift,
    hidden_weight,
    hidden_bias,
    return_weight,
    return_bias,
):
    gathered = (
        lax.all_gather(input_proj, "fsdp", axis=0, tiled=True),
        lax.all_gather(output_proj, "fsdp", axis=0, tiled=True),
        lax.all_gather(hidden_weight, "fsdp", axis=0, tiled=True),
        lax.all_gather(return_weight, "fsdp", axis=0, tiled=True),
        lax.all_gather(first_gain, "fsdp", axis=0, tiled=True),
        lax.all_gather(first_shift, "fsdp", axis=0, tiled=True),
        lax.all_gather(query_bias, "fsdp", axis=0, tiled=True),
        lax.all_gather(value_bias, "fsdp", axis=0, tiled=True),
        lax.all_gather(output_bias, "fsdp", axis=0, tiled=True),
        lax.all_gather(second_gain, "fsdp", axis=0, tiled=True),
        lax.all_gather(second_shift, "fsdp", axis=0, tiled=True),
        lax.all_gather(hidden_bias, "fsdp", axis=0, tiled=True),
        lax.all_gather(return_bias, "fsdp", axis=0, tiled=True),
        lax.all_gather(position_table, "fsdp", axis=1, tiled=True),
    )
    (
        joint_proj,
        outproj_full,
        hidden_full,
        return_full,
        gain_one,
        shift_one,
        query_add,
        value_add,
        output_add,
        gain_two,
        shift_two,
        hidden_add,
        return_add,
        table_full,
    ) = gathered
    member = group_member[0]
    is_large = member == 1
    length = jnp.where(is_large, LARGE_LEN, SMALL_LEN)
    row_index = jnp.arange(ROWS, dtype=jnp.int32)
    place = row_index % length
    inter = interp_table(position_source)
    identity = (
        jnp.arange(LARGE_LEN, dtype=jnp.int32)[:, None]
        == jnp.arange(SMALL_LEN, dtype=jnp.int32)[None, :]
    ).astype(jnp.float32)
    mixing = jnp.where(is_large, inter, identity)
    picker = (place[:, None] == jnp.arange(LARGE_LEN, dtype=jnp.int32)[None, :]).astype(jnp.float32)
    spread = jnp.dot(picker, mixing, precision=lax.Precision.HIGHEST)
    position = jnp.dot(spread, table_full.astype(jnp.float32), precision=lax.Precision.HIGHEST)
    stream = tokens.astype(jnp.float32) + position
    first_out, first_hat, first_inv = layer_norm(
        stream, gain_one.astype(jnp.float32), shift_one.astype(jnp.float32)
    )
    first_low = first_out.astype(jnp.bfloat16)
    projected = jnp.dot(first_low, joint_proj, preferred_element_type=jnp.float32)
    query_low = (projected[:, :D] + query_add.astype(jnp.float32)).astype(jnp.bfloat16)
    keys_low = projected[:, D : 2 * D].astype(jnp.bfloat16)
    values_low = (projected[:, 2 * D :] + value_add.astype(jnp.float32)).astype(jnp.bfloat16)
    attended_low, lse_rows = lax.cond(
        is_large,
        partial(attend_forward, length=LARGE_LEN),
        partial(attend_forward, length=SMALL_LEN),
        query_low,
        keys_low,
        values_low,
    )
    mid = (
        stream
        + jnp.dot(attended_low, outproj_full, preferred_element_type=jnp.float32)
        + output_add.astype(jnp.float32)
    )
    second_out, second_hat, second_inv = layer_norm(
        mid, gain_two.astype(jnp.float32), shift_two.astype(jnp.float32)
    )
    second_low = second_out.astype(jnp.bfloat16)
    hidden_pre = jnp.dot(
        second_low, hidden_full, preferred_element_type=jnp.float32
    ) + hidden_add.astype(jnp.float32)
    activ, gelu_back = jax.vjp(partial(jax.nn.gelu, approximate=False), hidden_pre)
    activ_low = activ.astype(jnp.bfloat16)
    returned = jnp.dot(
        activ_low, return_full, preferred_element_type=jnp.float32
    ) + return_add.astype(jnp.float32)
    block_out = (mid + returned).astype(jnp.bfloat16)
    again = (
        lax.all_gather(input_proj, "fsdp", axis=0, tiled=True),
        lax.all_gather(output_proj, "fsdp", axis=0, tiled=True),
        lax.all_gather(hidden_weight, "fsdp", axis=0, tiled=True),
        lax.all_gather(return_weight, "fsdp", axis=0, tiled=True),
        lax.all_gather(first_gain, "fsdp", axis=0, tiled=True),
        lax.all_gather(second_gain, "fsdp", axis=0, tiled=True),
    )
    joint_back, outproj_back, hidden_back, return_back, gain_one_back, gain_two_back = again
    grad_out = output_grad.astype(jnp.float32)
    grad_return_w = jnp.einsum(
        "rf,rd->fd", activ_low, output_grad, preferred_element_type=jnp.float32
    )
    grad_return_add = jnp.sum(grad_out, axis=0)
    grad_activ = jnp.einsum(
        "rd,fd->rf", output_grad, return_back, preferred_element_type=jnp.float32
    )
    grad_hidden_low = gelu_back(grad_activ)[0].astype(jnp.bfloat16)
    grad_hidden_w = jnp.einsum(
        "rd,rf->df", second_low, grad_hidden_low, preferred_element_type=jnp.float32
    )
    grad_hidden_add = jnp.sum(grad_hidden_low.astype(jnp.float32), axis=0)
    grad_second = jnp.einsum(
        "rf,df->rd", grad_hidden_low, hidden_back, preferred_element_type=jnp.float32
    )
    grad_mid_norm, grad_gain_two, grad_shift_two = norm_back(
        grad_second, second_hat, second_inv, gain_two_back.astype(jnp.float32)
    )
    grad_mid = grad_out + grad_mid_norm
    grad_branch_low = grad_mid.astype(jnp.bfloat16)
    grad_outproj = jnp.einsum(
        "rd,re->de", attended_low, grad_branch_low, preferred_element_type=jnp.float32
    )
    grad_output_add = jnp.sum(grad_branch_low.astype(jnp.float32), axis=0)
    grad_attended = jnp.einsum(
        "re,de->rd", grad_branch_low, outproj_back, preferred_element_type=jnp.float32
    )
    grad_att_low = grad_attended.astype(jnp.bfloat16)
    grad_query_low, grad_keys_low, grad_values_low = lax.cond(
        is_large,
        partial(attend_backward, length=LARGE_LEN),
        partial(attend_backward, length=SMALL_LEN),
        query_low,
        keys_low,
        values_low,
        lse_rows,
        grad_att_low,
    )
    grad_joint_low = jnp.concatenate([grad_query_low, grad_keys_low, grad_values_low], axis=1)
    grad_joint = jnp.einsum(
        "rd,re->de", first_low, grad_joint_low, preferred_element_type=jnp.float32
    )
    grad_query_add = jnp.sum(grad_query_low.astype(jnp.float32), axis=0)
    grad_value_add = jnp.sum(grad_values_low.astype(jnp.float32), axis=0)
    grad_first = jnp.einsum(
        "re,de->rd", grad_joint_low, joint_back, preferred_element_type=jnp.float32
    )
    grad_stream_norm, grad_gain_one, grad_shift_one = norm_back(
        grad_first, first_hat, first_inv, gain_one_back.astype(jnp.float32)
    )
    grad_stream = grad_mid + grad_stream_norm
    tokens_grad = grad_stream.astype(jnp.bfloat16)
    grad_table = jnp.dot(spread.T, grad_stream, precision=lax.Precision.HIGHEST)
    dp_size = lax.axis_size("dp")
    fsdp_size = lax.axis_size("fsdp")
    group_high = dp_size * 7 // 16
    group_low = dp_size - group_high
    counts = image_counts.astype(jnp.float32)
    share = jnp.where(is_large, counts[1], counts[0]) / (counts[0] + counts[1])
    images = jnp.where(
        is_large,
        group_high * fsdp_size * (ROWS // LARGE_LEN),
        group_low * fsdp_size * (ROWS // SMALL_LEN),
    ).astype(jnp.float32)
    factor = share / images
    grads = (
        grad_joint,
        grad_outproj,
        grad_hidden_w,
        grad_return_w,
        grad_gain_one,
        grad_shift_one,
        grad_query_add,
        grad_value_add,
        grad_output_add,
        grad_gain_two,
        grad_shift_two,
        grad_hidden_add,
        grad_return_add,
        grad_table,
    )
    shares = (
        lax.psum_scatter(
            grads[0].astype(jnp.bfloat16), "fsdp", scatter_dimension=0, tiled=True
        ).astype(jnp.float32),
        lax.psum_scatter(
            grads[1].astype(jnp.bfloat16), "fsdp", scatter_dimension=0, tiled=True
        ).astype(jnp.float32),
        lax.psum_scatter(
            grads[2].astype(jnp.bfloat16), "fsdp", scatter_dimension=0, tiled=True
        ).astype(jnp.float32),
        lax.psum_scatter(
            grads[3].astype(jnp.bfloat16), "fsdp", scatter_dimension=0, tiled=True
        ).astype(jnp.float32),
        lax.psum_scatter(
            grads[4].astype(jnp.bfloat16), "fsdp", scatter_dimension=0, tiled=True
        ).astype(jnp.float32),
        lax.psum_scatter(
            grads[5].astype(jnp.bfloat16), "fsdp", scatter_dimension=0, tiled=True
        ).astype(jnp.float32),
        lax.psum_scatter(
            grads[6].astype(jnp.bfloat16), "fsdp", scatter_dimension=0, tiled=True
        ).astype(jnp.float32),
        lax.psum_scatter(
            grads[7].astype(jnp.bfloat16), "fsdp", scatter_dimension=0, tiled=True
        ).astype(jnp.float32),
        lax.psum_scatter(
            grads[8].astype(jnp.bfloat16), "fsdp", scatter_dimension=0, tiled=True
        ).astype(jnp.float32),
        lax.psum_scatter(
            grads[9].astype(jnp.bfloat16), "fsdp", scatter_dimension=0, tiled=True
        ).astype(jnp.float32),
        lax.psum_scatter(
            grads[10].astype(jnp.bfloat16), "fsdp", scatter_dimension=0, tiled=True
        ).astype(jnp.float32),
        lax.psum_scatter(
            grads[11].astype(jnp.bfloat16), "fsdp", scatter_dimension=0, tiled=True
        ).astype(jnp.float32),
        lax.psum_scatter(
            grads[12].astype(jnp.bfloat16), "fsdp", scatter_dimension=0, tiled=True
        ).astype(jnp.float32),
        lax.psum_scatter(
            grads[13].astype(jnp.bfloat16), "fsdp", scatter_dimension=1, tiled=True
        ).astype(jnp.float32),
    )
    merged = jax.tree.map(
        lambda part: part.astype(jnp.float32),
        lax.psum(shortened(tuple((piece * factor for piece in shares))), "dp"),
    )
    return (
        block_out,
        tokens_grad,
        merged[13],
        merged[4],
        merged[5],
        merged[0],
        merged[6],
        merged[7],
        merged[1],
        merged[8],
        merged[9],
        merged[10],
        merged[2],
        merged[11],
        merged[3],
        merged[12],
    )


def solution(mesh):
    in_specs = (
        P(("dp", "fsdp"), None),
        P(("dp", "fsdp"), None),
        P("dp"),
        P(),
        P(),
        P(None, "fsdp"),
        P("fsdp"),
        P("fsdp"),
        P("fsdp", None),
        P("fsdp"),
        P("fsdp"),
        P("fsdp", None),
        P("fsdp"),
        P("fsdp"),
        P("fsdp"),
        P("fsdp", None),
        P("fsdp"),
        P("fsdp", None),
        P("fsdp"),
    )
    out_specs = (
        P(("dp", "fsdp"), None),
        P(("dp", "fsdp"), None),
        P(None, "fsdp"),
        P("fsdp"),
        P("fsdp"),
        P("fsdp", None),
        P("fsdp"),
        P("fsdp"),
        P("fsdp", None),
        P("fsdp"),
        P("fsdp"),
        P("fsdp"),
        P("fsdp", None),
        P("fsdp"),
        P("fsdp", None),
        P("fsdp"),
    )
    return jax.shard_map(
        per_device, mesh=mesh, in_specs=in_specs, out_specs=out_specs, check_vma=False
    )
```

profile of v0, /device:TPU:0, one launch (start us, length us, event | category | flops | bytes accessed | tf_op | source)
XLA Modules:
  0.0 1341.6 jit_solution(7933301942073396000)
XLA Ops:
  11.0 12.6 all-gather.6
  78.5 12.1 all_gather.59
  90.6 16.1 %all_gather.48 = bf16[50,1024]{1,0:T(8,128)(2,1)S(1)} all-gather(bf16[50,256]{1,0:T(8,128)(2,1)S(1)} %copy-done.33), channel_id=1, replica_groups=mesh['dp'=8,'fsdp'=4] {'fsdp'}, dimensions={1}, use_global_device_ids=true | all-gather | bytes 128000 | tf_op jit(solution)/shard_map/all_gather | solution.py:161
  114.2 15.8 %all-gather.13.cloned.1.call-done = bf16[1024,3072]{1,0:T(8,128)(2,1)} async-done(((bf16[256,3072]{1,0:T(8,128)(2,1)}), bf16[1024,3072]{1,0:T(8,128)(2,1)}) %all-gather.13.cloned.1.call-update) | async-done | bytes 6291472 | tf_op jit(solution)/shard_map/all_gather | solution.py:148
  130.0 17.1 %fusion.72 = f32[1450,3072]{1,0:T(8,128)} fusion(bf16[1024,3072]{1,0:T(8,128)(2,1)} %all-gather.13.cloned.1.call-done, f32[1450,1024]{1,0:T(8,128)} %copy-done.7, f32[1024]{0:T(1024)S(1)} %bitcast.103, f32[1024]{0:T(1024)S(1)} %bitcast.95, f32[1450]{0:T(1024)S(1)} %add_rsqrt_fusion.1, f32[1450]{0:T(1024)S(1)} %broadcast_multiply_fusion.5), kind=kOutput, calls=%fused_computation.164 | convolution fusion | flops 9130035200 | bytes 30068048 | tf_op jit(solution)/shard_map/dot_general | solution.py:198
  160.3 92.4 %conditional.6 = (f32[1450,16]{0,1:T(8,128)}, bf16[1450,1024]{1,0:T(8,128)(2,1)S(1)}) conditional(s32[]{:T(128)} %convert_element_type.404, (bf16[1450,1024]{1,0:T(8,128)(2,1)}, bf16[1450,1024]{1,0:T(8,128)(2,1)S(1)}, bf16[1450,1024]{1,0:T(8,128)(2,1)}) %tuple.44, (bf16[1450,1024]{1,0:T(8,128)(2,1)}, bf16[1450,1024]{1,0:T(8,128)(2,1)S(1)}, ...), branch_computations={%region_3.6_spmd, %region_6.9_spmd} | conditional | flops 889557632 | bytes 82963216
  193.8 13.8 %multiply_reduce_fusion.1 = (f32[10,16,145]{2,1,0:T(8,128)S(1)}, f32[10,16,145,145]{2,3,1,0:T(8,128)}) fusion(bf16[10,145,16,64]{3,2,1,0:T(8,128)(2,1)} %reshape.401, bf16[10,145,16,64]{3,2,1,0:T(8,128)(2,1)} %reshape.400), kind=kOutput, calls=%fused_computation.15 | convolution fusion | flops 437296800 | bytes 19488000 | tf_op jit(solution)/shard_map/cond/branch_1_fun/nqhd,nkhd->nhqk/dot_general | solution.py:77
  207.6 10.6 exponential_reduce_fusion.1
  218.3 15.0 %convert_bitcast_fusion = bf16[10,145,16,64]{1,3,2,0:T(8,128)(2,1)} fusion(bf16[10,145,16,64]{3,2,1,0:T(8,128)(2,1)} %reshape.403, f32[10,16,145,145]{2,3,1,0:T(8,128)} %get-tuple-element.144, f32[10,16,145]{2,1,0:T(8,128)S(1)} %log_add_fusion.1), kind=kOutput, calls=%fused_computation.23 | convolution fusion | flops 442168800 | bytes 19488000 | tf_op jit(solution)/shard_map/cond/branch_1_fun/nhqk,nkhd->nqhd/dot_general | solution.py:88
  263.5 62.1 %all-gather.17.cloned.1.call-done = bf16[1024,4096]{1,0:T(8,128)(2,1)} async-done(((bf16[256,4096]{1,0:T(8,128)(2,1)}), bf16[1024,4096]{1,0:T(8,128)(2,1)}) %all-gather.17.cloned.1.call-update) | async-done | bytes 8388624 | tf_op jit(solution)/shard_map/all_gather | solution.py:150
  325.7 70.6 %multiply_convert_fusion.4 = (bf16[1450,4096]{1,0:T(8,128)(2,1)}, f32[1450,4096]{1,0:T(8,128)}, f32[1450,4096]{1,0:T(8,128)}) fusion(f32[4096]{0:T(1024)S(1)} %convert_element_type.416, bf16[1024,4096]{1,0:T(8,128)(2,1)} %all-gather.17.cloned.1.call-done, f32[1450,1024]{1,0:T(8,128)} %copy-done.8, f32[1024]{0:T(1024)S(1)} %bitcast.101, ...), kind=kOutput, calls=%fused_computation.59 | convolution fusion | flops 12562892800 | bytes 73755984 | tf_op jit(solution)/shard_map/dot_general | solution.py:219
  396.3 78.7 %all-gather.19.cloned.1.call-done = bf16[4096,1024]{1,0:T(8,128)(2,1)} async-done(((bf16[1024,1024]{1,0:T(8,128)(2,1)}), bf16[4096,1024]{1,0:T(8,128)(2,1)}) %all-gather.19.cloned.1.call-update) | async-done | bytes 8388624 | tf_op jit(solution)/shard_map/all_gather | solution.py:151
  475.0 32.7 %fusion.79 = (bf16[4096]{0:T(1024)(128)(2,1)}, bf16[1450,4096]{1,0:T(8,128)(2,1)}) fusion(f32[1450,4096]{1,0:T(8,128)} %get-tuple-element.140, bf16[1450,1024]{1,0:T(8,128)(2,1)} %param.24, bf16[4096,1024]{1,0:T(8,128)(2,1)} %all-gather.19.cloned.1.call-done, f32[1450,4096]{1,0:T(8,128)} %get-tuple-element.158, f32[4096]{0:T(1024)S(1)} %convert_element_type.416), kind=kOutput, calls=%fused_computation.170 | convolution fusion | flops 12258504704 | bytes 70774784 | tf_op jit(solution)/shard_map/rd,fd->rf/dot_general | solution.py:242
  507.7 22.8 %multiply_reduce_fusion.4 = (bf16[1024]{0:T(1024)(128)(2,1)}, f32[1450]{0:T(1024)S(1)}, f32[1450]{0:T(1024)S(1)}, bf16[1024]{0:T(1024)(128)(2,1)}, f32[1450,1024]{1,0:T(8,128)}) fusion(f32[1450,1024]{1,0:T(8,128)S(1)} %copy-done.9, f32[1450]{0:T(1024)S(1)} %add_rsqrt_fusion, f32[1450]{0:T(1024)S(1)} %broadcast_multiply_fusion.4, f32[1024]{0:T(1024)S(1)} %bitcast.92, ...), kind=kOutput, calls=%fused_computation.81 | convolution fusion | flops 12176840704 | bytes 32176800 | tf_op jit(solution)/shard_map/rf,df->rd/dot_general | solution.py:250
  552.4 217.2 %conditional.7 = (bf16[1450,1024]{1,0:T(8,128)(2,1)S(1)}, bf16[1450,1024]{1,0:T(8,128)(2,1)}, bf16[1450,1024]{1,0:T(8,128)(2,1)}) conditional(s32[]{:T(128)} %convert_element_type.404, (bf16[1450,1024]{1,0:T(8,128)(2,1)}, bf16[1450,1024]{1,0:T(8,128)(2,1)S(1)}, f32[1450,16]{0,1:T(8,128)S(1)}, bf16[1450,1024]{1,0:T(8,128)(2,1)}, ...), branch_computations={%region_13.15_spmd, %region_15.17_spmd} | conditional | flops 2199244032 | bytes 259700960
  603.6 10.5 copy.176
  620.2 15.8 %fusion.80 = f32[10,16,145,145]{2,3,1,0:T(8,128)} fusion(bf16[10,145,16,64]{1,3,2,0:T(8,128)(2,1)} %copy.173, bf16[10,145,16,64]{1,3,2,0:T(8,128)(2,1)} %copy.174), kind=kOutput, calls=%fused_computation.171 | convolution fusion | flops 430592000 | bytes 19395200 | tf_op jit(solution)/shard_map/cond/branch_1_fun/nqhd,nkhd->nhqk/dot_general | solution.py:77
  636.0 14.5 %fusion.40 = bf16[10,145,16,64]{1,3,2,0:T(8,128)(2,1)} fusion(bf16[10,145,16,64]{1,3,2,0:T(8,128)(2,1)} %copy.176, f32[10,16,145,145]{2,3,1,0:T(8,128)} %fusion.80, f32[10,16,145]{2,1,0:T(8,128)S(1)} %copy.175), kind=kOutput, calls=%fused_computation.54 | convolution fusion | flops 440684000 | bytes 19488000 | tf_op jit(solution)/shard_map/cond/branch_1_fun/nhqk,nqhd->nkhd/dot_general | solution.py:105
  669.8 21.7 %multiply_reduce_fusion.3 = (f32[10,16,145]{2,1,0:T(8,128)S(1)}, f32[10,16,145,145]{2,3,1,0:T(8,128)}) fusion(f32[10,16,145,145]{2,3,1,0:T(8,128)} %fusion.80, f32[10,16,145]{2,1,0:T(8,128)S(1)} %copy.175, bf16[10,145,16,64]{1,3,2,0:T(8,128)(2,1)} %copy.176, bf16[10,145,16,64]{3,2,1,0:T(8,128)(2,1)} %reshape.415), kind=kOutput, calls=%fused_computation.43 | convolution fusion | flops 444024800 | bytes 33036800 | tf_op jit(solution)/shard_map/cond/branch_1_fun/nqhd,nkhd->nhqk/dot_general | solution.py:108
  691.4 17.3 %multiply_convert_fusion.2 = bf16[10,16,145,145]{2,3,1,0:T(8,128)(2,1)S(1)} fusion(f32[10,16,145,145]{2,3,1,0:T(8,128)} %get-tuple-element.148, f32[10,16,145,145]{2,3,1,0:T(8,128)} %fusion.80, f32[10,16,145]{2,1,0:T(8,128)S(1)} %get-tuple-element.147, f32[10,16,145]{2,1,0:T(8,128)S(1)} %copy.175), kind=kLoop, calls=%fused_computation.42 | loop fusion | flops 16820000 | bytes 33825600 | tf_op jit(solution)/shard_map/cond/branch_1_fun/convert_element_type | solution.py:112
  731.7 10.4 copy.180
  749.9 10.4 copy.186
  769.7 18.2 %convolution_convert_fusion.3 = bf16[1024,3072]{1,0:T(8,128)(2,1)} fusion(bf16[1450,1024]{1,0:T(8,128)(2,1)} %get-tuple-element.93, bf16[1450,1024]{1,0:T(8,128)(2,1)} %get-tuple-element.92, bf16[1450,1024]{1,0:T(8,128)(2,1)S(1)} %get-tuple-element.91, f32[1450,1024]{1,0:T(8,128)} %copy-done.7, f32[1024]{0:T(1024)S(1)} %bitcast.104, f32[1024]{0:T(1024)S(1)} %bitcast.96, ...), kind=kOutput, calls=%fused_computation.94 | convolution fusion | flops 9159907328 | bytes 21159248 | tf_op jit(solution)/shard_map/rd,re->de/dot_general | solution.py:277
  788.6 22.2 %convolution_convert_fusion.1 = bf16[1024,4096]{1,0:T(8,128)(2,1)} fusion(bf16[1450,4096]{1,0:T(8,128)(2,1)} %get-tuple-element.162, f32[1450,1024]{1,0:T(8,128)} %copy-done.8, f32[1024]{0:T(1024)S(1)} %bitcast.102, f32[1024]{0:T(1024)S(1)} %bitcast.94, f32[1450]{0:T(1024)S(1)} %copy-done.32, f32[1450]{0:T(1024)S(1)} %copy-done.28), kind=kOutput, calls=%fused_computation.74 | convolution fusion | flops 12175099904 | bytes 26226000 | tf_op jit(solution)/shard_map/rd,rf->df/dot_general | solution.py:246
  812.6 18.5 %convolution_convert_fusion.2 = bf16[4096,1024]{1,0:T(8,128)(2,1)} fusion(bf16[1450,4096]{1,0:T(8,128)(2,1)} %get-tuple-element.139, bf16[1450,1024]{1,0:T(8,128)(2,1)S(1)} %copy-done.17), kind=kOutput, calls=%fused_computation.75 | convolution fusion | flops 12167675904 | bytes 23236608 | tf_op jit(solution)/shard_map/rf,rd->fd/dot_general | solution.py:238
  847.8 18.3 %multiply_reduce_fusion.5 = (bf16[1024]{0:T(1024)(128)(2,1)S(1)}, f32[1450]{0:T(1024)S(1)}, f32[1450]{0:T(1024)S(1)}, bf16[1024]{0:T(1024)(128)(2,1)S(1)}, f32[1450,1024]{1,0:T(8,128)}) fusion(f32[1450,1024]{1,0:T(8,128)} %copy-done.7, f32[1450]{0:T(1024)S(1)} %copy-done.30, f32[1450]{0:T(1024)S(1)} %copy-done.26, f32[1024]{0:T(1024)S(1)} %bitcast.97, ...), kind=kOutput, calls=%fused_computation.82 | convolution fusion | flops 9162696704 | bytes 27110048 | tf_op jit(solution)/shard_map/re,de->rd/dot_general | solution.py:282
  866.2 23.1 %all-reduce.11 = (bf16[1024]{0:T(1024)(128)(2,1)S(1)}, bf16[1024]{0:T(1024)(128)(2,1)S(1)}, bf16[1024]{0:T(1024)(128)(2,1)S(1)}, bf16[1024]{0:T(1024)(128)(2,1)S...) all-reduce(bf16[1024]{0:T(1024)(128)(2,1)S(1)} %get-tuple-element.1, ...), channel_id=3, replica_groups=mesh['dp'=8,'fsdp'=4] {'fsdp'}, use_global_device_ids=true, to_apply=%region_22.23.clone | all-reduce | flops 12288 | bytes 49152
  908.1 137.1 %reduce-scatter.12.cloned.1.call-done = bf16[256,4096]{1,0:T(8,128)(2,1)} async-done(((bf16[1024,4096]{1,0:T(8,128)(2,1)}), bf16[256,4096]{1,0:T(8,128)(2,1)}) %reduce-scatter.12.cloned.1.call-update) | async-done | bytes 2097168 | tf_op jit(solution)/shard_map/reduce_scatter | solution.py:326
  1048.6 144.4 %reduce-scatter.14.cloned.1.call-done = bf16[1024,1024]{1,0:T(8,128)(2,1)} async-done(((bf16[4096,1024]{1,0:T(8,128)(2,1)}), bf16[1024,1024]{1,0:T(8,128)(2,1)}) %reduce-scatter.14.cloned.1.call-update) | async-done | bytes 2097168 | tf_op jit(solution)/shard_map/reduce_scatter | solution.py:329
  1196.4 19.1 %add_convert_fusion.1 = bf16[1450,1024]{1,0:T(8,128)(2,1)} fusion(f32[1450,1024]{1,0:T(8,128)} %copy-done.8, bf16[1450,4096]{1,0:T(8,128)(2,1)} %get-tuple-element.139, bf16[4096,1024]{1,0:T(8,128)(2,1)} %all-gather.19.cloned.1.call-done, f32[1024]{0:T(1024)S(1)} %bitcast.106), kind=kOutput, calls=%fused_computation.87 | convolution fusion | flops 12167936000 | bytes 29179904 | tf_op jit(solution)/shard_map/dot_general | solution.py:224
  1216.2 25.7 %all-reduce.9 = (bf16[50,256]{1,0:T(8,128)(2,1)S(1)}, bf16[256]{0:T(256)(128)(2,1)S(1)}, bf16[256]{0:T(256)(128)(2,1)S(1)}, bf16[256]{0:T(256)(128)(2,1)S(1)}, b...) all-reduce(bf16[50,256]{1,0:T(8,128)(2,1)S(1)} %multiply_convert_fu, ...), channel_id=1, replica_groups=mesh['dp'=8,'fsdp'=4] {'dp'}, use_global_device_ids=true, to_apply=%region_20.21 | all-reduce | flops 15872 | bytes 63488 | tf_op jit(solution)/shard_map/psum | solution.py:365
  1247.7 75.9 %all-reduce.14.cloned.1.call-done = (bf16[256,3072]{1,0:T(8,128)(2,1)}, bf16[256,1024]{1,0:T(8,128)(2,1)}, bf16[256,4096]{1,0:T(8,128)(2,1)}, bf16[1024,1024]{1,0:T(8,128)(2,1)}) async-done(((bf16[256,3072]{1,0:T(8,128)(2,1)}, bf16[256,1024]{1,0:T(8,128)(2,1)}, bf16[256,4096]{1,0:T(8,128)(2,1)}, bf16[1024,1024]{1,0:T(8,128)(2,1)}), (bf16[256,3072]{1,0:T(8,128)(2,1)}, bf16[256,1024]{1,0:T(8,128)(2,1)}, ...) | async-done | bytes 6291472 | tf_op jit(solution)/shard_map/psum | solution.py:365
  (242 shorter events, 320.9 us)
Async XLA Ops:
  7.3 71.3 %copy-start.46 = (bf16[1024]{0:T(1024)(128)(2,1)S(1)}, bf16[1024]{0:T(1024)(128)(2,1)}, u32[]{:S(2)}) copy-start(bf16[1024]{0:T(1024)(128)(2,1)} %param.39) | copy-start | bytes 6148
  7.3 83.3 %copy-start.33 = (bf16[50,256]{1,0:T(8,128)(2,1)S(1)}, bf16[50,256]{1,0:T(8,128)(2,1)}, u32[]{:S(2)}) copy-start(bf16[50,256]{1,0:T(8,128)(2,1)} %param.28) | copy-start | bytes 76804
  7.3 99.5 %copy-start.41 = (s32[145,4]{0,1:T(4,128)S(1)}, s32[145,4]{0,1:T(4,128)}, u32[]{:S(2)}) copy-start(s32[145,4]{0,1:T(4,128)} %param.27) | copy-start | bytes 6964
  7.3 100.5 %copy-start.18 = (bf16[1450,1024]{1,0:T(8,128)(2,1)S(1)}, bf16[1450,1024]{1,0:T(8,128)(2,1)}, u32[]{:S(2)}) copy-start(bf16[1450,1024]{1,0:T(8,128)(2,1)} %param.23) | copy-start | bytes 8908804
  7.3 122.7 %all-gather.13.cloned.1.call-start = ((), (), s32[]{:S(2)}) async-start(), calls=%async_computation.5 | async-start | bytes 7864320 | tf_op jit(solution)/shard_map/all_gather | solution.py:148
  8.0 244.7 %all-gather.15.cloned.1.call-start = ((), (), s32[]{:S(2)}) async-start(), calls=%async_computation.6 | async-start | bytes 2621440 | tf_op jit(solution)/shard_map/all_gather | solution.py:149
  8.8 316.9 %all-gather.17.cloned.1.call-start = ((), (), s32[]{:S(2)}) async-start(), calls=%async_computation.7 | async-start | bytes 10485760 | tf_op jit(solution)/shard_map/all_gather | solution.py:150
  9.5 465.5 %all-gather.19.cloned.1.call-start = ((), (), s32[]{:S(2)}) async-start(), calls=%async_computation.8 | async-start | bytes 10485760 | tf_op jit(solution)/shard_map/all_gather | solution.py:151
  10.1 893.2 %reduce-scatter.10.cloned.1.call-start = ((), (), s32[]{:S(2)}) async-start(), calls=%async_computation.11 | async-start | bytes 2621440 | tf_op jit(solution)/shard_map/reduce_scatter | solution.py:323
  23.7 302.0 %copy-start.42 = (f32[4,1,256]{2,1,0:T(1,128)}, f32[4,1,256]{2,1,0:T(1,128)S(1)}, u32[]{:S(2)}) copy-start(f32[4,1,256]{2,1,0:T(1,128)S(1)} %convert_element_type.486) | copy-start | bytes 12292
  31.4 499.1 %copy-start.34 = (f32[4,1,256]{2,1,0:T(1,128)}, f32[4,1,256]{2,1,0:T(1,128)S(1)}, u32[]{:S(2)}) copy-start(f32[4,1,256]{2,1,0:T(1,128)S(1)} %convert_element_type.485) | copy-start | bytes 12292
  69.7 60.2 %copy-start.44 = (f32[4,1,256]{2,1,0:T(1,128)}, f32[4,1,256]{2,1,0:T(1,128)S(1)}, u32[]{:S(2)}) copy-start(f32[4,1,256]{2,1,0:T(1,128)S(1)} %convert_element_type.481) | copy-start | bytes 12292
  78.4 51.6 %copy-start.36 = (f32[4,1,256]{2,1,0:T(1,128)}, f32[4,1,256]{2,1,0:T(1,128)S(1)}, u32[]{:S(2)}) copy-start(f32[4,1,256]{2,1,0:T(1,128)S(1)} %convert_element_type.480) | copy-start | bytes 12292
  111.0 19.0 %copy-start.25 = (f32[1450]{0:T(1024)}, f32[1450]{0:T(1024)S(1)}, u32[]{:S(2)}) copy-start(f32[1450]{0:T(1024)S(1)} %broadcast_multiply_fusion.5) | copy-start | bytes 17404
  260.3 270.2 %copy-start.27 = (f32[1450]{0:T(1024)}, f32[1450]{0:T(1024)S(1)}, u32[]{:S(2)}) copy-start(f32[1450]{0:T(1024)S(1)} %broadcast_multiply_fusion.4) | copy-start | bytes 17404
  263.5 266.9 %copy-start.31 = (f32[1450]{0:T(1024)}, f32[1450]{0:T(1024)S(1)}, u32[]{:S(2)}) copy-start(f32[1450]{0:T(1024)S(1)} %add_rsqrt_fusion) | copy-start | bytes 17404
  475.0 32.7 %copy-start.9 = (f32[1450,1024]{1,0:T(8,128)S(1)}, f32[1450,1024]{1,0:T(8,128)}, u32[]{:S(2)}) copy-start(f32[1450,1024]{1,0:T(8,128)} %copy-done.8) | copy-start | bytes 17817604
  507.7 22.8 %copy-start.16 = (bf16[1450,1024]{1,0:T(8,128)(2,1)S(1)}, bf16[1450,1024]{1,0:T(8,128)(2,1)}, u32[]{:S(2)}) copy-start(bf16[1450,1024]{1,0:T(8,128)(2,1)} %param.24) | copy-start | bytes 8908804
  544.0 361.2 %reduce-scatter.8.cloned.1.call-start = ((), (), s32[]{:S(2)}) async-start(), calls=%async_computation.10 | async-start | bytes 7864320 | tf_op jit(solution)/shard_map/reduce_scatter | solution.py:320
  552.4 217.3 %copy-start.26 = (f32[1450]{0:T(1024)S(1)}, f32[1450]{0:T(1024)}, u32[]{:S(2)}) copy-start(f32[1450]{0:T(1024)} %copy-done.25) | copy-start | bytes 17404
  552.4 217.3 %copy-start.30 = (f32[1450]{0:T(1024)S(1)}, f32[1450]{0:T(1024)}, u32[]{:S(2)}) copy-start(f32[1450]{0:T(1024)} %copy-done.29) | copy-start | bytes 17404
  552.4 217.3 %copy-start.37 = (f32[4,1,256]{2,1,0:T(1,128)S(1)}, f32[4,1,256]{2,1,0:T(1,128)}, u32[]{:S(2)}) copy-start(f32[4,1,256]{2,1,0:T(1,128)} %copy-done.36) | copy-start | bytes 12292
  552.4 217.3 %copy-start.45 = (f32[4,1,256]{2,1,0:T(1,128)S(1)}, f32[4,1,256]{2,1,0:T(1,128)}, u32[]{:S(2)}) copy-start(f32[4,1,256]{2,1,0:T(1,128)} %copy-done.44) | copy-start | bytes 12292
  788.0 257.3 %reduce-scatter.12.cloned.1.call-start = ((), (), s32[]{:S(2)}) async-start(), calls=%async_computation.12 | async-start | bytes 10485760 | tf_op jit(solution)/shard_map/reduce_scatter | solution.py:326
  810.8 382.1 %reduce-scatter.14.cloned.1.call-start = ((), (), s32[]{:S(2)}) async-start(), calls=%async_computation.13 | async-start | bytes 10485760 | tf_op jit(solution)/shard_map/reduce_scatter | solution.py:329
  831.1 384.3 %reduce-scatter.6.cloned.1.call-start = ((), (), s32[]{:S(2)}) async-start(), calls=%async_computation.9 | async-start | bytes 143360 | tf_op jit(solution)/shard_map/reduce_scatter | solution.py:359
  847.8 18.3 %copy-start.38 = (bf16[1024]{0:T(1024)(128)(2,1)S(1)}, bf16[1024]{0:T(1024)(128)(2,1)}, u32[]{:S(2)}) copy-start(bf16[1024]{0:T(1024)(128)(2,1)} %get-tuple-element.135) | copy-start | bytes 6148
  847.8 18.3 %copy-start.39 = (bf16[1024]{0:T(1024)(128)(2,1)S(1)}, bf16[1024]{0:T(1024)(128)(2,1)}, u32[]{:S(2)}) copy-start(bf16[1024]{0:T(1024)(128)(2,1)} %get-tuple-element.151) | copy-start | bytes 6148
  847.8 18.3 %copy-start.40 = (bf16[4096]{0:T(1024)(128)(2,1)S(1)}, bf16[4096]{0:T(1024)(128)(2,1)}, u32[]{:S(2)}) copy-start(bf16[4096]{0:T(1024)(128)(2,1)} %get-tuple-element.161) | copy-start | bytes 24580
  847.8 18.3 %copy-start.47 = (bf16[1024]{0:T(1024)(128)(2,1)S(1)}, bf16[1024]{0:T(1024)(128)(2,1)}, u32[]{:S(2)}) copy-start(bf16[1024]{0:T(1024)(128)(2,1)} %get-tuple-element.104) | copy-start | bytes 6148
  847.8 18.3 %copy-start.48 = (bf16[1024]{0:T(1024)(128)(2,1)S(1)}, bf16[1024]{0:T(1024)(128)(2,1)}, u32[]{:S(2)}) copy-start(bf16[1024]{0:T(1024)(128)(2,1)} %get-tuple-element.110) | copy-start | bytes 6148
  903.2 420.4 %all-reduce.14.cloned.1.call-start = ((), (), s32[]{:S(2)}) async-start(), calls=%async_computation.14 | async-start | bytes 12582912 | tf_op jit(solution)/shard_map/psum | solution.py:365
  (34 other events, 194.0 us)
Sparse Core Ops, SparseCore 0:
  9.7 120.2 all-gather.12
  131.5 44.1 all-gather.14
  177.3 148.3 all-gather.16
  327.1 147.8 all-gather.18
  544.1 42.0 reduce-scatter.9
  788.1 109.6 reduce-scatter.7
  900.3 144.9 reduce-scatter.11
  1047.7 145.1 reduce-scatter.13
  1195.3 19.8 reduce-scatter.5
  1219.8 103.7 all-reduce.13
where the time goes:
time: 1350 us; the launch traced here: 1340 us
  waiting for transfers between devices  517 us (38%)
  matrix products  368 us (27%)
  local copies, waits for them, and re-layouts  179 us (13%)
  blocking collectives  152 us (11%)
  other arithmetic  87.3 us (6%)
  between operations  19.9 us (1%)
  loops' own time  17.8 us (1%)
    reduce_scatter x1, waiting for transfers between devices, per_device(): lax.psum_scatter(grads[3].astype(jnp.bfloat16), 'fsdp', scatter_dimension...  144 us
    reduce_scatter x1, waiting for transfers between devices, per_device(): lax.psum_scatter(grads[2].astype(jnp.bfloat16), 'fsdp', scatter_dimension...  137 us
    all_gather x1, waiting for transfers between devices, per_device(): lax.all_gather(return_weight, 'fsdp', axis=0, tiled=True)  78.7 us
    psum x1, waiting for transfers between devices, per_device(): lax.psum(shortened(tuple((piece * factor for piece in shares))), 'dp')  75.9 us
    dot_general x1, matrix products, per_device(): jnp.dot(second_low, hidden_full, preferred_element_type=jnp.float32)  70.6 us
    all_gather x1, waiting for transfers between devices, per_device(): lax.all_gather(hidden_weight, 'fsdp', axis=0, tiled=True)  62.1 us
    dot_general x1, matrix products, per_device(): jnp.einsum('rd,fd->rf', output_grad, return_back, preferred_element_type=...  32.7 us
    dot_general x2, matrix products, image_scores(): jnp.einsum('nqhd,nkhd->nhqk', query_img, keys_img, preferred_element_type...  29.6 us
  transfers between devices with their start and end apart: 10, of which 6 were waited for; matrix products, arithmetic and copies ran while one was open for 40% of the time, Pallas kernels for 0%

commit v1 on v0

v1 whole, which is shorter than its diff:
```python
from functools import partial
import math

import jax
import jax.numpy as jnp
from jax import lax
from jax.experimental import pallas as pl
from jax.experimental.pallas import tpu as pltpu
from jax.sharding import PartitionSpec as P

D = 1024
HEADS = 16
HEAD_DIM = 64
SG = 7
LG = 12
SMALL_LEN = 50
LARGE_LEN = 145
ROWS = 1450


EPS = 1e-06


def shortened(value):
    return jax.tree.map(lambda a: a.astype(jnp.bfloat16) if a.dtype == jnp.float32 else a, value)


def grid_fraction(index):
    scaled = jnp.maximum((2 * index + 1) * SG - LG, 0)
    lower = scaled // (2 * LG)
    return (scaled - 2 * LG * lower).astype(jnp.float32) / (2.0 * LG)


def interp_table(position_source):
    position = jnp.arange(LARGE_LEN, dtype=jnp.int32)
    patch = jnp.maximum(position - 1, 0)
    frac_row = grid_fraction(patch // LG)
    frac_col = grid_fraction(patch % LG)
    weights = jnp.stack(
        [
            (1.0 - frac_row) * (1.0 - frac_col),
            (1.0 - frac_row) * frac_col,
            frac_row * (1.0 - frac_col),
            frac_row * frac_col,
        ],
        axis=1,
    )
    class_row = (jnp.arange(4, dtype=jnp.int32) == 0).astype(jnp.float32)
    weights = jnp.where((position == 0)[:, None], class_row[None, :], weights)
    onehot = (
        position_source[:, :, None] == jnp.arange(SMALL_LEN, dtype=jnp.int32)[None, None, :]
    ).astype(jnp.float32)
    return jnp.sum(weights[:, :, None] * onehot, axis=1)


def layer_norm(values, gain, shift):
    average = jnp.mean(values, axis=-1, keepdims=True)
    centred = values - average
    variance = jnp.mean(centred * centred, axis=-1, keepdims=True)
    inv_std = lax.rsqrt(variance + EPS)
    normed = centred * inv_std
    return (normed * gain + shift, normed, inv_std)


def norm_back(grad_norm, normed, inv_std, gain):
    scaled = grad_norm * gain
    inner = (
        scaled
        - jnp.mean(scaled, axis=-1, keepdims=True)
        - normed * jnp.mean(scaled * normed, axis=-1, keepdims=True)
    )
    return (inv_std * inner, jnp.sum(grad_norm * normed, axis=0), jnp.sum(grad_norm, axis=0))


def image_scores(query_low, keys_low, length):
    images = ROWS // length
    query_img = query_low.reshape(images, length, HEADS, HEAD_DIM)
    keys_img = keys_low.reshape(images, length, HEADS, HEAD_DIM)
    logits = jnp.einsum("nqhd,nkhd->nhqk", query_img, keys_img, preferred_element_type=jnp.float32)
    return (logits / math.sqrt(HEAD_DIM), query_img, keys_img)


def attend_forward(query_low, keys_low, values_low, length):
    images = ROWS // length
    scores, _, _ = image_scores(query_low, keys_low, length)
    highest = jnp.max(scores, axis=-1, keepdims=True)
    log_total = highest + jnp.log(jnp.sum(jnp.exp(scores - highest), axis=-1, keepdims=True))
    probs = jnp.exp(scores - log_total)
    values_img = values_low.reshape(images, length, HEADS, HEAD_DIM)
    attended = jnp.einsum(
        "nhqk,nkhd->nqhd",
        probs.astype(jnp.bfloat16),
        values_img,
        preferred_element_type=jnp.float32,
    )
    lse_rows = jnp.transpose(log_total[..., 0], (0, 2, 1)).reshape(ROWS, HEADS)
    return (attended.reshape(ROWS, D).astype(jnp.bfloat16), lse_rows)


def attend_backward(query_low, keys_low, values_low, lse_rows, grad_att_low, length):
    images = ROWS // length
    scores, query_img, keys_img = image_scores(query_low, keys_low, length)
    log_total = jnp.transpose(lse_rows.reshape(images, length, HEADS), (0, 2, 1))[..., None]
    probs = jnp.exp(scores - log_total)
    values_img = values_low.reshape(images, length, HEADS, HEAD_DIM)
    grad_img = grad_att_low.reshape(images, length, HEADS, HEAD_DIM)
    grad_values = jnp.einsum(
        "nhqk,nqhd->nkhd", probs.astype(jnp.bfloat16), grad_img, preferred_element_type=jnp.float32
    )
    grad_probs = jnp.einsum(
        "nqhd,nkhd->nhqk", grad_img, values_img, preferred_element_type=jnp.float32
    )
    grad_scores = probs * (grad_probs - jnp.sum(grad_probs * probs, axis=-1, keepdims=True))
    grad_scores_low = grad_scores.astype(jnp.bfloat16)
    grad_query = jnp.einsum(
        "nhqk,nkhd->nqhd", grad_scores_low, keys_img, preferred_element_type=jnp.float32
    ) / math.sqrt(HEAD_DIM)
    grad_keys = jnp.einsum(
        "nhqk,nqhd->nkhd", grad_scores_low, query_img, preferred_element_type=jnp.float32
    ) / math.sqrt(HEAD_DIM)
    return (
        grad_query.reshape(ROWS, D).astype(jnp.bfloat16),
        grad_keys.reshape(ROWS, D).astype(jnp.bfloat16),
        grad_values.reshape(ROWS, D).astype(jnp.bfloat16),
    )


GROUP = 8


def swap(value, bit):
    size = lax.axis_size("dp")
    return lax.ppermute(value, "dp", [(i, i ^ (1 << bit)) for i in range(size)])


def assemble_kernel(half, d_ref, *refs):
    near, far, out, sem = refs[0:5], refs[5:10], refs[10], refs[11]
    copies = []
    for flip, (own, ax, by, a2, b2) in enumerate((near, far)):
        base = d_ref[0] ^ flip
        jobs = (
            (own, out.at[:, base]),
            (ax, out.at[pl.ds(0, half), base ^ 2]),
            (by, out.at[pl.ds(half, half), base ^ 4]),
            (a2.at[0], out.at[pl.ds(0, half), base ^ 4]),
            (a2.at[1], out.at[pl.ds(0, half), base ^ 6]),
            (b2.at[0], out.at[pl.ds(half, half), base ^ 2]),
            (b2.at[1], out.at[pl.ds(half, half), base ^ 6]),
        )
        for source, target in jobs:
            copies.append(pltpu.make_async_copy(source, target, sem.at[len(copies)]))
    for copy in copies:
        copy.start()
    for copy in copies:
        copy.wait()


def gather_rows(shard):
    shards = lax.axis_size("fsdp")
    rows, cols = shard.shape
    part = rows // GROUP
    place = lax.axis_index("dp") % GROUP
    piece = lax.dynamic_slice_in_dim(shard, place * part, part, 0)
    own = lax.all_gather(piece, "fsdp", axis=0, tiled=False)
    half = shards // 2
    top, low = own[:half], own[half:]
    ax, by = swap(top, 1), swap(low, 2)
    a2 = swap(jnp.stack([top, ax]), 2)
    b2 = swap(jnp.stack([low, by]), 1)
    near = (own, ax, by, a2, b2)
    far = tuple(swap(v, 0) for v in near)
    full = pl.pallas_call(
        partial(assemble_kernel, half),
        out_shape=jax.ShapeDtypeStruct((shards, GROUP, part, cols), shard.dtype),
        grid_spec=pltpu.PrefetchScalarGridSpec(
            num_scalar_prefetch=1,
            grid=(1,),
            in_specs=[pl.BlockSpec(memory_space=pl.ANY)] * 10,
            out_specs=pl.BlockSpec(memory_space=pl.ANY),
            scratch_shapes=[pltpu.SemaphoreType.DMA((14,))],
        ),
        name="assemble",
    )(place.astype(jnp.int32).reshape(1), *near, *far)
    return full.reshape(shards * rows, cols)


def gather_native(shard):
    rows = shard.shape[0]
    part = rows // GROUP
    place = lax.axis_index("dp") % GROUP
    piece = lax.dynamic_slice_in_dim(shard, place * part, part, 0)
    own = lax.all_gather(piece, "fsdp", axis=0, tiled=False)
    full = plane_gather(own, axis=1)
    return full.reshape(rows * own.shape[0], shard.shape[1])


def plane_gather(value, axis):
    size = lax.axis_size("dp")
    groups = None
    if size > GROUP:
        groups = [[g * GROUP + i for i in range(GROUP)] for g in range(size // GROUP)]
    return lax.all_gather(value, "dp", axis=axis, tiled=False, axis_index_groups=groups)


def rest_sum(value):
    size = lax.axis_size("dp")
    if size == GROUP:
        return value
    groups = [[g * GROUP + i for g in range(size // GROUP)] for i in range(GROUP)]
    return lax.psum(value, "dp", axis_index_groups=groups)


def pick(value, index, axis):
    return lax.dynamic_index_in_dim(value, index, axis, keepdims=False)


def add_low(left, right):
    return (left.astype(jnp.float32) + right.astype(jnp.float32)).astype(jnp.bfloat16)


def scatter_sum(grad):
    shards = lax.axis_size("fsdp")
    rows, cols = grad.shape
    part = rows // (shards * GROUP)
    half = shards // 2
    place = lax.axis_index("dp") % GROUP
    c, x, y = place & 1, (place >> 1) & 1, place >> 2
    cube = grad.reshape(shards, 2, 2, 2, part, cols)
    got = swap(pick(cube, 1 - c, 3), 0)
    pair = add_low(pick(cube, c, 3), got)
    top, low = pair[:half], pair[half:]
    top_got = swap(pick(top, 1 - x, 2), 1)
    low_got = swap(pick(low, 1 - y, 1), 2)
    top = add_low(pick(top, x, 2), top_got)
    low = add_low(pick(low, y, 1), low_got)
    top_got = swap(pick(top, 1 - y, 1), 2)
    low_got = swap(pick(low, 1 - x, 1), 1)
    top = add_low(pick(top, y, 1), top_got)
    low = add_low(pick(low, x, 1), low_got)
    both = jnp.concatenate([top, low], axis=0).reshape(shards * part, cols)
    piece = lax.psum_scatter(both, "fsdp", scatter_dimension=0, tiled=True)
    piece = rest_sum(piece)
    return plane_gather(piece, axis=0).reshape(GROUP * part, cols).astype(jnp.float32)


def small_sum(value):
    shards = lax.axis_size("fsdp")
    value = value.astype(jnp.bfloat16)
    for bit in range(3):
        value = add_low(value, swap(value, bit))
    value = rest_sum(value)
    me = lax.axis_index("fsdp")
    total = pick(value, me, 0).astype(jnp.float32)
    for step in range(1, shards):
        send = pick(value, (me + step) % shards, 0)
        got = lax.ppermute(send, "fsdp", [(i, (i + step) % shards) for i in range(shards)])
        total = total + got.astype(jnp.float32)
    return total


def per_device(
    tokens,
    output_grad,
    group_member,
    image_counts,
    position_source,
    position_table,
    first_gain,
    first_shift,
    input_proj,
    query_bias,
    value_bias,
    output_proj,
    output_bias,
    second_gain,
    second_shift,
    hidden_weight,
    hidden_bias,
    return_weight,
    return_bias,
):
    dp_size = lax.axis_size("dp")
    fsdp_size = lax.axis_size("fsdp")
    small_parts = (
        first_gain,
        first_shift,
        query_bias,
        value_bias,
        output_bias,
        second_gain,
        second_shift,
        return_bias,
        hidden_bias,
        position_table.reshape(-1),
    )
    sizes = [v.shape[0] for v in small_parts]
    joined = jnp.concatenate(small_parts)
    pad = -joined.shape[0] % 2048
    joined = jnp.pad(joined, (0, pad)).reshape(-1, 128)
    smalls = lax.all_gather(joined, "fsdp", axis=0, tiled=False).reshape(fsdp_size, -1)
    smalls = smalls.astype(jnp.float32)
    offsets = [sum(sizes[:i]) for i in range(len(sizes))]
    vectors = [smalls[:, o : o + n] for o, n in zip(offsets, sizes)]
    (
        gain_one,
        shift_one,
        query_add,
        value_add,
        output_add,
        gain_two,
        shift_two,
        return_add,
        hidden_add,
    ) = [v.reshape(-1) for v in vectors[:9]]
    table_full = (
        vectors[9].reshape(fsdp_size, SMALL_LEN, -1).transpose(1, 0, 2).reshape(SMALL_LEN, D)
    )
    joint_proj = gather_rows(input_proj)
    hidden_full = gather_rows(hidden_weight)
    outproj_full = gather_native(output_proj)
    return_full = gather_rows(return_weight)
    member = group_member[0]
    is_large = member == 1
    length = jnp.where(is_large, LARGE_LEN, SMALL_LEN)
    group_high = dp_size * 7 // 16
    group_low = dp_size - group_high
    counts = image_counts.astype(jnp.float32)
    share = jnp.where(is_large, counts[1], counts[0]) / (counts[0] + counts[1])
    images = jnp.where(
        is_large,
        group_high * fsdp_size * (ROWS // LARGE_LEN),
        group_low * fsdp_size * (ROWS // SMALL_LEN),
    ).astype(jnp.float32)
    factor = share / images

    def weight_grad(left, right):
        product = lax.dot_general(
            left, right, (((0,), (0,)), ((), ())), preferred_element_type=jnp.float32
        )
        return scatter_sum((product * factor).astype(jnp.bfloat16))

    row_index = jnp.arange(ROWS, dtype=jnp.int32)
    place = row_index % length
    inter = interp_table(position_source)
    identity = (
        jnp.arange(LARGE_LEN, dtype=jnp.int32)[:, None]
        == jnp.arange(SMALL_LEN, dtype=jnp.int32)[None, :]
    ).astype(jnp.float32)
    mixing = jnp.where(is_large, inter, identity)
    picker = (place[:, None] == jnp.arange(LARGE_LEN, dtype=jnp.int32)[None, :]).astype(jnp.float32)
    spread = jnp.dot(picker, mixing, precision=lax.Precision.HIGHEST)
    position = jnp.dot(spread, table_full, precision=lax.Precision.HIGHEST)
    stream = tokens.astype(jnp.float32) + position
    first_out, first_hat, first_inv = layer_norm(stream, gain_one, shift_one)
    first_low = first_out.astype(jnp.bfloat16)
    joint_add = jnp.concatenate([query_add, jnp.zeros_like(query_add), value_add])
    projected = jnp.dot(first_low, joint_proj, preferred_element_type=jnp.float32)
    projected = (projected + joint_add).astype(jnp.bfloat16)
    query_low = projected[:, :D]
    keys_low = projected[:, D : 2 * D]
    values_low = projected[:, 2 * D :]
    attended_low, lse_rows = lax.cond(
        is_large,
        partial(attend_forward, length=LARGE_LEN),
        partial(attend_forward, length=SMALL_LEN),
        query_low,
        keys_low,
        values_low,
    )
    mid = stream + jnp.dot(attended_low, outproj_full, preferred_element_type=jnp.float32) + output_add
    second_out, second_hat, second_inv = layer_norm(mid, gain_two, shift_two)
    second_low = second_out.astype(jnp.bfloat16)
    hidden_pre = jnp.dot(second_low, hidden_full, preferred_element_type=jnp.float32) + hidden_add
    activ, gelu_back = jax.vjp(partial(jax.nn.gelu, approximate=False), hidden_pre)
    activ_low = activ.astype(jnp.bfloat16)
    return_w_out = weight_grad(activ_low, output_grad)
    returned = jnp.dot(activ_low, return_full, preferred_element_type=jnp.float32) + return_add
    block_out = (mid + returned).astype(jnp.bfloat16)
    grad_out = output_grad.astype(jnp.float32)
    grad_return_add = jnp.sum(grad_out, axis=0)
    grad_activ = jnp.einsum(
        "rd,fd->rf", output_grad, return_full, preferred_element_type=jnp.float32
    )
    grad_hidden_low = gelu_back(grad_activ)[0].astype(jnp.bfloat16)
    hidden_w_out = weight_grad(second_low, grad_hidden_low)
    grad_hidden_add = jnp.sum(grad_hidden_low.astype(jnp.float32), axis=0)
    grad_second = jnp.einsum(
        "rf,df->rd", grad_hidden_low, hidden_full, preferred_element_type=jnp.float32
    )
    grad_mid_norm, grad_gain_two, grad_shift_two = norm_back(
        grad_second, second_hat, second_inv, gain_two
    )
    grad_mid = grad_out + grad_mid_norm
    grad_branch_low = grad_mid.astype(jnp.bfloat16)
    outproj_out = weight_grad(attended_low, grad_branch_low)
    grad_output_add = jnp.sum(grad_branch_low.astype(jnp.float32), axis=0)
    grad_attended = jnp.einsum(
        "re,de->rd", grad_branch_low, outproj_full, preferred_element_type=jnp.float32
    )
    grad_att_low = grad_attended.astype(jnp.bfloat16)
    grad_query_low, grad_keys_low, grad_values_low = lax.cond(
        is_large,
        partial(attend_backward, length=LARGE_LEN),
        partial(attend_backward, length=SMALL_LEN),
        query_low,
        keys_low,
        values_low,
        lse_rows,
        grad_att_low,
    )
    grad_joint_low = jnp.concatenate([grad_query_low, grad_keys_low, grad_values_low], axis=1)
    joint_out = weight_grad(first_low, grad_joint_low)
    grad_query_add = jnp.sum(grad_query_low.astype(jnp.float32), axis=0)
    grad_value_add = jnp.sum(grad_values_low.astype(jnp.float32), axis=0)
    grad_first = jnp.einsum(
        "re,de->rd", grad_joint_low, joint_proj, preferred_element_type=jnp.float32
    )
    grad_stream_norm, grad_gain_one, grad_shift_one = norm_back(
        grad_first, first_hat, first_inv, gain_one
    )
    grad_stream = grad_mid + grad_stream_norm
    tokens_grad = grad_stream.astype(jnp.bfloat16)
    grad_table = jnp.dot(spread.T, grad_stream, precision=lax.Precision.HIGHEST)
    table_rows = grad_table.reshape(SMALL_LEN, fsdp_size, -1).transpose(1, 0, 2)
    small_grads = (
        grad_gain_one,
        grad_shift_one,
        grad_query_add,
        grad_value_add,
        grad_output_add,
        grad_gain_two,
        grad_shift_two,
        grad_return_add,
        grad_hidden_add,
        table_rows,
    )
    packed = jnp.concatenate([v.reshape(fsdp_size, -1) for v in small_grads], axis=1) * factor
    packed = jnp.pad(packed, ((0, 0), (0, pad))).reshape(fsdp_size, -1, 128)
    summed = small_sum(packed).reshape(-1)
    small_outs = [summed[o : o + n] for o, n in zip(offsets, sizes)]
    return (
        block_out,
        tokens_grad,
        small_outs[9].reshape(SMALL_LEN, -1),
        small_outs[0],
        small_outs[1],
        joint_out,
        small_outs[2],
        small_outs[3],
        outproj_out,
        small_outs[4],
        small_outs[5],
        small_outs[6],
        hidden_w_out,
        small_outs[8],
        return_w_out,
        small_outs[7],
    )


def solution(mesh):
    in_specs = (
        P(("dp", "fsdp"), None),
        P(("dp", "fsdp"), None),
        P("dp"),
        P(),
        P(),
        P(None, "fsdp"),
        P("fsdp"),
        P("fsdp"),
        P("fsdp", None),
        P("fsdp"),
        P("fsdp"),
        P("fsdp", None),
        P("fsdp"),
        P("fsdp"),
        P("fsdp"),
        P("fsdp", None),
        P("fsdp"),
        P("fsdp", None),
        P("fsdp"),
    )
    out_specs = (
        P(("dp", "fsdp"), None),
        P(("dp", "fsdp"), None),
        P(None, "fsdp"),
        P("fsdp"),
        P("fsdp"),
        P("fsdp", None),
        P("fsdp"),
        P("fsdp"),
        P("fsdp", None),
        P("fsdp"),
        P("fsdp"),
        P("fsdp"),
        P("fsdp", None),
        P("fsdp"),
        P("fsdp", None),
        P("fsdp"),
    )
    return jax.shard_map(
        per_device, mesh=mesh, in_specs=in_specs, out_specs=out_specs, check_vma=False
    )
```

time: 1350 us -> 1720 us (1.27)
  Pallas kernels: 0 us -> 703 us
  waiting for transfers between devices: 517 us -> 160 us
  starting transfers between devices: 0.78 us -> 120 us
  blocking collectives: 152 us -> 69.5 us
  matrix products: 368 us -> 342 us
    pallas_call x0 -> x3, Pallas kernels: none -> 703 us  [gather_rows(): pl.pallas_call(partial(assemble_kernel, half), out_shape=jax.ShapeDtypeSt...]
    reduce_scatter x5 -> x4, waiting for transfers between devices: 282 us -> 0.04 us  [scatter_sum(): piece = lax.psum_scatter(both, 'fsdp', scatter_dimension=0, tiled=True)]
    ppermute x0 -> x53, starting transfers between devices: none -> 119 us  [the longest x50 115 us: swap(): return lax.ppermute(value, 'dp', [(i, i ^ 1 << bit) for i in range(size)])]
    ppermute x0 -> x53, waiting for transfers between devices: none -> 97 us  [the longest x50 97 us: swap(): return lax.ppermute(value, 'dp', [(i, i ^ 1 << bit) for i in range(size)])]
    all_gather x4 -> x6, waiting for transfers between devices: 157 us -> 62.8 us  [the longest x4 62.8 us: plane_gather(): lax.all_gather(value, 'dp', axis=axis, tiled=False, axis_index_groups=gro...]
    psum x1 -> x0, waiting for transfers between devices: 75.9 us -> none  [per_device(): lax.psum(shortened(tuple((piece * factor for piece in shares))), 'dp')]
    all_gather x10 -> x4, blocking collectives: 103 us -> 69.5 us  [the longest x1 28.9 us: gather_rows(): own = lax.all_gather(piece, 'fsdp', axis=0, tiled=False)]
    convert_element_type x0 -> x4, local copies, waits for them, and re-layouts: none -> 30.6 us  [the longest x2 15.3 us: attend_backward(): grad_values.reshape(ROWS, D).astype(jnp.bfloat16)]
  transfers between devices with their start and end apart: 10 -> 63, of which waited for: 6 -> 20; matrix products, arithmetic and copies ran while one was open for 40% -> 20% of each run, Pallas kernels for 0% -> 26%
where the time goes in v1:
time: 1720 us; the launch traced here: 1710 us
  Pallas kernels  703 us (41%)
  matrix products  342 us (20%)
  local copies, waits for them, and re-layouts  178 us (10%)
  waiting for transfers between devices  160 us (9%)
  starting transfers between devices  120 us (7%)
  other arithmetic  90.7 us (5%)
  blocking collectives  69.5 us (4%)
  loops' own time  33.6 us (2%)
  between operations  19.4 us (1%)
    pallas_call x3, Pallas kernels, gather_rows(): pl.pallas_call(partial(assemble_kernel, half), out_shape=jax.ShapeDtypeSt...  703 us
    ppermute x50, starting transfers between devices, swap(): return lax.ppermute(value, 'dp', [(i, i ^ 1 << bit) for i in range(size)])  115 us
    ppermute x50, waiting for transfers between devices, swap(): return lax.ppermute(value, 'dp', [(i, i ^ 1 << bit) for i in range(size)])  97 us
    dot_general x1, matrix products, per_device(): jnp.dot(second_low, hidden_full, preferred_element_type=jnp.float32)  70.7 us
    all_gather x4, waiting for transfers between devices, plane_gather(): lax.all_gather(value, 'dp', axis=axis, tiled=False, axis_index_groups=gro...  62.8 us
    dot_general x4, matrix products, weight_grad(): lax.dot_general(left, right, (((0,), (0,)), ((), ())), preferred_element_...  55.3 us
  transfers between devices with their start and end apart: 63, of which 20 were waited for; matrix products, arithmetic and copies ran while one was open for 20% of the time, Pallas kernels for 26%

profile of v1, /device:TPU:0, one launch (start us, length us, event | category | flops | bytes accessed | tf_op | source)
XLA Modules:
  0.0 1714.8 jit_solution(1327194517419597663)
XLA Ops:
  12.3 28.9 %all-gather = bf16[128,3072]{1,0:T(8,128)(2,1)S(1)} all-gather(bf16[32,3072]{1,0:T(8,128)(2,1)S(1)} %constant_dynamic-slice_fusion.11), channel_id=2, replica_groups=mesh['dp'=8,'fsdp'=4] {'fsdp'}, dimensions={0}, use_global_device_ids=true | all-gather | bytes 983040 | tf_op jit(solution)/shard_map/all_gather | solution.py:164
  45.0 15.6 all-gather.1
  69.7 14.6 all_gather.57
  101.4 17.0 collective-permute-start.3
  140.8 191.8 %assemble.3 = bf16[4,8,32,3072]{3,2,1,0:T(8,128)(2,1)} custom-call(s32[1]{0:T(128)} %bitcast.15.d_ref, bf16[4,32,3072]{2,1,0:T(8,128)(2,1)} %bitcast.337, bf16[2,32,3072]{2,1,0:T(8,128)(2,1)} %copy-done.24, bf16[2,32,3072]{2,1,0:T(8,128)(2,1)} %copy-done.25, bf16[2,2,32,3072]{3,2,1,0:T(8,128)(2,1)} %collective-permute-done.2.refs_3_, ...), custom_call_target="tpu_custom_call" | custom-call | tf_op jit(solution)/shard_map/assemble/pallas_call | solution.py:172
  332.7 13.9 add_convert_fusion
  356.1 87.8 %conditional.6 = (f32[1450,16]{0,1:T(8,128)S(1)}, bf16[1450,1024]{1,0:T(8,128)(2,1)}) conditional(s32[]{:T(128)} %convert_element_type.563, (bf16[1450,1024]{1,0:T(8,128)(2,1)}, bf16[1450,1024]{1,0:T(8,128)(2,1)}, bf16[1450,1024]{1,0:T(8,128)(2,1)}) %tuple.50, (bf16[1450,1024]{1,0:T(8,128)(2,1)}, bf16[1450,1024]{1,0:T(8,128)(2,1)}, ...), branch_computations={%region_3.6_spmd, %region_6.9_spmd} | conditional | flops 889557632 | bytes 82963216
  373.6 13.5 multiply_reduce_fusion
  465.3 13.2 collective-permute-done.21.refs_4_
  480.3 255.3 %assemble.4 = bf16[4,8,32,4096]{3,2,1,0:T(8,128)(2,1)} custom-call(s32[1]{0:T(128)} %bitcast.15.d_ref, bf16[4,32,4096]{2,1,0:T(8,128)(2,1)} %bitcast.345, bf16[2,32,4096]{2,1,0:T(8,128)(2,1)} %copy-done.20, bf16[2,32,4096]{2,1,0:T(8,128)(2,1)} %copy-done.21, bf16[2,2,32,4096]{3,2,1,0:T(8,128)(2,1)} %collective-permute-done.11.refs_3_, ...), custom_call_target="tpu_custom_call" | custom-call | tf_op jit(solution)/shard_map/assemble/pallas_call | solution.py:172
  735.7 70.7 %multiply_convert_fusion.6 = (bf16[1450,4096]{1,0:T(8,128)(2,1)}, f32[1450,4096]{1,0:T(8,128)}, f32[1450,4096]{1,0:T(8,128)}) fusion(f32[4096]{0:T(1024)S(1)} %bitcast.380, bf16[1024,4096]{1,0:T(8,128)(2,1)} %bitcast.328, f32[1450,1024]{1,0:T(8,128)} %copy-done.3, f32[1024]{0:T(1024)S(1)} %bitcast.394, f32[1024]{0:T(1024)S(1)} %bitcast.388, ...), kind=kOutput, calls=%fused_computation.72 | convolution fusion | flops 12562892800 | bytes 73755984 | tf_op jit(solution)/shard_map/dot_general | solution.py:373
  806.4 255.3 %assemble.5 = bf16[4,8,128,1024]{3,2,1,0:T(8,128)(2,1)} custom-call(s32[1]{0:T(128)} %bitcast.15.d_ref, bf16[4,128,1024]{2,1,0:T(8,128)(2,1)} %bitcast.34.refs_0_, bf16[2,128,1024]{2,1,0:T(8,128)(2,1)} %collective-permute-done.18.refs_1_, bf16[2,128,1024]{2,1,0:T(8,128)(2,1)} %collective-permute-done.19.refs_2_, ...), custom_call_target="tpu_custom_call" | custom-call | tf_op jit(solution)/shard_map/assemble/pallas_call | solution.py:172
  1061.8 32.4 %convert_reduce_fusion.4 = (f32[4096]{0:T(1024)}, bf16[1450,4096]{1,0:T(8,128)(2,1)}) fusion(f32[1450,4096]{1,0:T(8,128)} %get-tuple-element.133, bf16[4096,1024]{1,0:T(8,128)(2,1)} %bitcast.326, bf16[1450,1024]{1,0:T(8,128)(2,1)} %param.24, f32[1450,4096]{1,0:T(8,128)} %get-tuple-element.203, f32[4096]{0:T(1024)S(1)} %bitcast.381), kind=kOutput, calls=%fused_computation.71 | convolution fusion | flops 12264443904 | bytes 70782976 | tf_op jit(solution)/shard_map/rd,fd->rf/dot_general | solution.py:381
  1094.1 22.4 %multiply_reduce_fusion.4 = (f32[1024]{0:T(1024)}, f32[1450]{0:T(1024)S(1)}, f32[1450]{0:T(1024)S(1)}, f32[1024]{0:T(1024)}, f32[1450,1024]{1,0:T(8,128)}) fusion(f32[1450,1024]{1,0:T(8,128)} %copy-done.3, f32[1450]{0:T(1024)S(1)} %add_rsqrt_fusion, f32[1450]{0:T(1024)S(1)} %broadcast_multiply_fusion.4, f32[1024]{0:T(1024)S(1)} %bitcast.389, ...), kind=kOutput, calls=%fused_computation.98 | convolution fusion | flops 12176840704 | bytes 32180896 | tf_op jit(solution)/shard_map/rf,df->rd/dot_general | solution.py:387
  1116.6 19.7 %multiply_convert_fusion.8 = bf16[1024,4096]{1,0:T(8,128)(2,1)} fusion(bf16[1450,4096]{1,0:T(8,128)(2,1)} %get-tuple-element.207, f32[]{:T(128)S(6)} %div.204, f32[1450,1024]{1,0:T(8,128)S(1)} %copy-done.4, f32[1024]{0:T(1024)S(1)} %bitcast.395, f32[1024]{0:T(1024)S(1)} %bitcast.390, f32[1450]{0:T(1024)S(1)} %add_rsqrt_fusion, ...), kind=kOutput, calls=%fused_computation.88 | convolution fusion | flops 12179294208 | bytes 26226004 | tf_op jit(solution)/shard_map/dot_general | solution.py:337
  1136.3 18.6 %multiply_convert_fusion.7 = bf16[4096,1024]{1,0:T(8,128)(2,1)} fusion(bf16[1450,4096]{1,0:T(8,128)(2,1)} %get-tuple-element.132, bf16[1450,1024]{1,0:T(8,128)(2,1)S(1)} %copy-done.18, f32[]{:T(128)S(6)} %div.204), kind=kOutput, calls=%fused_computation.87 | convolution fusion | flops 12171870208 | bytes 23236612 | tf_op jit(solution)/shard_map/dot_general | solution.py:337
  1163.4 170.6 %conditional.7 = (f32[4,256]{1,0:T(4,128)S(1)}, f32[4,256]{1,0:T(4,128)S(1)}, bf16[1450,1024]{1,0:T(8,128)(2,1)}, bf16[1450,1024]{1,0:T(8,128)(2,1)}, bf16[1450,1024]{1,0:T(8,128)(2,1)}) conditional(s32[]{:T(128)} %convert_element_type.563, (bf16[1450,1024]{1,0:T(8,128)(2,1)}, bf16[1450,1024]{1,0:T(8,128)(2,1)}, f32[1450,16]{0,1:T(8,128)S(1)}, ...), branch_computations={%region_13.17_spmd, %region_17.21_spmd} | conditional | flops 2206665984 | bytes 235597440
  1199.1 13.5 subtract_exponential_fusion
  1238.1 14.1 multiply_reduce_fusion.2
  1252.2 12.2 multiply_convert_fusion.2
  1264.4 10.9 fusion.29
  1275.3 12.3 convert_reduce_fusion.1
  1339.0 54.9 %collective-permute-start.48 = (bf16[4,2,2,128,1024]{4,3,2,1,0:T(8,128)(2,1)}, bf16[4,2,2,128,1024]{4,3,2,1,0:T(8,128)(2,1)}, u32[]{:S(2)}, u32[]{:S(2)}) collective-permute-start(bf16[4,2,2,128,1024]{4,3,2,1,0:T(8,128)(2,1)} %dynamic-slice_bitcast_fusion), channel_id=1, source_target_pairs={{0,4},{4,0},{8,12},{12,8},{16,20},{20,16},{24,28},{28,24},{1,5},{5... | collective-permute-start | bytes 12582920 | tf_op jit(solution)/shard_map/ppermute | solution.py:133
  1396.8 13.0 multiply_convert_fusion.9
  1417.7 17.7 %multiply_reduce_fusion.5 = (f32[1024]{0:T(1024)S(1)}, f32[1450]{0:T(1024)S(1)}, f32[1450]{0:T(1024)S(1)}, f32[1024]{0:T(1024)S(1)}, f32[1450,1024]{1,0:T(8,128)}) fusion(f32[1450,1024]{1,0:T(8,128)S(1)} %bitcast.321, f32[1450]{0:T(1024)S(1)} %copy-done.38, f32[1450]{0:T(1024)S(1)} %copy-done.36, f32[1024]{0:T(1024)S(1)} %bitcast.386, ...), kind=kOutput, calls=%fused_computation.100 | convolution fusion | flops 9135970304 | bytes 27114144 | tf_op jit(solution)/shard_map/re,de->rd/dot_general | solution.py:415
  1448.4 11.0 collective-permute-done.36
  1490.5 12.5 collective-permute-done.51
  1509.6 15.8 collective-permute-done.46
  1567.0 10.7 fusion.98
  1600.4 19.1 %add_convert_fusion.1 = bf16[1450,1024]{1,0:T(8,128)(2,1)} fusion(f32[1450,1024]{1,0:T(8,128)} %copy-done.3, bf16[1450,4096]{1,0:T(8,128)(2,1)} %get-tuple-element.132, bf16[4096,1024]{1,0:T(8,128)(2,1)} %bitcast.327, f32[1024]{0:T(1024)S(1)} %bitcast.397), kind=kOutput, calls=%fused_computation.104 | convolution fusion | flops 12167936000 | bytes 29179904 | tf_op jit(solution)/shard_map/dot_general | solution.py:377
  1647.2 26.4 %all-gather.26.cloned.1.call-done = bf16[1024,1024]{1,0:T(8,128)(2,1)} async-done(((bf16[128,1024]{1,0:T(8,128)(2,1)}), bf16[1024,1024]{1,0:T(8,128)(2,1)}) %all-gather.26.cloned.1.call-update) | async-done | bytes 2097168 | tf_op jit(solution)/shard_map/all_gather | solution.py:202
  1677.7 25.8 %all-gather.24.cloned.1.call-done = bf16[256,4096]{1,0:T(8,128)(2,1)} async-done(((bf16[32,4096]{1,0:T(8,128)(2,1)}), bf16[256,4096]{1,0:T(8,128)(2,1)}) %all-gather.24.cloned.1.call-update) | async-done | bytes 2097168 | tf_op jit(solution)/shard_map/all_gather | solution.py:202
  (447 shorter events, 409.1 us)
Async XLA Ops:
  7.2 125.8 %all-gather.18.cloned.1.call-start = ((), (), s32[]{:S(2)}) async-start(), calls=%async_computation.9 | async-start | bytes 1310720 | tf_op jit(solution)/shard_map/all_gather | solution.py:164
  9.5 125.7 %all-gather.20.cloned.1.call-start = ((), (), s32[]{:S(2)}) async-start(), calls=%async_computation.10 | async-start | bytes 1310720 | tf_op jit(solution)/shard_map/all_gather | solution.py:164
  11.3 442.5 %all-gather.16.cloned.1.call-start = ((), (), s32[]{:S(2)}) async-start(), calls=%async_computation.8 | async-start | bytes 2359296 | tf_op jit(solution)/shard_map/all_gather | solution.py:202
  41.2 77.1 %collective-permute-start = (bf16[2,32,3072]{2,1,0:T(8,128)(2,1)S(1)}, bf16[2,32,3072]{2,1,0:T(8,128)(2,1)S(1)}, u32[]{:S(2)}, u32[]{:S(2)}) collective-permute-start(bf16[2,32,3072]{2,1,0:T(8,128)(2,1)S(1)} %bitcast.364), channel_id=1, source_target_pairs={{0,8},{4,12},{8,0},{12,4},{16,24},{20,28},{24,16},{28,20},{1,9},{5... | collective-permute-start | bytes 1179656 | tf_op jit(solution)/shard_map/ppermute | solution.py:133
  42.6 58.7 %collective-permute-start.1 = (bf16[2,32,3072]{2,1,0:T(8,128)(2,1)S(1)}, bf16[2,32,3072]{2,1,0:T(8,128)(2,1)S(1)}, u32[]{:S(2)}, u32[]{:S(2)}) collective-permute-start(bf16[2,32,3072]{2,1,0:T(8,128)(2,1)S(1)} %bitcast.366), channel_id=1, source_target_pairs={{0,16},{4,20},{8,24},{12,28},{16,0},{20,4},{24,8},{28,12},{1,17},{... | collective-permute-start | bytes 1179656 | tf_op jit(solution)/shard_map/ppermute | solution.py:133
  44.2 94.4 %collective-permute-start.4 = (bf16[4,32,3072]{2,1,0:T(8,128)(2,1)S(1)}, bf16[4,32,3072]{2,1,0:T(8,128)(2,1)}, u32[]{:S(2)}, u32[]{:S(2)}) collective-permute-start(bf16[4,32,3072]{2,1,0:T(8,128)(2,1)S(1)} %bitcast.336), channel_id=1, source_target_pairs={{0,4},{4,0},{8,12},{12,8},{16,20},{20,16},{24,28},{28,24},{1,5},{5... | collective-permute-start | bytes 2359304 | tf_op jit(solution)/shard_map/ppermute | solution.py:133
  60.6 1517.2 %reduce-scatter.5.cloned.1.call-start = ((), (), s32[]{:S(2)}) async-start(), calls=%async_computation.4 | async-start | bytes 983040 | tf_op jit(solution)/shard_map/reduce_scatter | solution.py:241
  136.5 215.4 %collective-permute-start.18 = (bf16[2,128,1024]{2,1,0:T(8,128)(2,1)S(1)}, bf16[2,128,1024]{2,1,0:T(8,128)(2,1)}, u32[]{:S(2)}, u32[]{:S(2)}) collective-permute-start(bf16[2,128,1024]{2,1,0:T(8,128)(2,1)S(1)} %bitcast.358), channel_id=1, source_target_pairs={{0,8},{4,12},{8,0},{12,4},{16,24},{20,28},{24,16},{28,20},{1,9},{5... | collective-permute-start | bytes 1572872 | tf_op jit(solution)/shard_map/ppermute | solution.py:133
  137.2 309.0 %collective-permute-start.19 = (bf16[2,128,1024]{2,1,0:T(8,128)(2,1)S(1)}, bf16[2,128,1024]{2,1,0:T(8,128)(2,1)}, u32[]{:S(2)}, u32[]{:S(2)}) collective-permute-start(bf16[2,128,1024]{2,1,0:T(8,128)(2,1)S(1)} %bitcast.356), channel_id=1, source_target_pairs={{0,16},{4,20},{8,24},{12,28},{16,0},{20,4},{24,8},{28,12},{1,17},{... | collective-permute-start | bytes 1572872 | tf_op jit(solution)/shard_map/ppermute | solution.py:133
  138.6 209.8 %collective-permute-start.9 = (bf16[2,32,4096]{2,1,0:T(8,128)(2,1)}, bf16[2,32,4096]{2,1,0:T(8,128)(2,1)S(1)}, u32[]{:S(2)}, u32[]{:S(2)}) collective-permute-start(bf16[2,32,4096]{2,1,0:T(8,128)(2,1)} %bitcast.27), channel_id=1, source_target_pairs={{0,8},{4,12},{8,0},{12,4},{16,24},{20,28},{24,16},{28,20},{1,9},{5... | collective-permute-start | bytes 1572872 | tf_op jit(solution)/shard_map/ppermute | solution.py:133
  139.4 207.2 %collective-permute-start.10 = (bf16[2,32,4096]{2,1,0:T(8,128)(2,1)}, bf16[2,32,4096]{2,1,0:T(8,128)(2,1)S(1)}, u32[]{:S(2)}, u32[]{:S(2)}) collective-permute-start(bf16[2,32,4096]{2,1,0:T(8,128)(2,1)} %bitcast.360), channel_id=1, source_target_pairs={{0,16},{4,20},{8,24},{12,28},{16,0},{20,4},{24,8},{28,12},{1,17},{... | collective-permute-start | bytes 1572872 | tf_op jit(solution)/shard_map/ppermute | solution.py:133
  347.7 105.5 %collective-permute-start.12 = (bf16[2,2,32,4096]{3,2,1,0:T(8,128)(2,1)}, bf16[2,2,32,4096]{3,2,1,0:T(8,128)(2,1)}, u32[]{:S(2)}, u32[]{:S(2)}) collective-permute-start(bf16[2,2,32,4096]{3,2,1,0:T(8,128)(2,1)} %pad_maximum_fusion.1), channel_id=1, source_target_pairs={{0,8},{4,12},{8,0},{12,4},{16,24},{20,28},{24,16},{28,20},{1,9},{5... | collective-permute-start | bytes 3145736 | tf_op jit(solution)/shard_map/ppermute | solution.py:133
  350.7 102.6 %collective-permute-start.11 = (bf16[2,2,32,4096]{3,2,1,0:T(8,128)(2,1)}, bf16[2,2,32,4096]{3,2,1,0:T(8,128)(2,1)}, u32[]{:S(2)}, u32[]{:S(2)}) collective-permute-start(bf16[2,2,32,4096]{3,2,1,0:T(8,128)(2,1)} %pad_maximum_fusion), channel_id=1, source_target_pairs={{0,16},{4,20},{8,24},{12,28},{16,0},{20,4},{24,8},{28,12},{1,17},{... | collective-permute-start | bytes 3145736 | tf_op jit(solution)/shard_map/ppermute | solution.py:133
  352.0 101.1 %collective-permute-start.14 = (bf16[2,32,4096]{2,1,0:T(8,128)(2,1)S(1)}, bf16[2,32,4096]{2,1,0:T(8,128)(2,1)}, u32[]{:S(2)}, u32[]{:S(2)}) collective-permute-start(bf16[2,32,4096]{2,1,0:T(8,128)(2,1)S(1)} %collective-permute-done.9.refs_1_), channel_id=1, source_target_pairs={{0,4},{4,0},{8,12},{12,8},{16,20},{20,16},{24,28},{28,24},{1,5},{5... | collective-permute-start | bytes 1572872 | tf_op jit(solution)/shard_map/ppermute | solution.py:133
  352.0 101.1 %collective-permute-start.15 = (bf16[2,32,4096]{2,1,0:T(8,128)(2,1)S(1)}, bf16[2,32,4096]{2,1,0:T(8,128)(2,1)}, u32[]{:S(2)}, u32[]{:S(2)}) collective-permute-start(bf16[2,32,4096]{2,1,0:T(8,128)(2,1)S(1)} %collective-permute-done.10.refs_2_), channel_id=1, source_target_pairs={{0,4},{4,0},{8,12},{12,8},{16,20},{20,16},{24,28},{28,24},{1,5},{5... | collective-permute-start | bytes 1572872 | tf_op jit(solution)/shard_map/ppermute | solution.py:133
  465.1 341.3 %collective-permute-start.22 = (bf16[4,128,1024]{2,1,0:T(8,128)(2,1)}, bf16[4,128,1024]{2,1,0:T(8,128)(2,1)}, u32[]{:S(2)}, u32[]{:S(2)}) collective-permute-start(bf16[4,128,1024]{2,1,0:T(8,128)(2,1)} %bitcast.34.refs_0_), channel_id=1, source_target_pairs={{0,4},{4,0},{8,12},{12,8},{16,20},{20,16},{24,28},{28,24},{1,5},{5... | collective-permute-start | bytes 3145736 | tf_op jit(solution)/shard_map/ppermute | solution.py:133
  478.5 327.9 %collective-permute-start.23 = (bf16[2,128,1024]{2,1,0:T(8,128)(2,1)}, bf16[2,128,1024]{2,1,0:T(8,128)(2,1)}, u32[]{:S(2)}, u32[]{:S(2)}) collective-permute-start(bf16[2,128,1024]{2,1,0:T(8,128)(2,1)} %collective-permute-done.18.refs_1_), channel_id=1, source_target_pairs={{0,4},{4,0},{8,12},{12,8},{16,20},{20,16},{24,28},{28,24},{1,5},{5... | collective-permute-start | bytes 1572872 | tf_op jit(solution)/shard_map/ppermute | solution.py:133
  478.6 327.8 %collective-permute-start.24 = (bf16[2,128,1024]{2,1,0:T(8,128)(2,1)}, bf16[2,128,1024]{2,1,0:T(8,128)(2,1)}, u32[]{:S(2)}, u32[]{:S(2)}) collective-permute-start(bf16[2,128,1024]{2,1,0:T(8,128)(2,1)} %collective-permute-done.19.refs_2_), channel_id=1, source_target_pairs={{0,4},{4,0},{8,12},{12,8},{16,20},{20,16},{24,28},{28,24},{1,5},{5... | collective-permute-start | bytes 1572872 | tf_op jit(solution)/shard_map/ppermute | solution.py:133
  479.0 327.4 %collective-permute-start.26 = (bf16[2,2,128,1024]{3,2,1,0:T(8,128)(2,1)}, bf16[2,2,128,1024]{3,2,1,0:T(8,128)(2,1)}, u32[]{:S(2)}, u32[]{:S(2)}) collective-permute-start(bf16[2,2,128,1024]{3,2,1,0:T(8,128)(2,1)} %collective-permute-done.21.refs_4_), channel_id=1, source_target_pairs={{0,4},{4,0},{8,12},{12,8},{16,20},{20,16},{24,28},{28,24},{1,5},{5... | collective-permute-start | bytes 3145736 | tf_op jit(solution)/shard_map/ppermute | solution.py:133
  479.1 327.3 %collective-permute-start.25 = (bf16[2,2,128,1024]{3,2,1,0:T(8,128)(2,1)}, bf16[2,2,128,1024]{3,2,1,0:T(8,128)(2,1)}, u32[]{:S(2)}, u32[]{:S(2)}) collective-permute-start(bf16[2,2,128,1024]{3,2,1,0:T(8,128)(2,1)} %collective-permute-done.20.refs_3_), channel_id=1, source_target_pairs={{0,4},{4,0},{8,12},{12,8},{16,20},{20,16},{24,28},{28,24},{1,5},{5... | collective-permute-start | bytes 3145736 | tf_op jit(solution)/shard_map/ppermute | solution.py:133
  1339.0 128.9 %collective-permute-start.48 = (bf16[4,2,2,128,1024]{4,3,2,1,0:T(8,128)(2,1)}, bf16[4,2,2,128,1024]{4,3,2,1,0:T(8,128)(2,1)}, u32[]{:S(2)}, u32[]{:S(2)}) collective-permute-start(bf16[4,2,2,128,1024]{4,3,2,1,0:T(8,128)(2,1)} %dynamic-slice_bitcast_fusion), channel_id=1, source_target_pairs={{0,4},{4,0},{8,12},{12,8},{16,20},{20,16},{24,28},{28,24},{1,5},{5... | collective-permute-start | bytes 12582920 | tf_op jit(solution)/shard_map/ppermute | solution.py:133
  1416.8 61.3 %collective-permute-start.43 = (bf16[4,2,2,32,4096]{4,3,2,1,0:T(8,128)(2,1)}, bf16[4,2,2,32,4096]{4,3,2,1,0:T(8,128)(2,1)}, u32[]{:S(2)}, u32[]{:S(2)}) collective-permute-start(bf16[4,2,2,32,4096]{4,3,2,1,0:T(8,128)(2,1)} %dynamic-slice_bitcast_fusion.1), channel_id=1, source_target_pairs={{0,4},{4,0},{8,12},{12,8},{16,20},{20,16},{24,28},{28,24},{1,5},{5... | collective-permute-start | bytes 12582920 | tf_op jit(solution)/shard_map/ppermute | solution.py:133
  1446.4 104.3 %collective-permute-start.38 = (bf16[4,2,2,32,1024]{4,3,2,1,0:T(8,128)(2,1)}, bf16[4,2,2,32,1024]{4,3,2,1,0:T(8,128)(2,1)}, u32[]{:S(2)}, u32[]{:S(2)}) collective-permute-start(bf16[4,2,2,32,1024]{4,3,2,1,0:T(8,128)(2,1)} %dynamic-slice_bitcast_fusion.5), channel_id=1, source_target_pairs={{0,4},{4,0},{8,12},{12,8},{16,20},{20,16},{24,28},{28,24},{1,5},{5... | collective-permute-start | bytes 3145736 | tf_op jit(solution)/shard_map/ppermute | solution.py:133
  1487.2 38.3 %collective-permute-start.46 = (bf16[2,2,32,4096]{3,2,1,0:T(8,128)(2,1)}, bf16[2,2,32,4096]{3,2,1,0:T(8,128)(2,1)}, u32[]{:S(2)}, u32[]{:S(2)}) collective-permute-start(bf16[2,2,32,4096]{3,2,1,0:T(8,128)(2,1)} %dynamic-slice_bitcast_fusion.4), channel_id=1, source_target_pairs={{0,16},{4,20},{8,24},{12,28},{16,0},{20,4},{24,8},{28,12},{1,17},{... | collective-permute-start | bytes 3145736 | tf_op jit(solution)/shard_map/ppermute | solution.py:133
  1487.6 41.5 %collective-permute-start.44 = (bf16[2,2,32,4096]{3,2,0,1:T(8,128)(2,1)}, bf16[2,2,32,4096]{3,2,0,1:T(8,128)(2,1)}, u32[]{:S(2)}, u32[]{:S(2)}) collective-permute-start(bf16[2,2,32,4096]{3,2,0,1:T(8,128)(2,1)} %bitcast.314), channel_id=1, source_target_pairs={{0,8},{4,12},{8,0},{12,4},{16,24},{20,28},{24,16},{28,20},{1,9},{5... | collective-permute-start | bytes 3145736 | tf_op jit(solution)/shard_map/ppermute | solution.py:133
  1490.4 93.5 %reduce-scatter.11.cloned.1.call-start = ((), (), s32[]{:S(2)}) async-start(), calls=%async_computation.7 | async-start | bytes 1310720 | tf_op jit(solution)/shard_map/reduce_scatter | solution.py:241
  1504.7 33.4 %collective-permute-start.52 = (bf16[2,128,1024]{2,1,0:T(8,128)(2,1)S(1)}, bf16[2,128,1024]{2,1,0:T(8,128)(2,1)S(1)}, u32[]{:S(2)}, u32[]{:S(2)}) collective-permute-start(bf16[2,128,1024]{2,1,0:T(8,128)(2,1)S(1)} %dynamic-slice_bitcast_fusion.7), channel_id=1, source_target_pairs={{0,8},{4,12},{8,0},{12,4},{16,24},{20,28},{24,16},{28,20},{1,9},{5... | collective-permute-start | bytes 1572872 | tf_op jit(solution)/shard_map/ppermute | solution.py:133
  1539.6 60.8 %reduce-scatter.9.cloned.1.call-start = ((), (), s32[]{:S(2)}) async-start(), calls=%async_computation.6 | async-start | bytes 1310720 | tf_op jit(solution)/shard_map/reduce_scatter | solution.py:241
  1550.4 71.0 %reduce-scatter.7.cloned.1.call-start = ((), (), s32[]{:S(2)}) async-start(), calls=%async_computation.5 | async-start | bytes 327680 | tf_op jit(solution)/shard_map/reduce_scatter | solution.py:241
  1566.9 76.8 %all-gather.22.cloned.1.call-start = ((), (), s32[]{:S(2)}) async-start(), calls=%async_computation.11 | async-start | bytes 1769472 | tf_op jit(solution)/shard_map/all_gather | solution.py:202
  1577.9 95.8 %all-gather.26.cloned.1.call-start = ((), (), s32[]{:S(2)}) async-start(), calls=%async_computation.13 | async-start | bytes 2359296 | tf_op jit(solution)/shard_map/all_gather | solution.py:202
  1584.0 119.5 %all-gather.24.cloned.1.call-start = ((), (), s32[]{:S(2)}) async-start(), calls=%async_computation.12 | async-start | bytes 2359296 | tf_op jit(solution)/shard_map/all_gather | solution.py:202
  (95 other events, 3702.5 us)
Sparse Core Ops, SparseCore 0:
  10.2 37.7 all-gather.17
  50.1 29.5 all-gather.19
  81.6 27.1 all-gather.15
  1490.6 23.3 reduce-scatter.4
  1539.7 27.3 reduce-scatter.10
  1569.9 25.8 reduce-scatter.8
  1598.6 18.2 reduce-scatter.6
  1618.9 24.7 all-gather.21
  1645.7 27.8 all-gather.25
  1675.5 27.8 all-gather.23

commit v2 on v1

v2 whole, which is shorter than its diff:
```python
from functools import partial

import jax
import jax.numpy as jnp
from jax import lax
from jax.experimental import pallas as pl
from jax.experimental.pallas import tpu as pltpu
from jax.sharding import PartitionSpec as P

D = 1024
HEADS = 16
HEAD_DIM = 64
SG = 7
LG = 12
SMALL_LEN = 50
LARGE_LEN = 145
ROWS = 1450
PAD = 1472
GROUP = 8
WINDOW = 176
WINDOWS = 10
PAIRS = 4
FAR = -1e30
LOW = jnp.bfloat16


EPS = 1e-06


def grid_fraction(index):
    scaled = jnp.maximum((2 * index + 1) * SG - LG, 0)
    lower = scaled // (2 * LG)
    return (scaled - 2 * LG * lower).astype(jnp.float32) / (2.0 * LG)


def interp_table(position_source):
    position = jnp.arange(LARGE_LEN, dtype=jnp.int32)
    patch = jnp.maximum(position - 1, 0)
    frac_row = grid_fraction(patch // LG)
    frac_col = grid_fraction(patch % LG)
    weights = jnp.stack(
        [
            (1.0 - frac_row) * (1.0 - frac_col),
            (1.0 - frac_row) * frac_col,
            frac_row * (1.0 - frac_col),
            frac_row * frac_col,
        ],
        axis=1,
    )
    class_row = (jnp.arange(4, dtype=jnp.int32) == 0).astype(jnp.float32)
    weights = jnp.where((position == 0)[:, None], class_row[None, :], weights)
    onehot = (
        position_source[:, :, None] == jnp.arange(SMALL_LEN, dtype=jnp.int32)[None, None, :]
    ).astype(jnp.float32)
    return jnp.sum(weights[:, :, None] * onehot, axis=1)


def layer_norm(values, gain, shift):
    average = jnp.mean(values, axis=-1, keepdims=True)
    centred = values - average
    variance = jnp.mean(centred * centred, axis=-1, keepdims=True)
    inv_std = lax.rsqrt(variance + EPS)
    normed = centred * inv_std
    return (normed * gain + shift, normed, inv_std)


def norm_back(grad_norm, normed, inv_std, gain):
    scaled = grad_norm * gain
    inner = (
        scaled
        - jnp.mean(scaled, axis=-1, keepdims=True)
        - normed * jnp.mean(scaled * normed, axis=-1, keepdims=True)
    )
    return (inv_std * inner, jnp.sum(grad_norm * normed, axis=0), jnp.sum(grad_norm, axis=0))

def dot_nt(left, right):
    return lax.dot_general(
        left, right, (((1,), (1,)), ((), ())), preferred_element_type=jnp.float32
    )


def dot_nn(left, right):
    return lax.dot_general(
        left, right, (((1,), (0,)), ((), ())), preferred_element_type=jnp.float32
    )


def dot_tn(left, right):
    return lax.dot_general(
        left, right, (((0,), (0,)), ((), ())), preferred_element_type=jnp.float32
    )


def after(value, *others):
    return lax.optimization_barrier((value, *others))[0]


def window_start(window, step):
    return pl.multiple_of(jnp.minimum(window * step // 16 * 16, PAD - WINDOW), 16)


def image_of(row, length, step):
    image = jnp.where(row >= length, 1, 0) + jnp.where(row >= 2 * length, 1, 0)
    return jnp.where(row < 0, -1, jnp.where(row >= step, 3, image))


def fill_masks(mask_ref, length, step):
    def one(window, carry):
        base = window_start(window, step) - window * step
        shape = (WINDOW, WINDOW)
        rows = image_of(lax.broadcasted_iota(jnp.int32, shape, 0) + base, length, step)
        cols = image_of(lax.broadcasted_iota(jnp.int32, shape, 1) + base, length, step)
        mask_ref[window] = jnp.where(rows == cols, 0.0, FAR).astype(jnp.float32)
        return carry

    lax.fori_loop(0, WINDOWS, one, 0)


def split_heads(value):
    lane = lax.broadcasted_iota(jnp.int32, value.shape, 1)
    zero = jnp.zeros_like(value)
    return jnp.where(lane < HEAD_DIM, value, zero), jnp.where(lane < HEAD_DIM, zero, value)


def slabs(ref, at):
    return [ref[at, 128 * i : 128 * i + 128] for i in range(PAIRS)]


def join_heads(even, odd):
    lane = lax.broadcasted_iota(jnp.int32, even.shape, 1)
    return jnp.where(lane < HEAD_DIM, even, odd)


def keep_rows(ref, start, first, value):
    row = lax.broadcasted_iota(jnp.int32, value.shape, 0) + start
    value = jnp.where(row < ROWS, value, 0.0)
    at = pl.ds(start, WINDOW)
    old = ref[at, :].astype(jnp.float32)
    ref[at, :] = jnp.where(row >= first, value, old).astype(ref.dtype)


def forward_kernel(s_ref, q_ref, k_ref, v_ref, o_ref, mask_ref):
    length, step = s_ref[0], s_ref[1]

    @pl.when(pl.program_id(0) == 0)
    def _():
        fill_masks(mask_ref, length, step)

    def one(window, carry):
        start = window_start(window, step)
        at = pl.ds(start, WINDOW)
        query = [h for v in slabs(q_ref, at) for h in split_heads(v * LOW(0.125))]
        keys, values = slabs(k_ref, at), slabs(v_ref, at)
        mask = mask_ref[window]
        each = range(2 * PAIRS)
        scores = [dot_nt(query[i], keys[i // 2]) + mask for i in each]
        top = [jnp.max(v, axis=1, keepdims=True) for v in scores]
        raised = [jnp.exp(scores[i] - top[i]) for i in each]
        total = [jnp.sum(v, axis=1, keepdims=True) for v in raised]
        out = [dot_nn(raised[i].astype(LOW), values[i // 2]) for i in each]
        out = [out[i] * (1.0 / total[i]) for i in each]
        for j in range(PAIRS):
            piece = join_heads(out[2 * j], out[2 * j + 1])
            keep_rows(o_ref.at[:, 128 * j : 128 * j + 128], start, window * step, piece)
        return carry

    lax.fori_loop(0, WINDOWS, one, 0)


def backward_kernel(s_ref, q_ref, k_ref, v_ref, g_ref, out_ref, mask_ref):
    length, step = s_ref[0], s_ref[1]
    fill_masks(mask_ref, length, step)

    def one(window, carry):
        start = window_start(window, step)
        at = pl.ds(start, WINDOW)
        query = [h for v in slabs(q_ref, at) for h in split_heads(v * LOW(0.125))]
        grad = [h for v in slabs(g_ref, at) for h in split_heads(v)]
        keys, values = slabs(k_ref, at), slabs(v_ref, at)
        mask = mask_ref[window]
        each = range(2 * PAIRS)
        scores = [dot_nt(keys[i // 2], query[i]) + mask for i in each]
        grad_probs = [dot_nt(values[i // 2], grad[i]) for i in each]
        top = [jnp.max(v, axis=0, keepdims=True) for v in scores]
        raised = [jnp.exp(scores[i] - top[i]) for i in each]
        scale = [1.0 / jnp.sum(v, axis=0, keepdims=True) for v in raised]
        probs = [raised[i] * scale[i] for i in each]
        inner = [jnp.sum(grad_probs[i] * probs[i], axis=0, keepdims=True) for i in each]
        grad_scores = [(probs[i] * (grad_probs[i] - inner[i])).astype(LOW) for i in each]
        grad_v = [dot_nn(probs[i].astype(LOW), grad[i]) for i in each]
        grad_k = [dot_nn(grad_scores[i], query[i]) for i in each]
        grad_q = [dot_tn(grad_scores[i], keys[i // 2]) for i in each]
        for j in range(PAIRS):
            cols = slice(128 * j, 128 * j + 128)
            first = window * step
            both = join_heads(grad_q[2 * j], grad_q[2 * j + 1]) * 0.125
            keep_rows(out_ref.at[0, :, cols], start, first, both)
            keep_rows(out_ref.at[1, :, cols], start, first, grad_k[2 * j] + grad_k[2 * j + 1])
            keep_rows(out_ref.at[2, :, cols], start, first, grad_v[2 * j] + grad_v[2 * j + 1])
        return carry

    lax.fori_loop(0, WINDOWS, one, 0)


def attend_forward(lengths, projected):
    width = 128 * PAIRS
    blocks = D // width

    def part(base):
        return pl.BlockSpec((PAD, width), lambda h, s: (0, h + base))

    return pl.pallas_call(
        forward_kernel,
        out_shape=jax.ShapeDtypeStruct((PAD, D), LOW),
        grid_spec=pltpu.PrefetchScalarGridSpec(
            num_scalar_prefetch=1,
            grid=(blocks,),
            in_specs=[part(0), part(blocks), part(2 * blocks)],
            out_specs=part(0),
            scratch_shapes=[pltpu.VMEM((WINDOWS, WINDOW, WINDOW), jnp.float32)],
        ),
        name="attend_forward",
    )(lengths, projected, projected, projected)


def attend_backward(numbers, projected, grad):
    width = 128 * PAIRS
    blocks = D // width

    def part(base):
        return pl.BlockSpec((PAD, width), lambda i, s: (0, s[2] + base))

    return pl.pallas_call(
        backward_kernel,
        out_shape=jax.ShapeDtypeStruct((3, PAD, width), LOW),
        grid_spec=pltpu.PrefetchScalarGridSpec(
            num_scalar_prefetch=1,
            grid=(1,),
            in_specs=[part(0), part(blocks), part(2 * blocks), part(0)],
            out_specs=pl.BlockSpec((3, PAD, width), lambda i, s: (0, 0, 0)),
            scratch_shapes=[pltpu.VMEM((WINDOWS, WINDOW, WINDOW), jnp.float32)],
        ),
        name="attend_backward",
    )(numbers, projected, projected, projected, grad)


def hidden_kernel(rows, x_ref, w_ref, b_ref, activ_ref, slope_ref):
    for i in range(PAD // rows):
        at = slice(i * rows, (i + 1) * rows)
        hidden = dot_nn(x_ref[at, :], w_ref[...]) + b_ref[...]
        cdf = 0.5 * lax.erf(hidden * 0.7071067811865476) + 0.5
        density = jnp.exp(-0.5 * hidden * hidden) * 0.3989422804014327
        activ_ref[at, :] = (hidden * cdf).astype(LOW)
        slope_ref[at, :] = (cdf + hidden * density).astype(LOW)


def hidden_layer(second, weight, bias):
    width = weight.shape[1]
    tile = 512
    return pl.pallas_call(
        partial(hidden_kernel, 184),
        out_shape=[jax.ShapeDtypeStruct((PAD, width), LOW)] * 2,
        grid=(width // tile,),
        in_specs=[
            pl.BlockSpec((PAD, D), lambda n: (0, 0)),
            pl.BlockSpec((D, tile), lambda n: (0, n)),
            pl.BlockSpec((1, tile), lambda n: (0, n)),
        ],
        out_specs=[pl.BlockSpec((PAD, tile), lambda n: (0, n))] * 2,
        name="hidden_layer",
    )(second, weight, bias.reshape(1, width))


def hidden_back_kernel(rows, g_ref, w_ref, slope_ref, out_ref, sum_ref):
    total = jnp.zeros_like(sum_ref)
    for i in range(PAD // rows):
        at = slice(i * rows, (i + 1) * rows)
        grad = dot_nt(g_ref[at, :], w_ref[...]) * slope_ref[at, :].astype(jnp.float32)
        grad = grad.astype(LOW)
        out_ref[at, :] = grad
        total = total + jnp.sum(grad.astype(jnp.float32), axis=0, keepdims=True)
    sum_ref[...] = total


def hidden_back(grad, weight, slope):
    width = weight.shape[0]
    tile = 512
    return pl.pallas_call(
        partial(hidden_back_kernel, 368),
        out_shape=[
            jax.ShapeDtypeStruct((PAD, width), LOW),
            jax.ShapeDtypeStruct((1, width), jnp.float32),
        ],
        grid=(width // tile,),
        in_specs=[
            pl.BlockSpec((PAD, D), lambda n: (0, 0)),
            pl.BlockSpec((tile, D), lambda n: (n, 0)),
            pl.BlockSpec((PAD, tile), lambda n: (0, n)),
        ],
        out_specs=[
            pl.BlockSpec((PAD, tile), lambda n: (0, n)),
            pl.BlockSpec((1, tile), lambda n: (0, n)),
        ],
        name="hidden_back",
    )(grad, weight, slope)


def grad_kernel(c_ref, f_ref, a_ref, b_ref, *refs):
    out_ref = refs[-1]
    right = b_ref[...].reshape(b_ref.shape[-2:])
    value = dot_tn(a_ref[...], right) * f_ref[0]
    if len(refs) == 2:
        value = value + refs[0][...].astype(jnp.float32)
    out_ref[...] = value.astype(LOW)


def grad_half(core, factor, left, right, got=None, tile_m=512, tile_n=512):
    rows = left.shape[1]
    stacked = right.ndim == 3
    cols = 3 * right.shape[2] if stacked else right.shape[1] // 2
    steps = cols // tile_n
    in_specs = [
        pl.BlockSpec(memory_space=pltpu.SMEM),
        pl.BlockSpec((PAD, tile_m), lambda m, n, c: (0, m)),
    ]
    if stacked:
        in_specs.append(pl.BlockSpec((1, PAD, tile_n), lambda m, n, c: (n, 0, 0)))
    else:
        in_specs.append(pl.BlockSpec((PAD, tile_n), lambda m, n, c: (0, n + c[0] * steps)))
    out_spec = pl.BlockSpec((tile_m, tile_n), lambda m, n, c: (m, n))
    operands = [core, factor, left, right]
    if got is not None:
        in_specs.append(out_spec)
        operands.append(got)
    return pl.pallas_call(
        grad_kernel,
        out_shape=jax.ShapeDtypeStruct((rows, cols), LOW),
        grid_spec=pltpu.PrefetchScalarGridSpec(
            num_scalar_prefetch=1,
            grid=(rows // tile_m, steps),
            in_specs=in_specs,
            out_specs=out_spec,
        ),
        name="grad_keep" if got is not None else "grad_send",
    )(*operands)


def swap(value, bit):
    size = lax.axis_size("dp")
    return lax.ppermute(value, "dp", [(i, i ^ (1 << bit)) for i in range(size)])


def assemble_kernel(half, d_ref, *refs):
    near, far, out, held, sem = refs[0:5], refs[5:10], refs[10], refs[11], refs[12]
    copies = []
    for flip, (own, ax, by, a2, b2) in enumerate((near, far)):
        base = d_ref[0] ^ flip
        jobs = (
            (own, held.at[:, base]),
            (ax, held.at[pl.ds(0, half), base ^ 2]),
            (by, held.at[pl.ds(half, half), base ^ 4]),
            (a2.at[0], held.at[pl.ds(0, half), base ^ 4]),
            (a2.at[1], held.at[pl.ds(0, half), base ^ 6]),
            (b2.at[0], held.at[pl.ds(half, half), base ^ 2]),
            (b2.at[1], held.at[pl.ds(half, half), base ^ 6]),
        )
        for source, target in jobs:
            copies.append(pltpu.make_async_copy(source, target, sem.at[len(copies)]))
    for copy in copies:
        copy.start()
    for copy in copies:
        copy.wait()
    last = pltpu.make_async_copy(held, out, sem.at[0])
    last.start()
    last.wait()


def gather_piece(shard):
    part = shard.shape[0] // GROUP
    place = lax.axis_index("dp") % GROUP
    piece = lax.dynamic_slice_in_dim(shard, place * part, part, 0)
    return lax.all_gather(piece, "fsdp", axis=0, tiled=False)


def gather_first(own):
    half = own.shape[0] // 2
    return swap(own[:half], 1), swap(own[half:], 2)


def gather_second(own, ax, by):
    half = own.shape[0] // 2
    return swap(jnp.stack([own[:half], ax]), 2), swap(jnp.stack([own[half:], by]), 1)


def gather_last(own, ax, by, a2, b2):
    shards, part, cols = own.shape
    place = lax.axis_index("dp") % GROUP
    near = (own, ax, by, a2, b2)
    far = tuple(swap(v, 0) for v in near)
    full = pl.pallas_call(
        partial(assemble_kernel, shards // 2),
        out_shape=jax.ShapeDtypeStruct((shards, GROUP, part, cols), own.dtype),
        grid_spec=pltpu.PrefetchScalarGridSpec(
            num_scalar_prefetch=1,
            grid=(1,),
            in_specs=[pl.BlockSpec(memory_space=pl.ANY)] * 10,
            out_specs=pl.BlockSpec(memory_space=pl.ANY),
            scratch_shapes=[
                pltpu.VMEM((shards, GROUP, part, cols), own.dtype),
                pltpu.SemaphoreType.DMA((14,)),
            ],
        ),
        name="assemble",
    )(place.astype(jnp.int32).reshape(1), *near, *far)
    return full.reshape(shards * GROUP * part, cols)


def plane_gather(value, axis):
    size = lax.axis_size("dp")
    groups = None
    if size > GROUP:
        groups = [[g * GROUP + i for i in range(GROUP)] for g in range(size // GROUP)]
    return lax.all_gather(value, "dp", axis=axis, tiled=False, axis_index_groups=groups)


def rest_sum(value):
    size = lax.axis_size("dp")
    if size == GROUP:
        return value
    groups = [[g * GROUP + i for g in range(size // GROUP)] for i in range(GROUP)]
    return lax.psum(value, "dp", axis_index_groups=groups)


def pick(value, index, axis):
    return lax.dynamic_index_in_dim(value, index, axis, keepdims=False)


def add_low(left, right):
    return (left.astype(jnp.float32) + right.astype(jnp.float32)).astype(LOW)


def axes():
    place = lax.axis_index("dp") % GROUP
    return (place >> 1) & 1, place >> 2


def sum_first(pair):
    shards = lax.axis_size("fsdp")
    rows, cols = pair.shape
    cube = pair.reshape(shards, 2, 2, rows // shards // 4, cols)
    x, y = axes()
    half = shards // 2
    top, low = cube[:half], cube[half:]
    return top, low, swap(pick(top, 1 - x, 2), 1), swap(pick(low, 1 - y, 1), 2)


def sum_second(top, low, top_got, low_got):
    x, y = axes()
    top = add_low(pick(top, x, 2), top_got)
    low = add_low(pick(low, y, 1), low_got)
    return top, low, swap(pick(top, 1 - y, 1), 2), swap(pick(low, 1 - x, 1), 1)


def sum_third(top, low, top_got, low_got):
    x, y = axes()
    top = add_low(pick(top, y, 1), top_got)
    low = add_low(pick(low, x, 1), low_got)
    both = jnp.concatenate([top, low], axis=0)
    shards, part, cols = both.shape
    piece = lax.psum_scatter(
        both.reshape(shards * part, cols), "fsdp", scatter_dimension=0, tiled=True
    )
    return rest_sum(piece)


def sum_last(piece, blocks):
    part, cols = piece.shape
    every = plane_gather(piece, axis=0).reshape(4, 2, part, blocks, cols // blocks)
    every = every.transpose(0, 2, 3, 1, 4)
    return every.reshape(4 * part, 2 * cols).astype(jnp.float32)


def small_sum(value):
    shards = lax.axis_size("fsdp")
    value = value.astype(LOW)
    for bit in range(3):
        value = add_low(value, swap(value, bit))
    value = rest_sum(value)
    me = lax.axis_index("fsdp")
    total = pick(value, me, 0).astype(jnp.float32)
    for step in range(1, shards):
        send = pick(value, (me + step) % shards, 0)
        got = lax.ppermute(send, "fsdp", [(i, (i + step) % shards) for i in range(shards)])
        total = total + got.astype(jnp.float32)
    return total


def per_device(
    tokens,
    output_grad,
    group_member,
    image_counts,
    position_source,
    position_table,
    first_gain,
    first_shift,
    input_proj,
    query_bias,
    value_bias,
    output_proj,
    output_bias,
    second_gain,
    second_shift,
    hidden_weight,
    hidden_bias,
    return_weight,
    return_bias,
):
    dp_size = lax.axis_size("dp")
    fsdp_size = lax.axis_size("fsdp")
    core = (lax.axis_index("dp") & 1).astype(jnp.int32)
    mine, other = core.reshape(1), (1 - core).reshape(1)
    small_parts = (
        first_gain,
        first_shift,
        query_bias,
        value_bias,
        output_bias,
        second_gain,
        second_shift,
        return_bias,
        hidden_bias,
        position_table.reshape(-1),
    )
    sizes = [v.shape[0] for v in small_parts]
    joined = jnp.concatenate(small_parts)
    pad = -joined.shape[0] % 2048
    joined = jnp.pad(joined, (0, pad)).reshape(-1, 128)
    joint_own = gather_piece(input_proj)
    smalls = lax.all_gather(joined, "fsdp", axis=0, tiled=False).reshape(fsdp_size, -1)
    smalls = smalls.astype(jnp.float32)
    offsets = [sum(sizes[:i]) for i in range(len(sizes))]
    vectors = [smalls[:, o : o + n] for o, n in zip(offsets, sizes)]
    (
        gain_one,
        shift_one,
        query_add,
        value_add,
        output_add,
        gain_two,
        shift_two,
        return_add,
        hidden_add,
    ) = [v.reshape(-1) for v in vectors[:9]]
    table_full = (
        vectors[9].reshape(fsdp_size, SMALL_LEN, -1).transpose(1, 0, 2).reshape(SMALL_LEN, D)
    )
    member = group_member[0]
    is_large = member == 1
    length = jnp.where(is_large, LARGE_LEN, SMALL_LEN)
    step = jnp.where(is_large, LARGE_LEN, 3 * SMALL_LEN)
    group_high = dp_size * 7 // 16
    group_low = dp_size - group_high
    counts = image_counts.astype(jnp.float32)
    share = jnp.where(is_large, counts[1], counts[0]) / (counts[0] + counts[1])
    images = jnp.where(
        is_large,
        group_high * fsdp_size * (ROWS // LARGE_LEN),
        group_low * fsdp_size * (ROWS // SMALL_LEN),
    ).astype(jnp.float32)
    factor = share / images
    scale = factor.reshape(1)

    row_index = jnp.arange(PAD, dtype=jnp.int32)
    place = row_index % length
    inter = interp_table(position_source)
    identity = (
        jnp.arange(LARGE_LEN, dtype=jnp.int32)[:, None]
        == jnp.arange(SMALL_LEN, dtype=jnp.int32)[None, :]
    ).astype(jnp.float32)
    mixing = jnp.where(is_large, inter, identity)
    picker = (place[:, None] == jnp.arange(LARGE_LEN, dtype=jnp.int32)[None, :]).astype(jnp.float32)
    spread = jnp.dot(picker, mixing, precision=lax.Precision.HIGHEST)
    position = jnp.dot(spread, table_full, precision=lax.Precision.HIGHEST)
    grad_pad = jnp.pad(output_grad, ((0, PAD - ROWS), (0, 0)))
    stream = jnp.pad(tokens, ((0, PAD - ROWS), (0, 0))).astype(jnp.float32) + position
    first_out, first_hat, first_inv = layer_norm(stream, gain_one, shift_one)
    first_low = first_out.astype(LOW)

    ax, by = gather_first(joint_own)
    a2, b2 = gather_second(joint_own, ax, by)
    outer_own = gather_piece(after(jnp.concatenate([output_proj, hidden_weight], axis=1), joint_own))
    joint_proj = gather_last(joint_own, ax, by, a2, b2)

    first_low = after(first_low, outer_own)
    outer_ax, outer_by = gather_first(outer_own)
    return_own = gather_piece(after(return_weight, outer_own))
    joint_add = jnp.concatenate([query_add, jnp.zeros_like(query_add), value_add])
    projected = jnp.dot(first_low, joint_proj, preferred_element_type=jnp.float32)
    projected = (projected + joint_add).astype(LOW)
    projected = after(projected, outer_ax, outer_by)
    outer_a2, outer_b2 = gather_second(outer_own, outer_ax, outer_by)
    attended = attend_forward(jnp.stack([length, step]), projected)
    attended = after(attended, outer_a2, outer_b2, return_own)
    return_ax, return_by = gather_first(return_own)
    outer = gather_last(outer_own, outer_ax, outer_by, outer_a2, outer_b2)
    outproj_full, hidden_full = outer[:, :D], outer[:, D:]
    mid = stream + jnp.dot(attended, outproj_full, preferred_element_type=jnp.float32) + output_add
    second_out, second_hat, second_inv = layer_norm(mid, gain_two, shift_two)
    second_low = second_out.astype(LOW)
    second_low = after(second_low, return_ax, return_by)
    return_a2, return_b2 = gather_second(return_own, return_ax, return_by)
    activ, slope = hidden_layer(second_low, hidden_full, hidden_add)
    activ, slope, return_a2, return_b2 = lax.optimization_barrier(
        (activ, slope, return_a2, return_b2)
    )
    return_full = gather_last(return_own, return_ax, return_by, return_a2, return_b2)

    return_send = grad_half(other, scale, activ, grad_pad)
    return_got = swap(return_send, 0)
    grad_hidden, grad_hidden_add = hidden_back(after(grad_pad, return_send), return_full, slope)
    return_pair = grad_half(mine, scale, activ, after(grad_pad, grad_hidden), return_got)
    return_one = sum_first(return_pair)

    hidden_send = grad_half(other, scale, after(second_low, return_pair), grad_hidden, tile_m=1024)
    hidden_got = swap(hidden_send, 0)
    hidden_pair = grad_half(
        mine, scale, after(second_low, hidden_send), grad_hidden, hidden_got, tile_m=1024
    )
    grad_hidden = after(grad_hidden, hidden_pair, *return_one)
    return_two = sum_second(*return_one)
    hidden_one = sum_first(hidden_pair)
    grad_second = dot_nt(grad_hidden, hidden_full)
    grad_mid_norm, grad_gain_two, grad_shift_two = norm_back(
        grad_second, second_hat, second_inv, gain_two
    )
    grad_mid = grad_pad.astype(jnp.float32) + grad_mid_norm
    grad_branch = grad_mid.astype(LOW)
    grad_output_add = jnp.sum(grad_branch.astype(jnp.float32), axis=0)
    grad_branch = after(grad_branch, *return_two)
    return_piece = sum_third(*return_two)
    output_send = grad_half(other, scale, attended, grad_branch)
    output_got = swap(output_send, 0)
    grad_att = dot_nt(after(grad_branch, output_send), outproj_full).astype(LOW)
    output_pair = grad_half(mine, scale, attended, after(grad_branch, grad_att), output_got)
    grad_att = after(grad_att, output_pair, *hidden_one)
    hidden_two = sum_second(*hidden_one)
    output_one = sum_first(output_pair)
    numbers = jnp.stack([length, step, 1 - core])
    heads_other = attend_backward(numbers, projected, grad_att)
    joint_send = grad_half(other, scale, first_low, heads_other, tile_m=1024)
    joint_got = swap(joint_send, 0)
    grad_att = after(grad_att, joint_send, *hidden_two, *output_one, return_piece)
    hidden_piece = sum_third(*hidden_two)
    output_two = sum_second(*output_one)
    return_w_out = sum_last(return_piece, 1)
    numbers = jnp.stack([length, step, core])
    heads_mine = attend_backward(numbers, projected, grad_att)
    joint_pair = grad_half(
        mine, scale, first_low, after(heads_mine, *output_two), joint_got, tile_m=1024
    )
    joint_one = sum_first(joint_pair)
    output_piece = sum_third(*output_two)
    heads_other = after(heads_other, joint_pair)
    low_heads = jnp.where(core == 0, heads_mine, heads_other)
    high_heads = jnp.where(core == 0, heads_other, heads_mine)
    grad_first = 0.0
    for i in range(3):
        base = i * D
        grad_first = grad_first + dot_nt(low_heads[i], joint_proj[:, base : base + 512])
        grad_first = grad_first + dot_nt(high_heads[i], joint_proj[:, base + 512 : base + D])
    head_sums = [
        jnp.concatenate([jnp.sum(h[i].astype(jnp.float32), axis=0) for h in (low_heads, high_heads)])
        for i in (0, 2)
    ]
    grad_query_add, grad_value_add = head_sums
    grad_stream_norm, grad_gain_one, grad_shift_one = norm_back(
        grad_first, first_hat, first_inv, gain_one
    )
    grad_stream = grad_mid + grad_stream_norm
    tokens_grad = grad_stream[:ROWS].astype(LOW)
    in_rows = (row_index < ROWS)[:, None]
    grad_table = jnp.dot(
        jnp.where(in_rows, spread, 0.0).T, grad_stream, precision=lax.Precision.HIGHEST
    )
    activ = after(activ, grad_stream, *joint_one)
    joint_two = sum_second(*joint_one)
    hidden_w_out = sum_last(hidden_piece, 1)
    outproj_out = sum_last(output_piece, 1)
    returned = jnp.dot(activ, return_full, preferred_element_type=jnp.float32) + return_add
    block_out = (mid + returned)[:ROWS].astype(LOW)
    joint_piece = sum_third(*joint_two)
    joint_out = sum_last(joint_piece, 3)
    grad_return_add = jnp.sum(output_grad.astype(jnp.float32), axis=0)
    table_rows = grad_table.reshape(SMALL_LEN, fsdp_size, -1).transpose(1, 0, 2)
    small_grads = (
        grad_gain_one,
        grad_shift_one,
        grad_query_add,
        grad_value_add,
        grad_output_add,
        grad_gain_two,
        grad_shift_two,
        grad_return_add,
        grad_hidden_add,
        table_rows,
    )
    packed = jnp.concatenate([v.reshape(fsdp_size, -1) for v in small_grads], axis=1) * factor
    packed = jnp.pad(packed, ((0, 0), (0, pad))).reshape(fsdp_size, -1, 128)
    summed = small_sum(packed).reshape(-1)
    small_outs = [summed[o : o + n] for o, n in zip(offsets, sizes)]
    return (
        block_out,
        tokens_grad,
        small_outs[9].reshape(SMALL_LEN, -1),
        small_outs[0],
        small_outs[1],
        joint_out,
        small_outs[2],
        small_outs[3],
        outproj_out,
        small_outs[4],
        small_outs[5],
        small_outs[6],
        hidden_w_out,
        small_outs[8],
        return_w_out,
        small_outs[7],
    )


def solution(mesh):
    in_specs = (
        P(("dp", "fsdp"), None),
        P(("dp", "fsdp"), None),
        P("dp"),
        P(),
        P(),
        P(None, "fsdp"),
        P("fsdp"),
        P("fsdp"),
        P("fsdp", None),
        P("fsdp"),
        P("fsdp"),
        P("fsdp", None),
        P("fsdp"),
        P("fsdp"),
        P("fsdp"),
        P("fsdp", None),
        P("fsdp"),
        P("fsdp", None),
        P("fsdp"),
    )
    out_specs = (
        P(("dp", "fsdp"), None),
        P(("dp", "fsdp"), None),
        P(None, "fsdp"),
        P("fsdp"),
        P("fsdp"),
        P("fsdp", None),
        P("fsdp"),
        P("fsdp"),
        P("fsdp", None),
        P("fsdp"),
        P("fsdp"),
        P("fsdp"),
        P("fsdp", None),
        P("fsdp"),
        P("fsdp", None),
        P("fsdp"),
    )
    return jax.shard_map(
        per_device, mesh=mesh, in_specs=in_specs, out_specs=out_specs, check_vma=False
    )
```

time: 1720 us -> 753 us (0.44)
  Pallas kernels: 703 us -> 209 us
  matrix products: 342 us -> 124 us
  starting transfers between devices: 120 us -> 42.3 us
  local copies, waits for them, and re-layouts: 178 us -> 101 us
  waiting for transfers between devices: 160 us -> 123 us
  loops' own time: 33.6 us -> 0 us
  blocking collectives: 69.5 us -> 45.1 us
    pallas_call x3 -> x16, Pallas kernels: 703 us -> 209 us  [the longest x8 76.6 us: grad_half(): pl.pallas_call(grad_kernel, out_shape=jax.ShapeDtypeStruct((rows, cols),...]
    dot_general x19 -> x11, matrix products: 319 us -> 101 us  [the longest x8 71.4 us: dot_nt(): lax.dot_general(left, right, (((1,), (1,)), ((), ())), preferred_element_...]
    ppermute x50, starting transfers between devices: 115 us -> 38.5 us  [swap(): return lax.ppermute(value, 'dp', [(i, i ^ 1 << bit) for i in range(size)])]
    all_gather x4 -> x3, waiting for transfers between devices: 62.8 us -> 0.01 us  [plane_gather(): lax.all_gather(value, 'dp', axis=axis, tiled=False, axis_index_groups=gro...]
    reshape x9 -> x0, local copies, waits for them, and re-layouts: 62 us -> none  [the longest x2 17.9 us: image_scores(): query_img = query_low.reshape(images, length, HEADS, HEAD_DIM)]
    convert_element_type x29 -> x24, other arithmetic: 60.9 us -> 23.6 us  [the longest x19 9.85 us: add_low(): return (left.astype(jnp.float32) + right.astype(jnp.float32)).astype(LOW)]
    unnamed x2 -> x0, loops' own time: 33.6 us -> none
    convert_element_type x8 -> x6, local copies, waits for them, and re-layouts: 58.2 us -> 25.5 us  [sum_last(): return every.reshape(4 * part, 2 * cols).astype(jnp.float32)]
  transfers between devices with their start and end apart: 63 -> 62, of which waited for: 20 -> 19; matrix products, arithmetic and copies ran while one was open for 20% -> 37% of each run, Pallas kernels for 26% -> 23%
where the time goes in v2:
time: 753 us; the launch traced here: 742 us
  Pallas kernels  209 us (28%)
  matrix products  124 us (16%)
  waiting for transfers between devices  123 us (16%)
  local copies, waits for them, and re-layouts  101 us (13%)
  other arithmetic  79.1 us (11%)
  blocking collectives  45.1 us (6%)
  starting transfers between devices  42.3 us (6%)
  between operations  18.8 us (2%)
    ppermute x50, waiting for transfers between devices, swap(): return lax.ppermute(value, 'dp', [(i, i ^ 1 << bit) for i in range(size)])  123 us
    pallas_call x8, Pallas kernels, grad_half(): pl.pallas_call(grad_kernel, out_shape=jax.ShapeDtypeStruct((rows, cols),...  76.6 us
    dot_general x8, matrix products, dot_nt(): lax.dot_general(left, right, (((1,), (1,)), ((), ())), preferred_element_...  71.4 us
    pallas_call x2, Pallas kernels, attend_backward(): pl.pallas_call(backward_kernel, out_shape=jax.ShapeDtypeStruct((3, PAD, w...  43.8 us
    ppermute x50, starting transfers between devices, swap(): return lax.ppermute(value, 'dp', [(i, i ^ 1 << bit) for i in range(size)])  38.5 us
    unnamed x138, local copies, waits for them, and re-layouts  29.7 us
    pallas_call x1, Pallas kernels, hidden_layer(): pl.pallas_call(partial(hidden_kernel, 184), out_shape=[jax.ShapeDtypeStru...  27.5 us
    convert_element_type x6, local copies, waits for them, and re-layouts, sum_last(): return every.reshape(4 * part, 2 * cols).astype(jnp.float32)  25.5 us
  transfers between devices with their start and end apart: 62, of which 19 were waited for; matrix products, arithmetic and copies ran while one was open for 37% of the time, Pallas kernels for 23%

profile of v2, /device:TPU:0, one launch (start us, length us, event | category | flops | bytes accessed | tf_op | source)
XLA Modules:
  0.0 742.3 jit_solution(3657876439921953599)
XLA Ops:
  8.4 21.3 %all-gather = bf16[128,3072]{1,0:T(8,128)(2,1)S(1)} all-gather(bf16[32,3072]{1,0:T(8,128)(2,1)S(1)} %constant_dynamic-slice_fusion.10), channel_id=2, replica_groups=mesh['dp'=8,'fsdp'=4] {'fsdp'}, dimensions={0}, use_global_device_ids=true | all-gather | bytes 983040 | tf_op jit(solution)/shard_map/all_gather | solution.py:382
  38.6 14.5 %all_gather.45 = bf16[4,128,128]{2,1,0:T(8,128)(2,1)S(1)} all-gather(bf16[1,128,128]{2,1,0:T(8,128)(2,1)S(1)} %pad_bitcast_fusion.1), channel_id=1, replica_groups=mesh['dp'=8,'fsdp'=4] {'fsdp'}, dimensions={0}, use_global_device_ids=true | all-gather | bytes 163840 | tf_op jit(solution)/shard_map/all_gather | solution.py:540
  59.6 7.3 fusion.64
  82.9 11.5 %collective-permute-done.2.refs_3_ = bf16[2,2,32,3072]{3,2,1,0:T(8,128)(2,1)} collective-permute-done((bf16[2,2,32,3072]{3,2,1,0:T(8,128)(2,1)}, bf16[2,2,32,3072]{3,2,1,0:T(8,128)(2,1)}, u32[]{:S(2)}, u32[]{:S(2)}) %collective-permute-start.2) | collective-permute-done | bytes 786464 | tf_op jit(solution)/shard_map/ppermute | solution.py:350
  97.2 8.2 %collective-permute-done.10.refs_2_ = bf16[2,32,5120]{2,1,0:T(8,128)(2,1)} collective-permute-done((bf16[2,32,5120]{2,1,0:T(8,128)(2,1)}, bf16[2,32,5120]{2,1,0:T(8,128)(2,1)}, u32[]{:S(2)}, u32[]{:S(2)}) %collective-permute-start.10) | collective-permute-done | bytes 655392 | tf_op jit(solution)/shard_map/ppermute | solution.py:350
  146.3 14.7 %add_convert_fusion.q_ref.k_ref.v_ref = bf16[1472,3072]{1,0:T(8,128)(2,1)} fusion(bf16[1472,1024]{1,0:T(8,128)(2,1)} %add_convert_fusion.2.a_ref, bf16[1024,3072]{1,0:T(8,128)(2,1)} %bitcast.289, f32[3072]{0:T(1024)S(1)} %pad_maximum_fusion.11), kind=kOutput, calls=%fused_computation | convolution fusion | flops 9270067200 | bytes 18362368 | tf_op jit(solution)/shard_map/dot_general | solution.py:599
  161.0 19.7 %attend_forward.1.a_ref = bf16[1472,1024]{1,0:T(8,128)(2,1)} custom-call(s32[2]{0:T(128)} %pad_add_fusion.s_ref, bf16[1472,3072]{1,0:T(8,128)(2,1)} %add_convert_fusion.q_ref.k_ref.v_ref, bf16[1472,3072]{1,0:T(8,128)(2,1)} %add_convert_fusion.q_ref.k_ref.v_ref, bf16[1472,3072]{1,0:T(8,128)(2,1)} %add_convert_fusion.q_ref.k_ref.v_ref), custom_call_target="tpu_custom_call" | custom-call | tf_op jit(solution)/shard_map/attend_forward/pallas_call | solution.py:212
  187.0 8.0 %assemble.4 = bf16[4,8,32,5120]{3,2,1,0:T(8,128)(2,1)} custom-call(s32[1]{0:T(128)} %bitcast.7.d_ref, bf16[4,32,5120]{2,1,0:T(8,128)(2,1)} %bitcast.309, bf16[2,32,5120]{2,1,0:T(8,128)(2,1)} %copy-done.13, bf16[2,32,5120]{2,1,0:T(8,128)(2,1)} %collective-permute-done.10.refs_2_, bf16[2,2,32,5120]{3,2,1,0:T(8,128)(2,1)} %collective-permute-done.11.refs_3_, ...), custom_call_target="tpu_custom_call" | custom-call | tf_op jit(solution)/shard_map/assemble/pallas_call | solution.py:400
  195.1 8.1 %fusion.65 = (f32[1472]{0:T(1024)S(1)}, f32[1472,1024]{1,0:T(8,128)S(1)}) fusion(f32[1024]{0:T(1024)S(1)} %bitcast.351, f32[1472,1024]{1,0:T(8,128)} %get-tuple-element.133, bf16[1472,1024]{1,0:T(8,128)(2,1)} %attend_forward.1.a_ref, bf16[1024,5120]{1,0:T(8,128)(2,1)} %bitcast.280), kind=kOutput, calls=%fused_computation.237 | convolution fusion | flops 3091528192 | bytes 17180416 | tf_op jit(solution)/shard_map/dot_general | solution.py:608
  206.5 7.7 %slice.312.w_ref = bf16[1024,4096]{1,0:T(8,128)(2,1)} slice(bf16[1024,5120]{1,0:T(8,128)(2,1)} %bitcast.281), slice={[0:1024], [1024:5120]} | slice | bytes 16777216 | tf_op jit(solution)/shard_map/slice | solution.py:607
  218.9 27.5 %hidden_layer.1 = (bf16[1472,4096]{1,0:T(8,128)(2,1)}, bf16[1472,4096]{1,0:T(8,128)(2,1)}) custom-call(bf16[1472,1024]{1,0:T(8,128)(2,1)} %add_convert_fusion.1.x_ref.a_ref, bf16[1024,4096]{1,0:T(8,128)(2,1)} %slice.312.w_ref, f32[1,4096]{1,0:T(1,128)} %bitcast.342), custom_call_target="tpu_custom_call" | custom-call | tf_op jit(solution)/shard_map/hidden_layer/pallas_call | solution.py:260
  247.4 12.9 %grad_send.4 = bf16[4096,512]{1,0:T(8,128)(2,1)} custom-call(s32[1]{0:T(128)} %bitcast.29.c_ref, f32[1]{0:T(128)} %bitcast.32.f_ref, bf16[1472,4096]{1,0:T(8,128)(2,1)} %get-tuple-element.68.a_ref, bf16[1472,1024]{1,0:T(8,128)(2,1)} %pad.18.b_ref.g_ref), custom_call_target="tpu_custom_call" | custom-call | tf_op jit(solution)/shard_map/grad_send/pallas_call | solution.py:335
  261.4 10.7 %collective-permute-done.23.refs_6_ = bf16[2,128,1024]{2,1,0:T(8,128)(2,1)S(1)} collective-permute-done((bf16[2,128,1024]{2,1,0:T(8,128)(2,1)S(1)}, bf16[2,128,1024]{2,1,0:T(8,128)(2,1)S(1)}, u32[]{:S(2)}, u32[]{:S(2)}) %collective-permute-start.23) | collective-permute-done | bytes 524320 | tf_op jit(solution)/shard_map/ppermute | solution.py:350
  282.8 21.0 %hidden_back.1 = (bf16[1472,4096]{1,0:T(8,128)(2,1)}, f32[1,4096]{1,0:T(1,128)}) custom-call(bf16[1472,1024]{1,0:T(8,128)(2,1)} %pad.18.b_ref.g_ref, bf16[4096,1024]{1,0:T(8,128)(2,1)} %bitcast.284, bf16[1472,4096]{1,0:T(8,128)(2,1)} %get-tuple-element.55.slope_ref), custom_call_target="tpu_custom_call" | custom-call | tf_op jit(solution)/shard_map/hidden_back/pallas_call | solution.py:288
  303.8 13.5 %grad_keep.4 = bf16[4096,512]{1,0:T(8,128)(2,1)} custom-call(s32[1]{0:T(128)} %bitcast.34.c_ref, f32[1]{0:T(128)} %bitcast.32.f_ref, bf16[1472,4096]{1,0:T(8,128)(2,1)} %get-tuple-element.68.a_ref, bf16[1472,1024]{1,0:T(8,128)(2,1)} %pad.18.b_ref.g_ref, bf16[4096,512]{1,0:T(8,128)(2,1)} %collective-permute-done.27.refs_0_), custom_call_target="tpu_custom_call" | custom-call | tf_op jit(solution)/shard_map/grad_keep/pallas_call | solution.py:335
  317.2 10.7 %grad_send.5 = bf16[1024,2048]{1,0:T(8,128)(2,1)} custom-call(s32[1]{0:T(128)} %bitcast.29.c_ref, f32[1]{0:T(128)} %bitcast.32.f_ref, bf16[1472,1024]{1,0:T(8,128)(2,1)} %add_convert_fusion.1.x_ref.a_ref, bf16[1472,4096]{1,0:T(8,128)(2,1)} %get-tuple-element.60.b_ref), custom_call_target="tpu_custom_call" | custom-call | tf_op jit(solution)/shard_map/grad_send/pallas_call | solution.py:335
  338.0 20.7 %collective-permute-done.30 = bf16[2,2,256,512]{3,2,1,0:T(8,128)(2,1)} collective-permute-done((bf16[2,2,256,512]{3,2,1,0:T(8,128)(2,1)}, bf16[2,2,256,512]{3,2,1,0:T(8,128)(2,1)}, u32[]{:S(2)}, u32[]{:S(2)}) %collective-permute-start.30) | collective-permute-done | bytes 1048608 | tf_op jit(solution)/shard_map/ppermute | solution.py:350
  365.9 7.6 %collective-permute-done.32 = bf16[2,256,512]{2,1,0:T(8,128)(2,1)S(1)} collective-permute-done((bf16[2,256,512]{2,1,0:T(8,128)(2,1)S(1)}, bf16[2,256,512]{2,1,0:T(8,128)(2,1)S(1)}, u32[]{:S(2)}, u32[]{:S(2)}) %collective-permute-start.32) | collective-permute-done | bytes 524320 | tf_op jit(solution)/shard_map/ppermute | solution.py:350
  377.8 11.5 %grad_keep.5 = bf16[1024,2048]{1,0:T(8,128)(2,1)} custom-call(s32[1]{0:T(128)} %bitcast.34.c_ref, f32[1]{0:T(128)} %bitcast.32.f_ref, bf16[1472,1024]{1,0:T(8,128)(2,1)} %add_convert_fusion.1.x_ref.a_ref, bf16[1472,4096]{1,0:T(8,128)(2,1)} %get-tuple-element.60.b_ref, bf16[1024,2048]{1,0:T(8,128)(2,1)} %collective-permute-done.28.refs_0_), custom_call_target="tpu_custom_call" | custom-call | tf_op jit(solution)/shard_map/grad_keep/pallas_call | solution.py:335
  392.3 22.0 %multiply_reduce_fusion = (f32[1024]{0:T(1024)S(1)}, f32[1472]{0:T(1024)S(1)}, f32[1472]{0:T(1024)S(1)}, f32[1024]{0:T(1024)S(1)}, f32[1472,1024]{1,0:T(8,128)}) fusion(f32[1472,1024]{1,0:T(8,128)} %copy-done.2, f32[1472]{0:T(1024)S(1)} %add_rsqrt_fusion, f32[1472]{0:T(1024)S(1)} %broadcast_multiply_fusion.4, f32[1024]{0:T(1024)S(1)} %bitcast.344, ...), kind=kOutput, calls=%fused_computation.1 | convolution fusion | flops 12361592832 | bytes 32541696 | tf_op jit(solution)/shard_map/dot_general | solution.py:77
  430.9 8.1 %collective-permute-done.34 = bf16[2,2,64,2048]{3,2,0,1:T(8,128)(2,1)} collective-permute-done((bf16[2,2,64,2048]{3,2,0,1:T(8,128)(2,1)}, bf16[2,2,64,2048]{3,2,0,1:T(8,128)(2,1)}, u32[]{:S(2)}, u32[]{:S(2)}) %collective-permute-start.34) | collective-permute-done | bytes 1048608 | tf_op jit(solution)/shard_map/ppermute | solution.py:350
  457.8 21.9 %attend_backward.2.b_ref = bf16[3,1472,512]{2,1,0:T(8,128)(2,1)} custom-call(s32[3]{0:T(128)} %pad_add_fusion.3.s_ref, bf16[1472,3072]{1,0:T(8,128)(2,1)} %add_convert_fusion.q_ref.k_ref.v_ref, bf16[1472,3072]{1,0:T(8,128)(2,1)} %add_convert_fusion.q_ref.k_ref.v_ref, bf16[1472,3072]{1,0:T(8,128)(2,1)} %add_convert_fusion.q_ref.k_ref.v_ref, ...), custom_call_target="tpu_custom_call" | custom-call | tf_op jit(solution)/shard_map/attend_backward/pallas_call | solution.py:233
  479.7 8.9 %grad_send.7 = bf16[1024,1536]{1,0:T(8,128)(2,1)} custom-call(s32[1]{0:T(128)} %bitcast.29.c_ref, f32[1]{0:T(128)} %bitcast.32.f_ref, bf16[1472,1024]{1,0:T(8,128)(2,1)} %add_convert_fusion.2.a_ref, bf16[3,1472,512]{2,1,0:T(8,128)(2,1)} %attend_backward.2.b_ref), custom_call_target="tpu_custom_call" | custom-call | tf_op jit(solution)/shard_map/grad_send/pallas_call | solution.py:335
  494.1 6.9 collective-permute-done.39
  508.2 22.0 %attend_backward.3.b_ref = bf16[3,1472,512]{2,1,0:T(8,128)(2,1)} custom-call(s32[3]{0:T(128)} %pad_add_fusion.1.s_ref, bf16[1472,3072]{1,0:T(8,128)(2,1)} %add_convert_fusion.q_ref.k_ref.v_ref, bf16[1472,3072]{1,0:T(8,128)(2,1)} %add_convert_fusion.q_ref.k_ref.v_ref, bf16[1472,3072]{1,0:T(8,128)(2,1)} %add_convert_fusion.q_ref.k_ref.v_ref, ...), custom_call_target="tpu_custom_call" | custom-call | tf_op jit(solution)/shard_map/attend_backward/pallas_call | solution.py:233
  530.1 9.4 %grad_keep.7 = bf16[1024,1536]{1,0:T(8,128)(2,1)} custom-call(s32[1]{0:T(128)} %bitcast.34.c_ref, f32[1]{0:T(128)} %bitcast.32.f_ref, bf16[1472,1024]{1,0:T(8,128)(2,1)} %add_convert_fusion.2.a_ref, bf16[3,1472,512]{2,1,0:T(8,128)(2,1)} %attend_backward.3.b_ref, bf16[1024,1536]{1,0:T(8,128)(2,1)} %collective-permute-done.42.refs_0_), custom_call_target="tpu_custom_call" | custom-call | tf_op jit(solution)/shard_map/grad_keep/pallas_call | solution.py:335
  544.4 20.2 %collective-permute-done.44 = bf16[2,2,64,1536]{3,2,1,0:T(8,128)(2,1)S(1)} collective-permute-done((bf16[2,2,64,1536]{3,2,1,0:T(8,128)(2,1)S(1)}, bf16[2,2,64,1536]{3,2,1,0:T(8,128)(2,1)S(1)}, u32[]{:S(2)}, u32[]{:S(2)}) %collective-permute-start.44) | collective-permute-done | bytes 786464 | tf_op jit(solution)/shard_map/ppermute | solution.py:350
  569.9 8.1 %collective-permute-done.52 = bf16[2,64,1536]{2,1,0:T(8,128)(2,1)S(1)} collective-permute-done((bf16[2,64,1536]{2,1,0:T(8,128)(2,1)S(1)}, bf16[2,64,1536]{2,1,0:T(8,128)(2,1)S(1)}, u32[]{:S(2)}, u32[]{:S(2)}) %collective-permute-start.52) | collective-permute-done | bytes 393248 | tf_op jit(solution)/shard_map/ppermute | solution.py:350
  614.4 17.7 %multiply_reduce_fusion.1 = (f32[1024]{0:T(1024)S(1)}, f32[1472]{0:T(1024)S(1)}, f32[1472]{0:T(1024)S(1)}, f32[1024]{0:T(1024)S(1)}, f32[1472,1024]{1,0:T(8,128)}) fusion(f32[1472,1024]{1,0:T(8,128)} %get-tuple-element.133, f32[1472]{0:T(1024)S(1)} %copy-done.29, f32[1472]{0:T(1024)S(1)} %copy-done.27, f32[1024]{0:T(1024)S(1)} %bitcast.340, ...), kind=kOutput, calls=%fused_computation.3 | convolution fusion | flops 1564601344 | bytes 44796928 | tf_op jit(solution)/shard_map/dot_general | solution.py:77
  632.1 7.2 multiply_add_fusion
  649.0 9.4 %all-gather.4 = bf16[512,512]{1,0:T(8,128)(2,1)S(1)} all-gather(bf16[64,512]{1,0:T(8,128)(2,1)} %reduce-scatter.9.cloned.1.call-done), channel_id=6, replica_groups=mesh['dp'=8,'fsdp'=4] {'dp'}, dimensions={0}, use_global_device_ids=true | all-gather | bytes 589824 | tf_op jit(solution)/shard_map/all_gather | solution.py:423
  682.5 17.5 %fusion.66 = f32[1472,1024]{1,0:T(8,128)S(1)} fusion(bf16[1472,4096]{1,0:T(8,128)(2,1)} %get-tuple-element.68.a_ref, bf16[4096,1024]{1,0:T(8,128)(2,1)} %bitcast.285), kind=kOutput, calls=%fused_computation.238 | convolution fusion | flops 12348030976 | bytes 26476544 | tf_op jit(solution)/shard_map/dot_general | solution.py:690
  (412 shorter events, 287.3 us)
Async XLA Ops:
  7.3 66.9 %all-gather.13.cloned.1.call-start = ((), (), s32[]{:S(2)}) async-start(), calls=%async_computation.8 | async-start | bytes 1638400 | tf_op jit(solution)/shard_map/all_gather | solution.py:382
  29.7 78.5 %collective-permute-start.4 = (bf16[4,32,3072]{2,1,0:T(8,128)(2,1)S(1)}, bf16[4,32,3072]{2,1,0:T(8,128)(2,1)}, u32[]{:S(2)}, u32[]{:S(2)}) collective-permute-start(bf16[4,32,3072]{2,1,0:T(8,128)(2,1)S(1)} %bitcast.304), channel_id=1, source_target_pairs={{0,4},{4,0},{8,12},{12,8},{16,20},{20,16},{24,28},{28,24},{1,5},{5... | collective-permute-start | bytes 2359304 | tf_op jit(solution)/shard_map/ppermute | solution.py:350
  32.7 91.2 %all-gather.15.cloned.1.call-start = ((), (), s32[]{:S(2)}) async-start(), calls=%async_computation.9 | async-start | bytes 1310720 | tf_op jit(solution)/shard_map/all_gather | solution.py:382
  33.6 37.9 %collective-permute-start = (bf16[2,32,3072]{2,1,0:T(8,128)(2,1)}, bf16[2,32,3072]{2,1,0:T(8,128)(2,1)S(1)}, u32[]{:S(2)}, u32[]{:S(2)}) collective-permute-start(bf16[2,32,3072]{2,1,0:T(8,128)(2,1)} %bitcast.8), channel_id=1, source_target_pairs={{0,8},{4,12},{8,0},{12,4},{16,24},{20,28},{24,16},{28,20},{1,9},{5... | collective-permute-start | bytes 1179656 | tf_op jit(solution)/shard_map/ppermute | solution.py:350
  35.1 45.1 %collective-permute-start.1 = (bf16[2,32,3072]{2,1,0:T(8,128)(2,1)}, bf16[2,32,3072]{2,1,0:T(8,128)(2,1)}, u32[]{:S(2)}, u32[]{:S(2)}) collective-permute-start(bf16[2,32,3072]{2,1,0:T(8,128)(2,1)} %bitcast.9), channel_id=1, source_target_pairs={{0,16},{4,20},{8,24},{12,28},{16,0},{20,4},{24,8},{28,12},{1,17},{... | collective-permute-start | bytes 1179656 | tf_op jit(solution)/shard_map/ppermute | solution.py:350
  77.7 27.6 %collective-permute-start.10 = (bf16[2,32,5120]{2,1,0:T(8,128)(2,1)}, bf16[2,32,5120]{2,1,0:T(8,128)(2,1)}, u32[]{:S(2)}, u32[]{:S(2)}) collective-permute-start(bf16[2,32,5120]{2,1,0:T(8,128)(2,1)} %bitcast.16), channel_id=1, source_target_pairs={{0,16},{4,20},{8,24},{12,28},{16,0},{20,4},{24,8},{28,12},{1,17},{... | collective-permute-start | bytes 1966088 | tf_op jit(solution)/shard_map/ppermute | solution.py:350
  80.2 427.9 %reduce-scatter.5.cloned.1.call-start = ((), (), s32[]{:S(2)}) async-start(), calls=%async_computation.4 | async-start | bytes 1310720 | tf_op jit(solution)/shard_map/reduce_scatter | solution.py:470
  81.4 41.9 %collective-permute-start.3 = (bf16[2,2,32,3072]{3,2,1,0:T(8,128)(2,1)S(1)}, bf16[2,2,32,3072]{3,2,1,0:T(8,128)(2,1)}, u32[]{:S(2)}, u32[]{:S(2)}) collective-permute-start(bf16[2,2,32,3072]{3,2,1,0:T(8,128)(2,1)S(1)} %pad_maximum_fusion.8), channel_id=1, source_target_pairs={{0,8},{4,12},{8,0},{12,4},{16,24},{20,28},{24,16},{28,20},{1,9},{5... | collective-permute-start | bytes 2359304 | tf_op jit(solution)/shard_map/ppermute | solution.py:350
  94.5 33.1 %collective-permute-start.7 = (bf16[2,2,32,3072]{3,2,1,0:T(8,128)(2,1)}, bf16[2,2,32,3072]{3,2,1,0:T(8,128)(2,1)}, u32[]{:S(2)}, u32[]{:S(2)}) collective-permute-start(bf16[2,2,32,3072]{3,2,1,0:T(8,128)(2,1)} %collective-permute-done.2.refs_3_), channel_id=1, source_target_pairs={{0,4},{4,0},{8,12},{12,8},{16,20},{20,16},{24,28},{28,24},{1,5},{5... | collective-permute-start | bytes 2359304 | tf_op jit(solution)/shard_map/ppermute | solution.py:350
  105.4 34.2 %collective-permute-start.11 = (bf16[2,2,32,5120]{3,2,1,0:T(8,128)(2,1)}, bf16[2,2,32,5120]{3,2,1,0:T(8,128)(2,1)}, u32[]{:S(2)}, u32[]{:S(2)}) collective-permute-start(bf16[2,2,32,5120]{3,2,1,0:T(8,128)(2,1)} %pad_maximum_fusion.1), channel_id=1, source_target_pairs={{0,16},{4,20},{8,24},{12,28},{16,0},{20,4},{24,8},{28,12},{1,17},{... | collective-permute-start | bytes 3932168 | tf_op jit(solution)/shard_map/ppermute | solution.py:350
  108.2 31.8 %collective-permute-start.12 = (bf16[2,2,32,5120]{3,2,1,0:T(8,128)(2,1)}, bf16[2,2,32,5120]{3,2,1,0:T(8,128)(2,1)}, u32[]{:S(2)}, u32[]{:S(2)}) collective-permute-start(bf16[2,2,32,5120]{3,2,1,0:T(8,128)(2,1)} %pad_maximum_fusion.2), channel_id=1, source_target_pairs={{0,8},{4,12},{8,0},{12,4},{16,24},{20,28},{24,16},{28,20},{1,9},{5... | collective-permute-start | bytes 3932168 | tf_op jit(solution)/shard_map/ppermute | solution.py:350
  133.9 51.0 %collective-permute-start.13 = (bf16[4,32,5120]{2,1,0:T(8,128)(2,1)S(1)}, bf16[4,32,5120]{2,1,0:T(8,128)(2,1)}, u32[]{:S(2)}, u32[]{:S(2)}) collective-permute-start(bf16[4,32,5120]{2,1,0:T(8,128)(2,1)S(1)} %bitcast.310), channel_id=1, source_target_pairs={{0,4},{4,0},{8,12},{12,8},{16,20},{20,16},{24,28},{28,24},{1,5},{5... | collective-permute-start | bytes 3932168 | tf_op jit(solution)/shard_map/ppermute | solution.py:350
  139.5 47.1 %collective-permute-start.14 = (bf16[2,32,5120]{2,1,0:T(8,128)(2,1)S(1)}, bf16[2,32,5120]{2,1,0:T(8,128)(2,1)}, u32[]{:S(2)}, u32[]{:S(2)}) collective-permute-start(bf16[2,32,5120]{2,1,0:T(8,128)(2,1)S(1)} %collective-permute-done.9.refs_1_), channel_id=1, source_target_pairs={{0,4},{4,0},{8,12},{12,8},{16,20},{20,16},{24,28},{28,24},{1,5},{5... | collective-permute-start | bytes 1966088 | tf_op jit(solution)/shard_map/ppermute | solution.py:350
  140.1 46.9 %collective-permute-start.15 = (bf16[2,32,5120]{2,1,0:T(8,128)(2,1)}, bf16[2,32,5120]{2,1,0:T(8,128)(2,1)}, u32[]{:S(2)}, u32[]{:S(2)}) collective-permute-start(bf16[2,32,5120]{2,1,0:T(8,128)(2,1)} %collective-permute-done.10.refs_2_), channel_id=1, source_target_pairs={{0,4},{4,0},{8,12},{12,8},{16,20},{20,16},{24,28},{28,24},{1,5},{5... | collective-permute-start | bytes 1966088 | tf_op jit(solution)/shard_map/ppermute | solution.py:350
  145.8 41.2 %collective-permute-start.16 = (bf16[2,2,32,5120]{3,2,1,0:T(8,128)(2,1)}, bf16[2,2,32,5120]{3,2,1,0:T(8,128)(2,1)}, u32[]{:S(2)}, u32[]{:S(2)}) collective-permute-start(bf16[2,2,32,5120]{3,2,1,0:T(8,128)(2,1)} %collective-permute-done.11.refs_3_), channel_id=1, source_target_pairs={{0,4},{4,0},{8,12},{12,8},{16,20},{20,16},{24,28},{28,24},{1,5},{5... | collective-permute-start | bytes 3932168 | tf_op jit(solution)/shard_map/ppermute | solution.py:350
  145.8 41.2 %collective-permute-start.17 = (bf16[2,2,32,5120]{3,2,1,0:T(8,128)(2,1)}, bf16[2,2,32,5120]{3,2,1,0:T(8,128)(2,1)}, u32[]{:S(2)}, u32[]{:S(2)}) collective-permute-start(bf16[2,2,32,5120]{3,2,1,0:T(8,128)(2,1)} %collective-permute-done.12.refs_4_), channel_id=1, source_target_pairs={{0,4},{4,0},{8,12},{12,8},{16,20},{20,16},{24,28},{28,24},{1,5},{5... | collective-permute-start | bytes 3932168 | tf_op jit(solution)/shard_map/ppermute | solution.py:350
  184.9 61.5 %collective-permute-start.20 = (bf16[2,2,128,1024]{3,2,1,0:T(8,128)(2,1)}, bf16[2,2,128,1024]{3,2,1,0:T(8,128)(2,1)S(1)}, u32[]{:S(2)}, u32[]{:S(2)}) collective-permute-start(bf16[2,2,128,1024]{3,2,1,0:T(8,128)(2,1)} %pad_maximum_fusion.3), channel_id=1, source_target_pairs={{0,16},{4,20},{8,24},{12,28},{16,0},{20,4},{24,8},{28,12},{1,17},{... | collective-permute-start | bytes 3145736 | tf_op jit(solution)/shard_map/ppermute | solution.py:350
  186.6 59.8 %collective-permute-start.21 = (bf16[2,2,128,1024]{3,2,1,0:T(8,128)(2,1)}, bf16[2,2,128,1024]{3,2,1,0:T(8,128)(2,1)}, u32[]{:S(2)}, u32[]{:S(2)}) collective-permute-start(bf16[2,2,128,1024]{3,2,1,0:T(8,128)(2,1)} %pad_maximum_fusion.4), channel_id=1, source_target_pairs={{0,8},{4,12},{8,0},{12,4},{16,24},{20,28},{24,16},{28,20},{1,9},{5... | collective-permute-start | bytes 3145736 | tf_op jit(solution)/shard_map/ppermute | solution.py:350
  260.3 43.5 %collective-permute-start.27 = (bf16[4096,512]{1,0:T(8,128)(2,1)}, bf16[4096,512]{1,0:T(8,128)(2,1)}, u32[]{:S(2)}, u32[]{:S(2)}) collective-permute-start(bf16[4096,512]{1,0:T(8,128)(2,1)} %grad_send.4), channel_id=1, source_target_pairs={{0,4},{4,0},{8,12},{12,8},{16,20},{20,16},{24,28},{28,24},{1,5},{5... | collective-permute-start | bytes 12582920 | tf_op jit(solution)/shard_map/ppermute | solution.py:350
  327.9 49.8 %collective-permute-start.28 = (bf16[1024,2048]{1,0:T(8,128)(2,1)}, bf16[1024,2048]{1,0:T(8,128)(2,1)}, u32[]{:S(2)}, u32[]{:S(2)}) collective-permute-start(bf16[1024,2048]{1,0:T(8,128)(2,1)} %grad_send.5), channel_id=1, source_target_pairs={{0,4},{4,0},{8,12},{12,8},{16,20},{20,16},{24,28},{28,24},{1,5},{5... | collective-permute-start | bytes 12582920 | tf_op jit(solution)/shard_map/ppermute | solution.py:350
  333.2 25.5 %collective-permute-start.30 = (bf16[2,2,256,512]{3,2,1,0:T(8,128)(2,1)}, bf16[2,2,256,512]{3,2,1,0:T(8,128)(2,1)}, u32[]{:S(2)}, u32[]{:S(2)}) collective-permute-start(bf16[2,2,256,512]{3,2,1,0:T(8,128)(2,1)} %dynamic-slice_bitcast_fusion.1), channel_id=1, source_target_pairs={{0,16},{4,20},{8,24},{12,28},{16,0},{20,4},{24,8},{28,12},{1,17},{... | collective-permute-start | bytes 3145736 | tf_op jit(solution)/shard_map/ppermute | solution.py:350
  336.4 25.6 %collective-permute-start.29 = (bf16[2,2,256,512]{3,2,0,1:T(8,128)(2,1)}, bf16[2,2,256,512]{3,2,0,1:T(8,128)(2,1)}, u32[]{:S(2)}, u32[]{:S(2)}) collective-permute-start(bf16[2,2,256,512]{3,2,0,1:T(8,128)(2,1)} %bitcast.274), channel_id=1, source_target_pairs={{0,8},{4,12},{8,0},{12,4},{16,24},{20,28},{24,16},{28,20},{1,9},{5... | collective-permute-start | bytes 3145736 | tf_op jit(solution)/shard_map/ppermute | solution.py:350
  377.7 205.2 %reduce-scatter.11.cloned.1.call-start = ((), (), s32[]{:S(2)}) async-start(), calls=%async_computation.7 | async-start | bytes 1310720 | tf_op jit(solution)/shard_map/reduce_scatter | solution.py:470
  441.6 48.2 %collective-permute-start.36 = (bf16[2,64,2048]{2,1,0:T(8,128)(2,1)}, bf16[2,64,2048]{2,1,0:T(8,128)(2,1)}, u32[]{:S(2)}, u32[]{:S(2)}) collective-permute-start(bf16[2,64,2048]{2,1,0:T(8,128)(2,1)} %dynamic-slice_bitcast_fusion.4), channel_id=1, source_target_pairs={{0,16},{4,20},{8,24},{12,28},{16,0},{20,4},{24,8},{28,12},{1,17},{... | collective-permute-start | bytes 1572872 | tf_op jit(solution)/shard_map/ppermute | solution.py:350
  444.8 43.8 %collective-permute-start.37 = (bf16[2,64,2048]{2,1,0:T(8,128)(2,1)}, bf16[2,64,2048]{2,1,0:T(8,128)(2,1)}, u32[]{:S(2)}, u32[]{:S(2)}) collective-permute-start(bf16[2,64,2048]{2,1,0:T(8,128)(2,1)} %dynamic-slice_bitcast_fusion.3), channel_id=1, source_target_pairs={{0,8},{4,12},{8,0},{12,4},{16,24},{20,28},{24,16},{28,20},{1,9},{5... | collective-permute-start | bytes 1572872 | tf_op jit(solution)/shard_map/ppermute | solution.py:350
  488.6 41.6 %collective-permute-start.42 = (bf16[1024,1536]{1,0:T(8,128)(2,1)}, bf16[1024,1536]{1,0:T(8,128)(2,1)}, u32[]{:S(2)}, u32[]{:S(2)}) collective-permute-start(bf16[1024,1536]{1,0:T(8,128)(2,1)} %grad_send.7), channel_id=1, source_target_pairs={{0,4},{4,0},{8,12},{12,8},{16,20},{20,16},{24,28},{28,24},{1,5},{5... | collective-permute-start | bytes 9437192 | tf_op jit(solution)/shard_map/ppermute | solution.py:350
  492.1 156.9 %reduce-scatter.9.cloned.1.call-start = ((), (), s32[]{:S(2)}) async-start(), calls=%async_computation.6 | async-start | bytes 327680 | tf_op jit(solution)/shard_map/reduce_scatter | solution.py:470
  507.5 159.9 %all-gather.21.cloned.1.call-start = ((), (), s32[]{:S(2)}) async-start(), calls=%async_computation.12 | async-start | bytes 2359296 | tf_op jit(solution)/shard_map/all_gather | solution.py:423
  508.1 174.3 %reduce-scatter.7.cloned.1.call-start = ((), (), s32[]{:S(2)}) async-start(), calls=%async_computation.5 | async-start | bytes 983040 | tf_op jit(solution)/shard_map/reduce_scatter | solution.py:470
  543.3 25.6 %collective-permute-start.43 = (bf16[2,2,64,1536]{3,2,0,1:T(8,128)(2,1)S(1)}, bf16[2,2,64,1536]{3,2,0,1:T(8,128)(2,1)S(1)}, u32[]{:S(2)}, u32[]{:S(2)}) collective-permute-start(bf16[2,2,64,1536]{3,2,0,1:T(8,128)(2,1)S(1)} %bitcast.332), channel_id=1, source_target_pairs={{0,8},{4,12},{8,0},{12,4},{16,24},{20,28},{24,16},{28,20},{1,9},{5... | collective-permute-start | bytes 2359304 | tf_op jit(solution)/shard_map/ppermute | solution.py:350
  579.2 126.6 %all-gather.19.cloned.1.call-start = ((), (), s32[]{:S(2)}) async-start(), calls=%async_computation.11 | async-start | bytes 2359296 | tf_op jit(solution)/shard_map/all_gather | solution.py:423
  583.0 134.1 %all-gather.17.cloned.1.call-start = ((), (), s32[]{:S(2)}) async-start(), calls=%async_computation.10 | async-start | bytes 1769472 | tf_op jit(solution)/shard_map/all_gather | solution.py:423
  (82 other events, 1629.0 us)
Sparse Core Ops, SparseCore 0:
  32.8 33.1 all-gather.12
  80.3 26.0 all-gather.14
  377.8 26.4 reduce-scatter.4
  492.2 25.1 reduce-scatter.10
  520.1 18.3 reduce-scatter.8
  540.4 34.4 all-gather.20
  579.3 22.2 reduce-scatter.6
  603.7 27.1 all-gather.18
  682.6 25.2 all-gather.16

commit v3 on v2

v3 whole, which is shorter than its diff:
```python
from functools import partial

import jax
import jax.numpy as jnp
from jax import lax
from jax.experimental import pallas as pl
from jax.experimental.pallas import tpu as pltpu
from jax.sharding import PartitionSpec as P

D = 1024
HEADS = 16
HEAD_DIM = 64
SG = 7
LG = 12
SMALL_LEN = 50
LARGE_LEN = 145
ROWS = 1450
PAD = 1472
GROUP = 8
WINDOW = 176
WINDOWS = 10
PAIRS = 4
ROW_TILE = 368
FAR = -1e30
LOW = jnp.bfloat16
ANYWHERE = pl.BlockSpec(memory_space=pl.ANY)


EPS = 1e-06


def grid_fraction(index):
    scaled = jnp.maximum((2 * index + 1) * SG - LG, 0)
    lower = scaled // (2 * LG)
    return (scaled - 2 * LG * lower).astype(jnp.float32) / (2.0 * LG)


def interp_table(position_source):
    position = jnp.arange(LARGE_LEN, dtype=jnp.int32)
    patch = jnp.maximum(position - 1, 0)
    frac_row = grid_fraction(patch // LG)
    frac_col = grid_fraction(patch % LG)
    weights = jnp.stack(
        [
            (1.0 - frac_row) * (1.0 - frac_col),
            (1.0 - frac_row) * frac_col,
            frac_row * (1.0 - frac_col),
            frac_row * frac_col,
        ],
        axis=1,
    )
    class_row = (jnp.arange(4, dtype=jnp.int32) == 0).astype(jnp.float32)
    weights = jnp.where((position == 0)[:, None], class_row[None, :], weights)
    onehot = (
        position_source[:, :, None] == jnp.arange(SMALL_LEN, dtype=jnp.int32)[None, None, :]
    ).astype(jnp.float32)
    return jnp.sum(weights[:, :, None] * onehot, axis=1)


def layer_norm(values, gain, shift):
    average = jnp.mean(values, axis=-1, keepdims=True)
    centred = values - average
    variance = jnp.mean(centred * centred, axis=-1, keepdims=True)
    inv_std = lax.rsqrt(variance + EPS)
    normed = centred * inv_std
    return (normed * gain + shift, normed, inv_std)


def norm_back(grad_norm, normed, inv_std, gain):
    scaled = grad_norm * gain
    inner = (
        scaled
        - jnp.mean(scaled, axis=-1, keepdims=True)
        - normed * jnp.mean(scaled * normed, axis=-1, keepdims=True)
    )
    return (inv_std * inner, jnp.sum(grad_norm * normed, axis=0), jnp.sum(grad_norm, axis=0))

def dot_nt(left, right):
    return lax.dot_general(
        left, right, (((1,), (1,)), ((), ())), preferred_element_type=jnp.float32
    )


def dot_nn(left, right):
    return lax.dot_general(
        left, right, (((1,), (0,)), ((), ())), preferred_element_type=jnp.float32
    )


def dot_tn(left, right):
    return lax.dot_general(
        left, right, (((0,), (0,)), ((), ())), preferred_element_type=jnp.float32
    )


def cost(flops, moved):
    return pl.CostEstimate(flops=int(flops), transcendentals=0, bytes_accessed=int(moved))


def after(value, *others):
    return lax.optimization_barrier((value, *others))[0]


def sync(*values):
    return lax.optimization_barrier(values)


def window_start(window, step):
    return pl.multiple_of(jnp.minimum(window * step // 16 * 16, PAD - WINDOW), 16)


def image_of(row, length, step):
    image = jnp.where(row >= length, 1, 0) + jnp.where(row >= 2 * length, 1, 0)
    return jnp.where(row < 0, -1, jnp.where(row >= step, 3, image))


def fill_masks(mask_ref, length, step):
    def one(window, carry):
        base = window_start(window, step) - window * step
        shape = (WINDOW, WINDOW)
        rows = image_of(lax.broadcasted_iota(jnp.int32, shape, 0) + base, length, step)
        cols = image_of(lax.broadcasted_iota(jnp.int32, shape, 1) + base, length, step)
        mask_ref[window] = jnp.where(rows == cols, 0.0, FAR).astype(jnp.float32)
        return carry

    lax.fori_loop(0, WINDOWS, one, 0)


def split_heads(value):
    lane = lax.broadcasted_iota(jnp.int32, value.shape, 1)
    zero = jnp.zeros_like(value)
    return jnp.where(lane < HEAD_DIM, value, zero), jnp.where(lane < HEAD_DIM, zero, value)


def slabs(refs, at):
    return [ref[at, i : i + 128] for ref in refs for i in range(0, ref.shape[1], 128)]


def join_heads(even, odd):
    lane = lax.broadcasted_iota(jnp.int32, even.shape, 1)
    return jnp.where(lane < HEAD_DIM, even, odd)


def keep_rows(ref, start, first, value):
    row = lax.broadcasted_iota(jnp.int32, value.shape, 0) + start
    value = jnp.where(row < ROWS, value, 0.0)
    at = pl.ds(start, WINDOW)
    old = ref[at, :].astype(jnp.float32)
    ref[at, :] = jnp.where(row >= first, value, old).astype(ref.dtype)


def forward_kernel(s_ref, q_ref, k_ref, v_ref, *refs):
    o_ref, mask_ref = refs[-2:]
    length, step = s_ref[0], s_ref[1]
    fill_masks(mask_ref, length, step)

    def one(window, carry):
        start = window_start(window, step)
        at = pl.ds(start, WINDOW)
        query = [h for v in slabs([q_ref], at) for h in split_heads(v * LOW(0.125))]
        keys, values = slabs([k_ref], at), slabs([v_ref], at)
        mask = mask_ref[window]
        each = range(2 * PAIRS)
        scores = [dot_nt(query[i], keys[i // 2]) + mask for i in each]
        top = [jnp.max(v, axis=1, keepdims=True) for v in scores]
        raised = [jnp.exp(scores[i] - top[i]) for i in each]
        total = [jnp.sum(v, axis=1, keepdims=True) for v in raised]
        out = [dot_nn(raised[i].astype(LOW), values[i // 2]) for i in each]
        out = [out[i] * (1.0 / total[i]) for i in each]
        for j in range(PAIRS):
            piece = join_heads(out[2 * j], out[2 * j + 1])
            keep_rows(o_ref.at[:, 128 * j : 128 * j + 128], start, window * step, piece)
        return carry

    lax.fori_loop(0, WINDOWS, one, 0)


def backward_kernel(s_ref, *refs):
    (q_refs, k_refs, v_refs, g_refs, out_refs), mask_ref = (
        [refs[2 * i : 2 * i + 2] for i in range(5)],
        refs[10],
    )
    length, step = s_ref[0], s_ref[1]
    fill_masks(mask_ref, length, step)

    def one(window, carry):
        start = window_start(window, step)
        at = pl.ds(start, WINDOW)
        query = [h for v in slabs(q_refs, at) for h in split_heads(v * LOW(0.125))]
        grad = [h for v in slabs(g_refs, at) for h in split_heads(v)]
        keys, values = slabs(k_refs, at), slabs(v_refs, at)
        mask = mask_ref[window]
        each = range(len(query))
        scores = [dot_nt(keys[i // 2], query[i]) + mask for i in each]
        grad_probs = [dot_nt(values[i // 2], grad[i]) for i in each]
        top = [jnp.max(v, axis=0, keepdims=True) for v in scores]
        raised = [jnp.exp(scores[i] - top[i]) for i in each]
        scale = [1.0 / jnp.sum(v, axis=0, keepdims=True) for v in raised]
        probs = [raised[i] * scale[i] for i in each]
        inner = [jnp.sum(grad_probs[i] * probs[i], axis=0, keepdims=True) for i in each]
        grad_scores = [(probs[i] * (grad_probs[i] - inner[i])).astype(LOW) for i in each]
        grad_v = [dot_nn(probs[i].astype(LOW), grad[i]) for i in each]
        grad_k = [dot_nn(grad_scores[i], query[i]) for i in each]
        grad_q = [dot_tn(grad_scores[i], keys[i // 2]) for i in each]
        first = window * step
        for j in range(len(keys)):
            out = out_refs[j // 2]
            cols = slice(j % 2 * 128, j % 2 * 128 + 128)
            both = join_heads(grad_q[2 * j], grad_q[2 * j + 1]) * 0.125
            keep_rows(out.at[0, :, cols], start, first, both)
            keep_rows(out.at[1, :, cols], start, first, grad_k[2 * j] + grad_k[2 * j + 1])
            keep_rows(out.at[2, :, cols], start, first, grad_v[2 * j] + grad_v[2 * j + 1])
        return carry

    lax.fori_loop(0, WINDOWS, one, 0)


def attend_forward(lengths, projected, half, before=None):
    width = 128 * PAIRS
    blocks = D // width

    def part(base):
        return pl.BlockSpec((PAD, width), lambda i, s: (0, half + base))

    return pl.pallas_call(
        forward_kernel,
        out_shape=jax.ShapeDtypeStruct((PAD, D), LOW),
        grid_spec=pltpu.PrefetchScalarGridSpec(
            num_scalar_prefetch=1,
            grid=(1,),
            in_specs=[part(0), part(blocks), part(2 * blocks)] + [ANYWHERE] * (before is not None),
            out_specs=part(0),
            scratch_shapes=[pltpu.VMEM((WINDOWS, WINDOW, WINDOW), jnp.float32)],
        ),
        input_output_aliases={} if before is None else {4: 0},
        cost_estimate=cost(1e10, 1e7),
        name="attend_forward",
    )(lengths, projected, projected, projected, *([] if before is None else [before]))


def attend_backward(numbers, projected, grad):
    width = D // 4

    def part(base, i):
        return pl.BlockSpec((PAD, width), lambda n, s: (0, s[2 + i] + base))

    return pl.pallas_call(
        backward_kernel,
        out_shape=[jax.ShapeDtypeStruct((3, PAD, width), LOW)] * 2,
        grid_spec=pltpu.PrefetchScalarGridSpec(
            num_scalar_prefetch=1,
            grid=(1,),
            in_specs=[part(base, i) for base in (0, 4, 8, 0) for i in (0, 1)],
            out_specs=[pl.BlockSpec((3, PAD, width), lambda n, s: (0, 0, 0))] * 2,
            scratch_shapes=[pltpu.VMEM((WINDOWS, WINDOW, WINDOW), jnp.float32)],
        ),
        cost_estimate=cost(2e10, 1e7),
        name="attend_backward",
    )(numbers, *([projected] * 6), grad, grad)


def hidden_kernel(rows, x_ref, w_ref, b_ref, activ_ref, slope_ref):
    for i in range(PAD // rows):
        at = slice(i * rows, (i + 1) * rows)
        hidden = dot_nn(x_ref[at, :], w_ref[...]) + b_ref[...]
        cdf = 0.5 * lax.erf(hidden * 0.7071067811865476) + 0.5
        density = jnp.exp(-0.5 * hidden * hidden) * 0.3989422804014327
        activ_ref[at, :] = (hidden * cdf).astype(LOW)
        slope_ref[at, :] = (cdf + hidden * density).astype(LOW)


def hidden_layer(second, weight, bias):
    width = bias.shape[0]
    tile = 512
    return pl.pallas_call(
        partial(hidden_kernel, 184),
        out_shape=[jax.ShapeDtypeStruct((PAD, width), LOW)] * 2,
        grid=(width // tile,),
        in_specs=[
            pl.BlockSpec((PAD, D), lambda n: (0, 0)),
            pl.BlockSpec((D, tile), lambda n: (0, n)),
            pl.BlockSpec((1, tile), lambda n: (0, n)),
        ],
        out_specs=[pl.BlockSpec((PAD, tile), lambda n: (0, n))] * 2,
        cost_estimate=cost(2.4e10, 4e7),
        name="hidden_layer",
    )(second, weight, bias.reshape(1, width))


def hidden_back_kernel(shards, steps, rows, s_ref, g_ref, slope_ref, *refs):
    parts, (out_ref, sum_ref, full), (held, sem) = refs[:5], refs[5:8], refs[8:]
    finish = fetch(shards, s_ref, parts, held, full, sem, steps)
    tile = out_ref.shape[1]
    weight = held[pl.ds(pl.multiple_of(pl.program_id(0) * tile, tile), tile), :]
    total = jnp.zeros_like(sum_ref)
    for i in range(PAD // rows):
        at = slice(i * rows, (i + 1) * rows)
        grad = dot_nt(g_ref[at, :], weight) * slope_ref[at, :].astype(jnp.float32)
        grad = grad.astype(LOW)
        out_ref[at, :] = grad
        total = total + column_sum(grad.astype(jnp.float32))
    sum_ref[...] = total
    finish()


def hidden_back(grad, slope, shard, sets):
    width = slope.shape[1]
    tile = 512
    steps = width // tile
    return pl.pallas_call(
        partial(hidden_back_kernel, lax.axis_size("fsdp"), steps, 368),
        out_shape=[
            jax.ShapeDtypeStruct((PAD, width), LOW),
            jax.ShapeDtypeStruct((1, width), jnp.float32),
            fetch_shape(shard),
        ],
        grid_spec=pltpu.PrefetchScalarGridSpec(
            num_scalar_prefetch=1,
            grid=(steps,),
            in_specs=[
                pl.BlockSpec((PAD, D), lambda n, s: (0, 0)),
                pl.BlockSpec((PAD, tile), lambda n, s: (0, n)),
            ]
            + [ANYWHERE] * 5,
            out_specs=[
                pl.BlockSpec((PAD, tile), lambda n, s: (0, n)),
                pl.BlockSpec((1, tile), lambda n, s: (0, n)),
                ANYWHERE,
            ],
            scratch_shapes=fetch_scratch(shard),
        ),
        cost_estimate=cost(1.8e10, 4e7),
        name="hidden_back",
    )(fetch_numbers(), grad, slope, shard, *sets)


def normalise(value):
    average = jnp.mean(value, axis=-1, keepdims=True)
    centred = value - average
    inv_std = lax.rsqrt(jnp.mean(centred * centred, axis=-1, keepdims=True) + EPS)
    return centred * inv_std, inv_std


def back_through_norm(grad, normed, inv_std, gain):
    scaled = grad * gain
    inner = (
        scaled
        - jnp.mean(scaled, axis=-1, keepdims=True)
        - normed * jnp.mean(scaled * normed, axis=-1, keepdims=True)
    )
    return inv_std * inner


def column_sum(value):
    return jnp.sum(value, axis=0, keepdims=True)


def rows_of(width, stacked=0):
    if stacked:
        return pl.BlockSpec((stacked, ROW_TILE, width), lambda i, *s: (0, i, 0))
    return pl.BlockSpec((ROW_TILE, width), lambda i, *s: (i, 0))


def whole(*shape):
    return pl.BlockSpec(shape, lambda i, *s: (0,) * len(shape))


def project_kernel(shards, steps, s_ref, a_ref, b_ref, *refs):
    parts, (out_ref, full), (held, sem) = refs[:5], refs[5:7], refs[7:]
    finish = fetch(shards, s_ref, parts, held, full, sem, steps)
    out_ref[...] = (dot_nn(a_ref[...], held[...]) + b_ref[...]).astype(LOW)
    finish()


def project(first, bias, shard, sets):
    width = shard.shape[1]
    steps = PAD // ROW_TILE
    return pl.pallas_call(
        partial(project_kernel, lax.axis_size("fsdp"), steps),
        out_shape=[jax.ShapeDtypeStruct((PAD, width), LOW), fetch_shape(shard)],
        grid_spec=pltpu.PrefetchScalarGridSpec(
            num_scalar_prefetch=1,
            grid=(steps,),
            in_specs=[rows_of(D), whole(1, width)] + [ANYWHERE] * 5,
            out_specs=[rows_of(width), ANYWHERE],
            scratch_shapes=fetch_scratch(shard),
        ),
        cost_estimate=cost(2 * PAD * D * width, 2e7),
        name="project",
    )(fetch_numbers(), first, bias.reshape(1, width), shard, *sets)


def branch_kernel(shards, steps, s_ref, a_ref, stream_ref, vec_ref, *refs):
    parts, (mid_ref, second_ref, full), (held, sem) = refs[:5], refs[5:8], refs[8:]
    finish = fetch(shards, s_ref, parts, held, full, sem, steps)
    weight = held[:, held.shape[1] - D :]
    mid = stream_ref[...] + dot_nn(a_ref[...], weight) + vec_ref[0:1, :]
    mid_ref[...] = mid
    normed, _ = normalise(mid)
    second_ref[...] = (normed * vec_ref[1:2, :] + vec_ref[2:3, :]).astype(LOW)
    finish()


def branch(attended, stream, vectors, shard, sets):
    steps = PAD // ROW_TILE
    return pl.pallas_call(
        partial(branch_kernel, lax.axis_size("fsdp"), steps),
        out_shape=[
            jax.ShapeDtypeStruct((PAD, D), jnp.float32),
            jax.ShapeDtypeStruct((PAD, D), LOW),
            fetch_shape(shard),
        ],
        grid_spec=pltpu.PrefetchScalarGridSpec(
            num_scalar_prefetch=1,
            grid=(steps,),
            in_specs=[rows_of(D), rows_of(D), whole(3, D)] + [ANYWHERE] * 5,
            out_specs=[rows_of(D), rows_of(D), ANYWHERE],
            scratch_shapes=fetch_scratch(shard),
        ),
        cost_estimate=cost(2 * PAD * D * D, 3e7),
        name="branch",
    )(fetch_numbers(), attended, stream, vectors, shard, *sets)


def return_kernel(a_ref, w_ref, mid_ref, vec_ref, out_ref):
    value = mid_ref[...] + dot_nn(a_ref[...], w_ref[...]) + vec_ref[...]
    out_ref[...] = value.astype(LOW)


def return_layer(activ, weight, mid, bias):
    width = weight.shape[0]
    return pl.pallas_call(
        return_kernel,
        out_shape=jax.ShapeDtypeStruct((ROWS, D), LOW),
        grid=(PAD // ROW_TILE,),
        in_specs=[rows_of(width), whole(width, D), rows_of(D), whole(1, D)],
        out_specs=rows_of(D),
        cost_estimate=cost(2 * PAD * D * width, 3e7),
        name="return_layer",
    )(activ, weight, mid, bias.reshape(1, D))


def second_back_kernel(
    h_ref, w_ref, o_ref, mid_ref, g_ref, gain_ref, out_ref, low_ref, att_ref, sums_ref
):
    @pl.when(pl.program_id(0) == 0)
    def _():
        sums_ref[...] = jnp.zeros_like(sums_ref)

    grad = dot_nt(h_ref[...], w_ref[...])
    normed, inv_std = normalise(mid_ref[...])
    out = g_ref[...].astype(jnp.float32)
    sums_ref[3:4, :] += column_sum(out)
    out = out + back_through_norm(grad, normed, inv_std, gain_ref[...])
    out_ref[...] = out
    low = out.astype(LOW)
    low_ref[...] = low
    att_ref[...] = dot_nt(low, o_ref[...]).astype(LOW)
    sums_ref[0:1, :] += column_sum(grad * normed)
    sums_ref[1:2, :] += column_sum(grad)
    sums_ref[2:3, :] += column_sum(low.astype(jnp.float32))


def second_back(grad_hidden, joined, mid, grad, gain):
    width = grad_hidden.shape[1]
    return pl.pallas_call(
        second_back_kernel,
        out_shape=[
            jax.ShapeDtypeStruct((PAD, D), jnp.float32),
            jax.ShapeDtypeStruct((PAD, D), LOW),
            jax.ShapeDtypeStruct((PAD, D), LOW),
            jax.ShapeDtypeStruct((8, D), jnp.float32),
        ],
        grid=(PAD // ROW_TILE,),
        in_specs=[
            rows_of(width),
            whole(D, width),
            pl.BlockSpec((D, D), lambda i: (0, width // D)),
            rows_of(D),
            rows_of(D),
            whole(1, D),
        ],
        out_specs=[rows_of(D), rows_of(D), rows_of(D), whole(8, D)],
        cost_estimate=cost(2 * PAD * D * width, 4e7),
        name="second_back",
    )(grad_hidden, joined, joined, mid, grad, gain.reshape(1, D))


def first_back_kernel(s_ref, *refs):
    heads, w_refs, (stream_ref, mid_ref, spread_ref, gain_ref) = refs[:4], refs[4:16], refs[16:20]
    out_ref, table_ref, sums_ref, heads_ref = refs[20:]

    @pl.when(pl.program_id(0) == 0)
    def _():
        sums_ref[...] = jnp.zeros_like(sums_ref)
        table_ref[...] = jnp.zeros_like(table_ref)
        heads_ref[...] = jnp.zeros_like(heads_ref)

    grad = 0.0
    for j, ref in enumerate(heads):
        for t in range(3):
            grad = grad + dot_nt(ref[t], w_refs[3 * j + t][...])
    normed, inv_std = normalise(stream_ref[...])
    out = mid_ref[...] + back_through_norm(grad, normed, inv_std, gain_ref[...])
    out_ref[...] = out.astype(LOW)
    sums_ref[0:1, :] += column_sum(grad * normed)
    sums_ref[1:2, :] += column_sum(grad)
    table_ref[...] += lax.dot_general(
        spread_ref[...],
        out,
        (((0,), (0,)), ((), ())),
        precision=lax.Precision.HIGHEST,
        preferred_element_type=jnp.float32,
    )
    for j, ref in enumerate(heads):
        for i, t in enumerate((0, 2)):
            at = 2 * j + i
            heads_ref[at : at + 1, :] += column_sum(ref[t].astype(jnp.float32))


def first_back(quarters, heads, joined, stream, grad_mid, spread, gain):
    width = D // 4
    w_specs = [
        pl.BlockSpec((D, width), lambda i, s, j=j, t=t: (0, 4 * t + s[j]))
        for j in range(4)
        for t in range(3)
    ]
    slots = spread.shape[1]
    return pl.pallas_call(
        first_back_kernel,
        out_shape=[
            jax.ShapeDtypeStruct((ROWS, D), LOW),
            jax.ShapeDtypeStruct((slots, D), jnp.float32),
            jax.ShapeDtypeStruct((8, D), jnp.float32),
            jax.ShapeDtypeStruct((8, width), jnp.float32),
        ],
        grid_spec=pltpu.PrefetchScalarGridSpec(
            num_scalar_prefetch=1,
            grid=(PAD // ROW_TILE,),
            in_specs=[rows_of(width, 3)] * 4
            + w_specs
            + [rows_of(D), rows_of(D), rows_of(slots), whole(1, D)],
            out_specs=[rows_of(D), whole(slots, D), whole(8, D), whole(8, width)],
        ),
        cost_estimate=cost(2 * PAD * D * 3 * D, 4e7),
        name="first_back",
    )(quarters, *heads, *([joined] * 12), stream, grad_mid, spread, gain.reshape(1, D))


def widen_kernel(moves, count, *refs):
    for source, at, target, to, width in moves:
        for core in (0, 1):
            value = refs[source][0, core, :, at : at + width].astype(jnp.float32)
            refs[count + target][:, to[core] : to[core] + width] = value


def widen(sources, widths, moves):
    rows = sources[0].shape[1]
    return pl.pallas_call(
        partial(widen_kernel, moves, len(sources)),
        out_shape=[jax.ShapeDtypeStruct((4 * rows, w), jnp.float32) for w in widths],
        grid=(4,),
        in_specs=[
            pl.BlockSpec((1, 2, rows, v.shape[2]), lambda i: (i, 0, 0, 0)) for v in sources
        ],
        out_specs=[pl.BlockSpec((rows, w), lambda i: (i, 0)) for w in widths],
        cost_estimate=cost(1, 6e6),
        name="widen",
    )(*[v.reshape(4, 2, rows, v.shape[2]) for v in sources])


def grad_value(f_ref, a_ref, b_ref):
    if len(b_ref.shape) == 2:
        return dot_tn(a_ref[...], b_ref[...]) * f_ref[0]
    return jnp.concatenate([dot_tn(a_ref[...], b_ref[i]) for i in range(3)], axis=1) * f_ref[0]


def grad_send_kernel(c_ref, f_ref, a_ref, b_ref, out_ref):
    out_ref[...] = grad_value(f_ref, a_ref, b_ref).astype(LOW)


def grad_keep_kernel(planes, c_ref, f_ref, a_ref, b_ref, got_ref, keep_ref, send_ref):
    value = (grad_value(f_ref, a_ref, b_ref) + got_ref[...].astype(jnp.float32)).astype(LOW)
    core, place = c_ref[0], c_ref[1]
    rows = value.shape[0] // planes // 4
    for quarter in range(4):
        bits = place ^ quarter
        role = jnp.where(core == 0, bits, (bits >> 1) | ((bits & 1) << 1))
        for ref, near in ((keep_ref, 0), (send_ref, 1)):

            @pl.when(role % 2 == near)
            def _(ref=ref, quarter=quarter, role=role):
                for plane in range(planes):
                    at = (plane * 4 + quarter) * rows
                    ref[role // 2, plane] = value[at : at + rows]


def grad_half(numbers, factor, left, right, got=None, tile_m=1024, tile_n=512):
    rows = left.shape[1]
    shards = lax.axis_size("fsdp")
    stacked = right.ndim == 3
    cols = 3 * right.shape[2] if stacked else right.shape[1] // 2
    tile_n = cols if stacked else tile_n
    steps = cols // tile_n
    in_specs = [
        pl.BlockSpec(memory_space=pltpu.SMEM),
        pl.BlockSpec((PAD, tile_m), lambda m, n, c: (0, m)),
    ]
    if stacked:
        in_specs.append(pl.BlockSpec((3, PAD, cols // 3), lambda m, n, c: (0, 0, 0)))
    else:
        in_specs.append(pl.BlockSpec((PAD, tile_n), lambda m, n, c: (0, n + c[0] * steps)))
    flat_spec = pl.BlockSpec((tile_m, tile_n), lambda m, n, c: (m, n))
    operands = [numbers, factor, left, right]
    if got is None:
        kernel, name = grad_send_kernel, "grad_send"
        out_shape, out_specs = jax.ShapeDtypeStruct((rows, cols), LOW), flat_spec
    else:
        planes = tile_m * shards // rows
        part = rows // shards // 4
        kernel, name = partial(grad_keep_kernel, planes), "grad_keep"
        in_specs.append(flat_spec)
        operands.append(got)
        out_shape = [jax.ShapeDtypeStruct((2, shards, part, cols), LOW)] * 2
        out_specs = [pl.BlockSpec((2, planes, part, tile_n), lambda m, n, c: (0, m, 0, n))] * 2
    return pl.pallas_call(
        kernel,
        out_shape=out_shape,
        grid_spec=pltpu.PrefetchScalarGridSpec(
            num_scalar_prefetch=1,
            grid=(rows // tile_m, steps),
            in_specs=in_specs,
            out_specs=out_specs,
        ),
        cost_estimate=cost(2 * PAD * rows * cols, 1e7),
        name=name,
    )(*operands)


def swap(value, even, odd):
    size = lax.axis_size("dp")
    return lax.ppermute(value, "dp", [(i, i ^ (odd if i % 2 else even)) for i in range(size)])


def swap_core(value):
    return swap(value, 1, 1)


def swap_first(value):
    return swap(value, 2, 4)


def swap_second(value):
    return swap(value, 4, 2)


def own_piece(shard):
    part = shard.shape[0] // GROUP
    place = lax.axis_index("dp") % GROUP
    return lax.dynamic_slice_in_dim(shard, place * part, part, 0)


def gather_z(shard):
    shards = lax.axis_size("fsdp")
    piece = own_piece(shard)
    return jnp.stack(
        [
            lax.ppermute(piece, "fsdp", [((i + k) % shards, i) for i in range(shards)])
            for k in range(1, shards)
        ]
    )


def gather_z_native(shard):
    every = lax.all_gather(own_piece(shard), "fsdp", axis=0, tiled=False)
    shards = every.shape[0]
    twice = jnp.concatenate([every, every[:-1]], axis=0)
    return lax.dynamic_slice_in_dim(twice, lax.axis_index("fsdp") + 1, shards - 1, 0)


def gather_first(own):
    return own, swap_first(own)


def gather_second(own, got):
    both = jnp.stack([own, got])
    return both, swap_second(both)


def gather_core(both, far):
    return both, far, swap_core(both), swap_core(far)


def fetch_copies(shards, s_ref, refs, held, sem):
    own, sets = refs[0], refs[1:]
    place, row = s_ref[0], s_ref[1]
    rows = own.shape[0]
    part = rows // GROUP
    copies = [
        pltpu.make_async_copy(
            own, held.at[pl.ds(pl.multiple_of(row * rows, rows), rows), :], sem.at[0]
        )
    ]
    for flip in range(2):
        base = place ^ flip
        first = jnp.where(base % 2 == 0, 2, 4)
        for source, bits in (
            (sets[2 * flip].at[0], 0),
            (sets[2 * flip].at[1], first),
            (sets[2 * flip + 1].at[0], 6 - first),
            (sets[2 * flip + 1].at[1], 6),
        ):
            for k in range(1, shards):
                at = lax.rem(row + k, shards) * rows + (base ^ bits) * part
                target = held.at[pl.ds(pl.multiple_of(at, part), part), :]
                copies.append(pltpu.make_async_copy(source.at[k - 1], target, sem.at[len(copies)]))
    return copies


def fetch(shards, s_ref, refs, held, full, sem, steps):
    def keep():
        return pltpu.make_async_copy(held, full, sem.at[0])

    @pl.when(pl.program_id(0) == 0)
    def _():
        copies = fetch_copies(shards, s_ref, refs, held, sem)
        for copy in copies:
            copy.start()
        for copy in copies:
            copy.wait()
        keep().start()

    def finish():
        @pl.when(pl.program_id(0) == steps - 1)
        def _():
            keep().wait()

    return finish


def fetch_numbers():
    place = lax.axis_index("dp") % GROUP
    return jnp.stack([place, lax.axis_index("fsdp")]).astype(jnp.int32)


def fetch_scratch(shard):
    shards = lax.axis_size("fsdp")
    return [
        pltpu.VMEM((shards * shard.shape[0], shard.shape[1]), shard.dtype),
        pltpu.SemaphoreType.DMA((1 + 8 * (shards - 1),)),
    ]


def fetch_shape(shard):
    shards = lax.axis_size("fsdp")
    return jax.ShapeDtypeStruct((shards * shard.shape[0], shard.shape[1]), shard.dtype)


def plane_gather(value, axis):
    size = lax.axis_size("dp")
    groups = None
    if size > GROUP:
        groups = [[g * GROUP + i for i in range(GROUP)] for g in range(size // GROUP)]
    return lax.all_gather(value, "dp", axis=axis, tiled=False, axis_index_groups=groups)


def rest_sum(value):
    size = lax.axis_size("dp")
    if size == GROUP:
        return value
    groups = [[g * GROUP + i for g in range(size // GROUP)] for i in range(GROUP)]
    return lax.psum(value, "dp", axis_index_groups=groups)


def add_low(left, right):
    return (left.astype(jnp.float32) + right.astype(jnp.float32)).astype(LOW)


def sum_first(got, *keeps):
    keep = jnp.concatenate(keeps, axis=-1)
    return add_low(keep[0], got[0]), swap_second(add_low(keep[1], got[1]))


def sum_z(kept, got):
    both = add_low(kept, got)
    shards, part, cols = both.shape
    piece = lax.psum_scatter(
        both.reshape(shards * part, cols), "fsdp", scatter_dimension=0, tiled=True
    )
    return rest_sum(piece)


def sum_z_direct(value):
    shards = lax.axis_size("fsdp")
    me = lax.axis_index("fsdp")
    total = lax.dynamic_index_in_dim(value, me, 0, keepdims=False).astype(jnp.float32)
    for step in range(1, shards):
        send = lax.dynamic_index_in_dim(value, (me + step) % shards, 0, keepdims=False)
        got = lax.ppermute(send, "fsdp", [(i, (i + step) % shards) for i in range(shards)])
        total = total + got.astype(jnp.float32)
    return total


def small_sum(value):
    every = lax.all_gather(value.astype(LOW), "dp", axis=0, tiled=False)
    return jnp.sum(every.astype(jnp.float32), axis=0)


def small_gather(value):
    shards = lax.axis_size("fsdp")
    parts = [value] + [
        lax.ppermute(value, "fsdp", [(i, (i + k) % shards) for i in range(shards)])
        for k in range(1, shards)
    ]
    parts = parts[::-1]
    twice = jnp.stack(parts + parts)
    return lax.dynamic_slice_in_dim(twice, shards - 1 - lax.axis_index("fsdp"), shards, 0)


def per_device(
    tokens,
    output_grad,
    group_member,
    image_counts,
    position_source,
    position_table,
    first_gain,
    first_shift,
    input_proj,
    query_bias,
    value_bias,
    output_proj,
    output_bias,
    second_gain,
    second_shift,
    hidden_weight,
    hidden_bias,
    return_weight,
    return_bias,
):
    dp_size = lax.axis_size("dp")
    fsdp_size = lax.axis_size("fsdp")
    core = (lax.axis_index("dp") & 1).astype(jnp.int32)
    quarter = ((lax.axis_index("dp") % GROUP) >> 1).astype(jnp.int32)
    mine, other = jnp.stack([core, quarter]), jnp.stack([1 - core, quarter])
    small_parts = (
        first_gain,
        first_shift,
        query_bias,
        value_bias,
        output_bias,
        second_gain,
        second_shift,
        return_bias,
        hidden_bias,
        position_table.reshape(-1),
    )
    sizes = [v.shape[0] for v in small_parts]
    wide = first_gain.shape[0]
    joined = jnp.concatenate([v.reshape(-1, wide) for v in small_parts], axis=0)
    pad = -joined.shape[0] % 16 * wide
    joined = jnp.pad(joined, ((0, pad // wide), (0, 0)))
    joint_z = gather_z(input_proj)
    smalls = small_gather(joined).reshape(fsdp_size, -1)
    smalls = smalls.astype(jnp.float32)
    offsets = [sum(sizes[:i]) for i in range(len(sizes))]
    vectors = [smalls[:, o : o + n] for o, n in zip(offsets, sizes)]
    (
        gain_one,
        shift_one,
        query_add,
        value_add,
        output_add,
        gain_two,
        shift_two,
        return_add,
        hidden_add,
    ) = [v.reshape(-1) for v in vectors[:9]]
    table_full = (
        vectors[9].reshape(fsdp_size, SMALL_LEN, -1).transpose(1, 0, 2).reshape(SMALL_LEN, D)
    )
    member = group_member[0]
    is_large = member == 1
    length = jnp.where(is_large, LARGE_LEN, SMALL_LEN)
    step = jnp.where(is_large, LARGE_LEN, 3 * SMALL_LEN)
    group_high = dp_size * 7 // 16
    group_low = dp_size - group_high
    counts = image_counts.astype(jnp.float32)
    share = jnp.where(is_large, counts[1], counts[0]) / (counts[0] + counts[1])
    images = jnp.where(
        is_large,
        group_high * fsdp_size * (ROWS // LARGE_LEN),
        group_low * fsdp_size * (ROWS // SMALL_LEN),
    ).astype(jnp.float32)
    factor = share / images
    scale = factor.reshape(1)

    row_index = jnp.arange(PAD, dtype=jnp.int32)
    place = jnp.where(row_index < ROWS, row_index % length, -1)
    inter = interp_table(position_source)
    identity = (
        jnp.arange(LARGE_LEN, dtype=jnp.int32)[:, None]
        == jnp.arange(SMALL_LEN, dtype=jnp.int32)[None, :]
    ).astype(jnp.float32)
    mixing = jnp.where(is_large, inter, identity)
    picker = (place[:, None] == jnp.arange(LARGE_LEN, dtype=jnp.int32)[None, :]).astype(jnp.float32)
    spread = jnp.dot(picker, mixing, precision=lax.Precision.HIGHEST)
    position = jnp.dot(spread, table_full, precision=lax.Precision.HIGHEST)
    grad_pad = jnp.pad(output_grad, ((0, PAD - ROWS), (0, 0)))
    stream = jnp.pad(tokens, ((0, PAD - ROWS), (0, 0))).astype(jnp.float32) + position
    first_low = layer_norm(stream, gain_one, shift_one)[0].astype(LOW)

    lengths = jnp.stack([length, step])

    joint_one = gather_first(joint_z)
    hidden_shard = jnp.concatenate([hidden_weight, output_proj], axis=1)
    hidden_z = gather_z_native(after(hidden_shard, joint_z))
    joint_two = gather_second(*joint_one)
    joint_sets = gather_core(*joint_two)
    return_z = gather_z_native(after(return_weight, hidden_z))
    hidden_z = after(hidden_z, joint_two[1])
    first_low, grad_pad, hidden_z, *joint_sets = sync(first_low, grad_pad, hidden_z, *joint_sets)
    hidden_one = gather_first(hidden_z)
    joint_add = jnp.concatenate([query_add, jnp.zeros_like(query_add), value_add])
    projected, joint_full = project(first_low, joint_add, input_proj, joint_sets)
    projected, *hidden_one = sync(projected, *hidden_one)
    hidden_two = gather_second(*hidden_one)
    attended = attend_forward(lengths, after(projected, hidden_two[0]), 0)
    attended, return_z, *hidden_two = sync(attended, return_z, *hidden_two)
    hidden_sets = gather_core(*hidden_two)
    return_one = gather_first(return_z)
    attended = attend_forward(lengths, projected, 1, after(attended, hidden_two[1], return_one[0]))
    attended, *rest = sync(attended, *hidden_sets, *return_one)
    hidden_sets, return_one = rest[:4], rest[4:]
    return_two = gather_second(*return_one)
    mid, second, hidden_full = branch(
        after(attended, return_two[0]),
        stream,
        jnp.stack([output_add, gain_two, shift_two]),
        hidden_shard,
        hidden_sets,
    )
    activ, slope = hidden_layer(second, hidden_full, hidden_add)
    activ, slope, *return_two = sync(activ, slope, *return_two)
    return_sets = gather_core(*return_two)
    return_send = grad_half(other, scale, activ, grad_pad)
    return_send, *return_sets = sync(return_send, *return_sets)
    return_got = swap_core(return_send)
    grad_hidden, grad_hidden_add, return_full = hidden_back(
        after(grad_pad, return_send), slope, return_weight, return_sets
    )
    grad_hidden, return_got = sync(grad_hidden, return_got)
    return_keep, return_out = grad_half(mine, scale, activ, grad_pad, return_got)
    return_in = swap_first(return_out)
    hidden_send = grad_half(other, scale, after(second, return_out), grad_hidden)
    hidden_got = swap_core(hidden_send)
    grad_mid, grad_branch, grad_att, sums_two = second_back(
        after(grad_hidden, hidden_send), hidden_full, mid, grad_pad, gain_two
    )
    grad_branch, hidden_got, return_in = sync(grad_branch, hidden_got, return_in)
    return_kept, return_in = sum_first(return_in, return_keep)
    hidden_keep, hidden_out = grad_half(
        mine, scale, after(second, return_kept), grad_hidden, hidden_got
    )
    hidden_out, grad_branch, return_in = sync(hidden_out, grad_branch, return_in)
    return_piece = sum_z(return_kept, return_in)
    hidden_in = swap_first(hidden_out)
    output_send = grad_half(other, scale, attended, grad_branch)
    output_got = swap_core(output_send)
    quarters = jnp.stack([2 * core, 2 - 2 * core, 2 * core + 1, 3 - 2 * core])
    mine_one, other_one = attend_backward(
        jnp.concatenate([lengths, quarters[:2]]), projected, after(grad_att, output_send)
    )
    mine_one, other_one, output_got, hidden_in = sync(mine_one, other_one, output_got, hidden_in)
    hidden_kept, hidden_in = sum_first(hidden_in, hidden_keep)
    joint_send = grad_half(other, scale, after(first_low, hidden_kept), other_one, tile_m=512)
    joint_send, return_piece = sync(joint_send, return_piece)
    joint_got = swap_core(joint_send)
    return_every = plane_gather(return_piece, axis=0)
    output_keep, output_out = grad_half(
        mine, scale, attended, after(grad_branch, joint_send), output_got
    )
    output_out, joint_got = sync(output_out, joint_got)
    joint_keep, joint_out = grad_half(mine, scale, first_low, mine_one, joint_got, tile_m=512)
    joint_out, hidden_in = sync(joint_out, hidden_in)
    hidden_piece = sum_z(hidden_kept, hidden_in)
    joint_out = jnp.concatenate([joint_out, output_out], axis=-1)
    joint_in = swap_first(joint_out)
    mine_two, other_two = attend_backward(
        jnp.concatenate([lengths, quarters[2:]]), projected, after(grad_att, joint_out)
    )
    mine_two, other_two, joint_in, return_every = sync(mine_two, other_two, joint_in, return_every)
    joint_kept, joint_in = sum_first(joint_in, joint_keep, output_keep)
    last_send = grad_half(other, scale, after(first_low, joint_kept), other_two, tile_m=512)
    last_got = swap_core(last_send)
    last_got, joint_in = sync(last_got, joint_in)
    joint_piece = sum_z(joint_kept, joint_in)
    last_keep, last_out = grad_half(mine, scale, first_low, mine_two, last_got, tile_m=512)
    last_in = swap_first(last_out)
    heads = sync(mine_one, other_one, mine_two, other_two, last_out)[:4]
    tokens_grad, grad_table, sums_one, head_sums = first_back(
        quarters, heads, joint_full, stream, grad_mid, spread, gain_one
    )
    tokens_grad, grad_table, sums_one, head_sums, last_in = sync(
        tokens_grad, grad_table, sums_one, head_sums, last_in
    )
    last_kept, last_in = sum_first(last_in, last_keep)
    hidden_every = plane_gather(hidden_piece, axis=0)
    joint_every = plane_gather(joint_piece, axis=0)

    head_sums = head_sums.reshape(2, 2, 2, -1).transpose(2, 1, 0, 3)
    head_sums = jnp.where(core == 0, head_sums, head_sums[:, ::-1])
    table_rows = grad_table.reshape(SMALL_LEN, fsdp_size, -1).transpose(1, 0, 2)
    small_grads = (
        sums_one[0],
        sums_one[1],
        head_sums[0],
        head_sums[1],
        sums_two[2],
        sums_two[0],
        sums_two[1],
        sums_two[3],
        grad_hidden_add,
        table_rows,
    )
    packed = jnp.concatenate([v.reshape(fsdp_size, -1) for v in small_grads], axis=1) * factor
    packed = jnp.pad(packed, ((0, 0), (0, pad))).reshape(fsdp_size, -1, 128).astype(LOW)
    packed, last_in = sync(packed, last_in)
    last_both = add_low(last_kept, last_in)
    last_piece = sum_z_direct(last_both).astype(LOW)
    small_piece = sum_z_direct(packed)
    block_out = return_layer(after(activ, packed, last_both), return_full, mid, return_add)
    block_out, last_piece, small_piece = sync(block_out, last_piece, small_piece)
    summed = small_sum(small_piece).reshape(-1)
    small_outs = [summed[o : o + n] for o, n in zip(offsets, sizes)]
    last_every = plane_gather(last_piece, axis=0)
    half, part = D // 2, D // 4
    (return_w_out,) = widen([return_every], [D], [(0, 0, 0, (0, half), half)])
    (hidden_w_out,) = widen([hidden_every], [4 * D], [(0, 0, 0, (0, 2 * D), 2 * D)])
    moves = [
        (i, t * part, 0, (t * D + i * part, t * D + half + i * part), part)
        for i in range(2)
        for t in range(3)
    ]
    joint_out, outproj_out = widen(
        [joint_every, last_every], [3 * D, D], moves + [(0, 3 * part, 1, (0, half), half)]
    )
    return (
        block_out,
        tokens_grad,
        small_outs[9].reshape(SMALL_LEN, -1),
        small_outs[0],
        small_outs[1],
        joint_out,
        small_outs[2],
        small_outs[3],
        outproj_out,
        small_outs[4],
        small_outs[5],
        small_outs[6],
        hidden_w_out,
        small_outs[8],
        return_w_out,
        small_outs[7],
    )


def solution(mesh):
    in_specs = (
        P(("dp", "fsdp"), None),
        P(("dp", "fsdp"), None),
        P("dp"),
        P(),
        P(),
        P(None, "fsdp"),
        P("fsdp"),
        P("fsdp"),
        P("fsdp", None),
        P("fsdp"),
        P("fsdp"),
        P("fsdp", None),
        P("fsdp"),
        P("fsdp"),
        P("fsdp"),
        P("fsdp", None),
        P("fsdp"),
        P("fsdp", None),
        P("fsdp"),
    )
    out_specs = (
        P(("dp", "fsdp"), None),
        P(("dp", "fsdp"), None),
        P(None, "fsdp"),
        P("fsdp"),
        P("fsdp"),
        P("fsdp", None),
        P("fsdp"),
        P("fsdp"),
        P("fsdp", None),
        P("fsdp"),
        P("fsdp"),
        P("fsdp"),
        P("fsdp", None),
        P("fsdp"),
        P("fsdp", None),
        P("fsdp"),
    )
    return jax.shard_map(
        per_device, mesh=mesh, in_specs=in_specs, out_specs=out_specs, check_vma=False
    )
```

time: 753 us -> 547 us (0.73)
  matrix products: 124 us -> 6.01 us
  Pallas kernels: 209 us -> 323 us
  waiting for transfers between devices: 123 us -> 58.9 us
  local copies, waits for them, and re-layouts: 101 us -> 45.1 us
  other arithmetic: 79.1 us -> 27.5 us
  blocking collectives: 45.1 us -> 20.4 us
    dot_general x12 -> x0, matrix products: 116 us -> none  [the longest x8 71.4 us: dot_nt(): lax.dot_general(left, right, (((1,), (1,)), ((), ())), preferred_element_...]
    pallas_call x14 -> x21, Pallas kernels: 162 us -> 272 us  [the longest x10 88.4 us: grad_half(): pl.pallas_call(kernel, out_shape=out_shape, grid_spec=pltpu.PrefetchScala...]
    ppermute x53 -> x37, waiting for transfers between devices: 123 us -> 39.9 us  [the longest x25 31.7 us: swap(): lax.ppermute(value, 'dp', [(i, i ^ (odd if i % 2 else even)) for i in ran...]
    all_gather x2 -> x1, blocking collectives: 35.8 us -> 9.58 us  [small_sum(): every = lax.all_gather(value.astype(LOW), 'dp', axis=0, tiled=False)]
    convert_element_type x6 -> x0, local copies, waits for them, and re-layouts: 25.5 us -> none  [sum_last(): return every.reshape(4 * part, 2 * cols).astype(jnp.float32)]
    slice x9 -> x5, local copies, waits for them, and re-layouts: 27 us -> 3.55 us  [the longest x2 2.64 us: gather_z_native(): twice = jnp.concatenate([every, every[:-1]], axis=0)]
    unnamed x138 -> x107, local copies, waits for them, and re-layouts: 29.7 us -> 15.2 us
    all_gather x2, waiting for transfers between devices: 0.01 us -> 14.2 us  [gather_z_native(): every = lax.all_gather(own_piece(shard), 'fsdp', axis=0, tiled=False)]
  transfers between devices with their start and end apart: 62 -> 45, of which waited for: 19 -> 12; matrix products, arithmetic and copies ran while one was open for 37% -> 12% of each run, Pallas kernels for 23% -> 53%
where the time goes in v3:
time: 547 us; the launch traced here: 539 us
  Pallas kernels  323 us (59%)
  waiting for transfers between devices  58.9 us (11%)
  local copies, waits for them, and re-layouts  45.1 us (8%)
  starting transfers between devices  38.8 us (7%)
  other arithmetic  27.5 us (5%)
  blocking collectives  20.4 us (4%)
  between operations  18.8 us (3%)
  matrix products  6.01 us (1%)
    pallas_call x10, Pallas kernels, grad_half(): pl.pallas_call(kernel, out_shape=out_shape, grid_spec=pltpu.PrefetchScala...  88.4 us
    pallas_call x2, Pallas kernels, attend_backward(): pl.pallas_call(backward_kernel, out_shape=[jax.ShapeDtypeStruct((3, PAD,...  44.3 us
    ppermute x25, waiting for transfers between devices, swap(): lax.ppermute(value, 'dp', [(i, i ^ (odd if i % 2 else even)) for i in ran...  31.7 us
    pallas_call x1, Pallas kernels, hidden_layer(): pl.pallas_call(partial(hidden_kernel, 184), out_shape=[jax.ShapeDtypeStru...  27.3 us
    pallas_call x1, Pallas kernels, second_back(): pl.pallas_call(second_back_kernel, out_shape=[jax.ShapeDtypeStruct((PAD,...  26.1 us
    pallas_call x2, Pallas kernels, attend_forward(): pl.pallas_call(forward_kernel, out_shape=jax.ShapeDtypeStruct((PAD, D), L...  24.3 us
    pallas_call x1, Pallas kernels, first_back(): pl.pallas_call(first_back_kernel, out_shape=[jax.ShapeDtypeStruct((ROWS,...  24.1 us
    pallas_call x1, Pallas kernels, hidden_back(): pl.pallas_call(partial(hidden_back_kernel, lax.axis_size('fsdp'), steps,...  24 us
  transfers between devices with their start and end apart: 45, of which 12 were waited for; matrix products, arithmetic and copies ran while one was open for 12% of the time, Pallas kernels for 53%

profile of v3, /device:TPU:0, one launch (start us, length us, event | category | flops | bytes accessed | tf_op | source)
XLA Modules:
  0.0 538.7 jit_solution(12710955345201714541)
XLA Ops:
  8.9 5.0 collective-permute-start.3
  35.5 5.1 collective-permute-done.2
  57.4 5.1 fusion.35
  63.4 8.8 %collective-permute-done.7.refs_2_ = bf16[2,3,32,3072]{3,2,1,0:T(8,128)(2,1)} collective-permute-done((bf16[2,3,32,3072]{3,2,1,0:T(8,128)(2,1)S(1)}, bf16[2,3,32,3072]{3,2,1,0:T(8,128)(2,1)}, u32[]{:S(2)}, u32[]{:S(2)}) %collective-permute-start.7) | collective-permute-done | bytes 1179680 | tf_op jit(solution)/shard_map/ppermute | solution.py:642
  74.6 9.4 %all-gather.13.cloned.1.call-done = bf16[128,5120]{1,0:T(8,128)(2,1)} async-done(((bf16[32,5120]{1,0:T(8,128)(2,1)}), bf16[128,5120]{1,0:T(8,128)(2,1)}) %all-gather.13.cloned.1.call-update) | async-done | bytes 1310736 | tf_op jit(solution)/shard_map/all_gather | solution.py:675
  89.6 16.4 %project.1 = (bf16[1472,3072]{1,0:T(8,128)(2,1)}, bf16[1024,3072]{1,0:T(8,128)(2,1)}) custom-call(s32[2]{0:T(128)} %pad_add_fusion.s_ref, bf16[1472,1024]{1,0:T(8,128)(2,1)} %add_convert_fusion.a_ref, f32[1,3072]{1,0:T(1,128)} %bitcast.198, bf16[256,3072]{1,0:T(8,128)(2,1)} %refs_0_.2, bf16[2,3,32,3072]{3,2,1,0:T(8,128)(2,1)} %copy-done.10, ...), custom_call_target="tpu_custom_call" | custom-call | flops 9261023232 | bytes 20000000 | tf_op jit(solution)/shard_map/project/pallas_call | solution.py:378
  110.4 4.9 all-gather.15.cloned.1.call-done
  117.0 12.2 %attend_forward.2.refs_0_ = bf16[1472,1024]{1,0:T(8,128)(2,1)} custom-call(s32[2]{0:T(128)} %pad_add_fusion.1.s_ref, bf16[1472,3072]{1,0:T(8,128)(2,1)} %get-tuple-element.146.q_ref.k_ref.v_ref.refs_0_.refs_1_.refs_2_.refs_3_.refs_4_.refs_5_, bf16[1472,3072]{1,0:T(8,128)(2,1)} %get-tuple-element.146.q_ref.k_ref.v_ref.refs_0_.refs_1_.refs_2_.refs_3_.refs_4_.refs_5_, ...), custom_call_target="tpu_custom_call" | custom-call | flops 10000000000 | bytes 10000000 | tf_op jit(solution)/shard_map/attend_forward/pallas_call | solution.py:225
  136.3 12.2 %attend_forward.3.a_ref = bf16[1472,1024]{1,0:T(8,128)(2,1)} custom-call(s32[2]{0:T(128)} %pad_add_fusion.1.s_ref, bf16[1472,3072]{1,0:T(8,128)(2,1)} %get-tuple-element.146.q_ref.k_ref.v_ref.refs_0_.refs_1_.refs_2_.refs_3_.refs_4_.refs_5_, ...), custom_call_target="tpu_custom_call", output_to_operand_aliasing={{}: (4, {})} | custom-call | flops 10000000000 | bytes 10000000 | tf_op jit(solution)/shard_map/attend_forward/pallas_call | solution.py:225
  150.1 16.8 %branch.1 = (f32[1472,1024]{1,0:T(8,128)}, bf16[1472,1024]{1,0:T(8,128)(2,1)}, bf16[1024,5120]{1,0:T(8,128)(2,1)}) custom-call(s32[2]{0:T(128)} %pad_add_fusion.s_ref, bf16[1472,1024]{1,0:T(8,128)(2,1)} %attend_forward.3.a_ref, f32[1472,1024]{1,0:T(8,128)} %copy-done, f32[3,1024]{1,0:T(4,128)} %pad_maximum_fusion.4.vec_ref, bf16[256,5120]{1,0:T(8,128)(2,1)} %copy-done.1, ...), custom_call_target="tpu_custom_call" | custom-call | flops 3087007744 | bytes 30000000 | tf_op jit(solution)/shard_map/branch/pallas_call | solution.py:406
  166.9 27.3 %hidden_layer.1 = (bf16[1472,4096]{1,0:T(8,128)(2,1)}, bf16[1472,4096]{1,0:T(8,128)(2,1)}) custom-call(bf16[1472,1024]{1,0:T(8,128)(2,1)} %get-tuple-element.187.x_ref.a_ref, bf16[1024,5120]{1,0:T(8,128)(2,1)} %get-tuple-element.162.w_ref.o_ref, f32[1,4096]{1,0:T(1,128)} %bitcast.195), custom_call_target="tpu_custom_call" | custom-call | flops 24000000000 | bytes 40000000 | tf_op jit(solution)/shard_map/hidden_layer/pallas_call | solution.py:275
  198.6 11.8 %grad_send.5 = bf16[4096,512]{1,0:T(8,128)(2,1)} custom-call(s32[2]{0:T(128)} %pad_add_fusion.4.c_ref, f32[1]{0:T(128)} %bitcast.32.f_ref, bf16[1472,4096]{1,0:T(8,128)(2,1)} %get-tuple-element.241.a_ref, bf16[1472,1024]{1,0:T(8,128)(2,1)} %pad.18.b_ref.g_ref), custom_call_target="tpu_custom_call" | custom-call | flops 6174015488 | bytes 10000000 | tf_op jit(solution)/shard_map/grad_send/pallas_call | solution.py:626
  211.2 24.0 %hidden_back.1 = (bf16[1472,4096]{1,0:T(8,128)(2,1)}, f32[1,4096]{1,0:T(1,128)}, bf16[4096,1024]{1,0:T(8,128)(2,1)}) custom-call(s32[2]{0:T(128)} %pad_add_fusion.s_ref, bf16[1472,1024]{1,0:T(8,128)(2,1)} %pad.18.b_ref.g_ref, bf16[1472,4096]{1,0:T(8,128)(2,1)} %get-tuple-element.171.slope_ref, bf16[1024,1024]{1,0:T(8,128)(2,1)} %refs_0_.3, ...), custom_call_target="tpu_custom_call" | custom-call | flops 17999998976 | bytes 40000000 | tf_op jit(solution)/shard_map/hidden_back/pallas_call | solution.py:310
  235.2 13.1 %grad_keep.5 = (bf16[2,4,256,512]{3,2,1,0:T(8,128)(2,1)}, bf16[2,4,256,512]{3,2,1,0:T(8,128)(2,1)}) custom-call(s32[2]{0:T(128)} %pad_add_fusion.5.c_ref, f32[1]{0:T(128)} %bitcast.32.f_ref, bf16[1472,4096]{1,0:T(8,128)(2,1)} %get-tuple-element.241.a_ref, bf16[1472,1024]{1,0:T(8,128)(2,1)} %pad.18.b_ref.g_ref, bf16[4096,512]{1,0:T(8,128)(2,1)} %collective-permute-done.18.got_ref), custom_call_target="tpu_custom_call" | custom-call | flops 6174015488 | bytes 10000000 | tf_op jit(solution)/shard_map/grad_keep/pallas_call | solution.py:626
  248.2 11.4 %grad_send.6 = bf16[1024,2048]{1,0:T(8,128)(2,1)} custom-call(s32[2]{0:T(128)} %pad_add_fusion.4.c_ref, f32[1]{0:T(128)} %bitcast.32.f_ref, bf16[1472,1024]{1,0:T(8,128)(2,1)} %get-tuple-element.187.x_ref.a_ref, bf16[1472,4096]{1,0:T(8,128)(2,1)} %get-tuple-element.181.b_ref.h_ref), custom_call_target="tpu_custom_call" | custom-call | flops 6174015488 | bytes 10000000 | tf_op jit(solution)/shard_map/grad_send/pallas_call | solution.py:626
  261.6 26.1 %second_back.1 = (f32[1472,1024]{1,0:T(8,128)}, bf16[1472,1024]{1,0:T(8,128)(2,1)}, bf16[1472,1024]{1,0:T(8,128)(2,1)}, f32[8,1024]{1,0:T(8,128)}) custom-call(bf16[1472,4096]{1,0:T(8,128)(2,1)} %get-tuple-element.181.b_ref.h_ref, bf16[1024,5120]{1,0:T(8,128)(2,1)} %get-tuple-element.162.w_ref.o_ref, bf16[1024,5120]{1,0:T(8,128)(2,1)} %get-tuple-element.162.w_ref.o_ref, ...), custom_call_target="tpu_custom_call" | custom-call | flops 12348030976 | bytes 40000000 | tf_op jit(solution)/shard_map/second_back/pallas_call | solution.py:466
  292.0 12.4 %grad_keep.6 = (bf16[2,4,64,2048]{3,2,1,0:T(8,128)(2,1)}, bf16[2,4,64,2048]{3,2,1,0:T(8,128)(2,1)}) custom-call(s32[2]{0:T(128)} %pad_add_fusion.5.c_ref, f32[1]{0:T(128)} %bitcast.32.f_ref, bf16[1472,1024]{1,0:T(8,128)(2,1)} %get-tuple-element.187.x_ref.a_ref, bf16[1472,4096]{1,0:T(8,128)(2,1)} %get-tuple-element.181.b_ref.h_ref, ...), custom_call_target="tpu_custom_call" | custom-call | flops 6174015488 | bytes 10000000 | tf_op jit(solution)/shard_map/grad_keep/pallas_call | solution.py:626
  307.7 5.8 %grad_send.7 = bf16[1024,512]{1,0:T(8,128)(2,1)} custom-call(s32[2]{0:T(128)} %pad_add_fusion.4.c_ref, f32[1]{0:T(128)} %bitcast.32.f_ref, bf16[1472,1024]{1,0:T(8,128)(2,1)} %attend_forward.3.a_ref, bf16[1472,1024]{1,0:T(8,128)(2,1)} %get-tuple-element.203.b_ref), custom_call_target="tpu_custom_call" | custom-call | flops 1543503872 | bytes 10000000 | tf_op jit(solution)/shard_map/grad_send/pallas_call | solution.py:626
  313.4 22.4 %attend_backward.2 = (bf16[3,1472,256]{2,1,0:T(8,128)(2,1)}, bf16[3,1472,256]{2,1,0:T(8,128)(2,1)}) custom-call(s32[4]{0:T(128)} %get-tuple-element.300.s_ref, bf16[1472,3072]{1,0:T(8,128)(2,1)} %get-tuple-element.146.q_ref.k_ref.v_ref.refs_0_.refs_1_.refs_2_.refs_3_.refs_4_.refs_5_, ...), custom_call_target="tpu_custom_call" | custom-call | flops 20000000000 | bytes 10000000 | tf_op jit(solution)/shard_map/attend_backward/pallas_call | solution.py:247
  340.1 6.7 %grad_send.8 = bf16[1024,768]{1,0:T(8,128)(2,1)} custom-call(s32[2]{0:T(128)} %pad_add_fusion.4.c_ref, f32[1]{0:T(128)} %bitcast.32.f_ref, bf16[1472,1024]{1,0:T(8,128)(2,1)} %add_convert_fusion.a_ref, bf16[3,1472,256]{2,1,0:T(8,128)(2,1)} %get-tuple-element.223.b_ref.refs_1_), custom_call_target="tpu_custom_call" | custom-call | flops 2315255808 | bytes 10000000 | tf_op jit(solution)/shard_map/grad_send/pallas_call | solution.py:626
  348.6 6.2 %grad_keep.7 = (bf16[2,4,64,512]{3,2,1,0:T(8,128)(2,1)}, bf16[2,4,64,512]{3,2,1,0:T(8,128)(2,1)}) custom-call(s32[2]{0:T(128)} %pad_add_fusion.5.c_ref, f32[1]{0:T(128)} %bitcast.32.f_ref, bf16[1472,1024]{1,0:T(8,128)(2,1)} %attend_forward.3.a_ref, bf16[1472,1024]{1,0:T(8,128)(2,1)} %get-tuple-element.203.b_ref, bf16[1024,512]{1,0:T(8,128)(2,1)} %copy-done.14), custom_call_target="tpu_custom_call" | custom-call | flops 1543503872 | bytes 10000000 | tf_op jit(solution)/shard_map/grad_keep/pallas_call | solution.py:626
  354.9 7.1 %grad_keep.8 = (bf16[2,4,64,768]{3,2,1,0:T(8,128)(2,1)}, bf16[2,4,64,768]{3,2,1,0:T(8,128)(2,1)}) custom-call(s32[2]{0:T(128)} %pad_add_fusion.5.c_ref, f32[1]{0:T(128)} %bitcast.32.f_ref, bf16[1472,1024]{1,0:T(8,128)(2,1)} %add_convert_fusion.a_ref, bf16[3,1472,256]{2,1,0:T(8,128)(2,1)} %get-tuple-element.222.b_ref.refs_0_, ...), custom_call_target="tpu_custom_call" | custom-call | flops 2315255808 | bytes 10000000 | tf_op jit(solution)/shard_map/grad_keep/pallas_call | solution.py:626
  371.1 21.9 %attend_backward.3 = (bf16[3,1472,256]{2,1,0:T(8,128)(2,1)}, bf16[3,1472,256]{2,1,0:T(8,128)(2,1)}) custom-call(s32[4]{0:T(128)} %add_add_fusion.1.s_ref, bf16[1472,3072]{1,0:T(8,128)(2,1)} %get-tuple-element.146.q_ref.k_ref.v_ref.refs_0_.refs_1_.refs_2_.refs_3_.refs_4_.refs_5_, ...), custom_call_target="tpu_custom_call" | custom-call | flops 20000000000 | bytes 10000000 | tf_op jit(solution)/shard_map/attend_backward/pallas_call | solution.py:247
  395.5 6.7 %grad_send.9 = bf16[1024,768]{1,0:T(8,128)(2,1)} custom-call(s32[2]{0:T(128)} %pad_add_fusion.4.c_ref, f32[1]{0:T(128)} %bitcast.32.f_ref, bf16[1472,1024]{1,0:T(8,128)(2,1)} %add_convert_fusion.a_ref, bf16[3,1472,256]{2,1,0:T(8,128)(2,1)} %get-tuple-element.225.b_ref.refs_3_), custom_call_target="tpu_custom_call" | custom-call | flops 2315255808 | bytes 10000000 | tf_op jit(solution)/shard_map/grad_send/pallas_call | solution.py:626
  404.2 10.3 %collective-permute-done.28 = bf16[4,64,1280]{2,1,0:T(8,128)(2,1)S(1)} collective-permute-done((bf16[4,64,1280]{2,1,0:T(8,128)(2,1)}, bf16[4,64,1280]{2,1,0:T(8,128)(2,1)S(1)}, u32[]{:S(2)}, u32[]{:S(2)}) %collective-permute-start.28) | collective-permute-done | bytes 655392 | tf_op jit(solution)/shard_map/ppermute | solution.py:642
  419.3 4.2 widen.5
  423.5 4.6 reduce-scatter.8.cloned.1.call-done
  428.2 7.4 %grad_keep.9 = (bf16[2,4,64,768]{3,2,1,0:T(8,128)(2,1)}, bf16[2,4,64,768]{3,2,1,0:T(8,128)(2,1)}) custom-call(s32[2]{0:T(128)} %pad_add_fusion.5.c_ref, f32[1]{0:T(128)} %bitcast.32.f_ref, bf16[1472,1024]{1,0:T(8,128)(2,1)} %add_convert_fusion.a_ref, bf16[3,1472,256]{2,1,0:T(8,128)(2,1)} %get-tuple-element.224.b_ref.refs_2_, ...), custom_call_target="tpu_custom_call" | custom-call | flops 2315255808 | bytes 10000000 | tf_op jit(solution)/shard_map/grad_keep/pallas_call | solution.py:626
  437.0 24.1 %first_back.1 = (bf16[1450,1024]{1,0:T(8,128)(2,1)}, f32[50,1024]{1,0:T(8,128)}, f32[8,1024]{1,0:T(8,128)}, f32[8,256]{1,0:T(8,128)}) custom-call(s32[4]{0:T(128)} %get-tuple-element.299.s_ref, bf16[3,1472,256]{2,1,0:T(8,128)(2,1)} %get-tuple-element.222.b_ref.refs_0_, bf16[3,1472,256]{2,1,0:T(8,128)(2,1)} %get-tuple-element.223.b_ref.refs_1_, ...), custom_call_target="tpu_custom_call" | custom-call | flops 9261023232 | bytes 40000000 | tf_op jit(solution)/shard_map/first_back/pallas_call | solution.py:529
  476.0 19.0 %return_layer.1 = bf16[1450,1024]{1,0:T(8,128)(2,1)} custom-call(bf16[1472,4096]{1,0:T(8,128)(2,1)} %get-tuple-element.241.a_ref, bf16[4096,1024]{1,0:T(8,128)(2,1)} %get-tuple-element.242.w_ref, f32[1472,1024]{1,0:T(8,128)} %get-tuple-element.182.mid_ref, f32[1,1024]{1,0:T(1,128)} %bitcast.199), custom_call_target="tpu_custom_call" | custom-call | flops 12348030976 | bytes 30000000 | tf_op jit(solution)/shard_map/return_layer/pallas_call | solution.py:432
  500.8 9.6 %all-gather.3 = bf16[1024,128]{1,0:T(8,128)(2,1)S(1)} all-gather(bf16[128,128]{1,0:T(8,128)(2,1)S(1)} %fusion.17), channel_id=5, replica_groups=mesh['dp'=8,'fsdp'=4] {'dp'}, dimensions={0}, use_global_device_ids=true | all-gather | bytes 294912 | tf_op jit(solution)/shard_map/all_gather | solution.py:805
  511.1 10.8 %all-gather.5 = bf16[512,768]{1,0:T(8,128)(2,1)} all-gather(bf16[64,768]{1,0:T(8,128)(2,1)S(1)} %fusion.15), channel_id=7, replica_groups=mesh['dp'=8,'fsdp'=4] {'dp'}, dimensions={0}, use_global_device_ids=true | all-gather | bytes 884736 | tf_op jit(solution)/shard_map/all_gather | solution.py:764
  (292 shorter events, 131.5 us)
Async XLA Ops:
  7.2 76.8 %all-gather.13.cloned.1.call-start = ((), (), s32[]{:S(2)}) async-start(), calls=%async_computation.6 | async-start | bytes 1638400 | tf_op jit(solution)/shard_map/all_gather | solution.py:675
  8.9 33.5 %collective-permute-start.3 = (bf16[32,3072]{1,0:T(8,128)(2,1)}, bf16[32,3072]{1,0:T(8,128)(2,1)}, u32[]{:S(2)}, u32[]{:S(2)}) collective-permute-start(bf16[32,3072]{1,0:T(8,128)(2,1)} %constant_dynamic-slice_fusion.2), channel_id=1, source_target_pairs={{1,0},{2,1},{3,2},{0,3},{5,4},{6,5},{7,6},{4,7},{9,8},{10,9},{11,1... | collective-permute-start | bytes 589832 | tf_op jit(solution)/shard_map/ppermute | solution.py:668
  13.9 28.4 %collective-permute-start.4 = (bf16[32,3072]{1,0:T(8,128)(2,1)}, bf16[32,3072]{1,0:T(8,128)(2,1)}, u32[]{:S(2)}, u32[]{:S(2)}) collective-permute-start(bf16[32,3072]{1,0:T(8,128)(2,1)} %constant_dynamic-slice_fusion.2), channel_id=1, source_target_pairs={{2,0},{3,1},{0,2},{1,3},{6,4},{7,5},{4,6},{5,7},{10,8},{11,9},{8,1... | collective-permute-start | bytes 589832 | tf_op jit(solution)/shard_map/ppermute | solution.py:668
  13.9 28.4 %collective-permute-start.5 = (bf16[32,3072]{1,0:T(8,128)(2,1)}, bf16[32,3072]{1,0:T(8,128)(2,1)}, u32[]{:S(2)}, u32[]{:S(2)}) collective-permute-start(bf16[32,3072]{1,0:T(8,128)(2,1)} %constant_dynamic-slice_fusion.2), channel_id=1, source_target_pairs={{3,0},{0,1},{1,2},{2,3},{7,4},{4,5},{5,6},{6,7},{11,8},{8,9},{9,10... | collective-permute-start | bytes 589832 | tf_op jit(solution)/shard_map/ppermute | solution.py:668
  53.7 61.5 %all-gather.15.cloned.1.call-start = ((), (), s32[]{:S(2)}) async-start(), calls=%async_computation.7 | async-start | bytes 1310720 | tf_op jit(solution)/shard_map/all_gather | solution.py:675
  55.8 16.4 %collective-permute-start.7 = (bf16[2,3,32,3072]{3,2,1,0:T(8,128)(2,1)S(1)}, bf16[2,3,32,3072]{3,2,1,0:T(8,128)(2,1)}, u32[]{:S(2)}, u32[]{:S(2)}) collective-permute-start(bf16[2,3,32,3072]{3,2,1,0:T(8,128)(2,1)S(1)} %pad_maximum_fusion.2.refs_1_), channel_id=1, source_target_pairs={{0,16},{4,12},{8,24},{12,4},{16,0},{20,28},{24,8},{28,20},{1,17},{... | collective-permute-start | bytes 3538952 | tf_op jit(solution)/shard_map/ppermute | solution.py:642
  63.3 22.6 %collective-permute-start.8 = (bf16[2,3,32,3072]{3,2,1,0:T(8,128)(2,1)S(1)}, bf16[2,3,32,3072]{3,2,1,0:T(8,128)(2,1)}, u32[]{:S(2)}, u32[]{:S(2)}) collective-permute-start(bf16[2,3,32,3072]{3,2,1,0:T(8,128)(2,1)S(1)} %pad_maximum_fusion.2.refs_1_), channel_id=1, source_target_pairs={{0,4},{4,0},{8,12},{12,8},{16,20},{20,16},{24,28},{28,24},{1,5},{5... | collective-permute-start | bytes 3538952 | tf_op jit(solution)/shard_map/ppermute | solution.py:642
  85.9 20.0 %collective-permute-start.10 = (bf16[3,32,5120]{2,1,0:T(8,128)(2,1)S(1)}, bf16[3,32,5120]{2,1,0:T(8,128)(2,1)S(1)}, u32[]{:S(2)}, u32[]{:S(2)}) collective-permute-start(bf16[3,32,5120]{2,1,0:T(8,128)(2,1)S(1)} %fusion.5), channel_id=1, source_target_pairs={{0,8},{4,20},{8,0},{12,28},{16,24},{20,4},{24,16},{28,12},{1,9},{5... | collective-permute-start | bytes 2949128 | tf_op jit(solution)/shard_map/ppermute | solution.py:642
  89.1 257.7 %reduce-scatter.4.cloned.1.call-start = ((), (), s32[]{:S(2)}) async-start(), calls=%async_computation.3 | async-start | bytes 1310720 | tf_op jit(solution)/shard_map/reduce_scatter | solution.py:787
  108.3 24.8 %collective-permute-start.11 = (bf16[2,3,32,5120]{3,2,1,0:T(8,128)(2,1)S(1)}, bf16[2,3,32,5120]{3,2,1,0:T(8,128)(2,1)}, u32[]{:S(2)}, u32[]{:S(2)}) collective-permute-start(bf16[2,3,32,5120]{3,2,1,0:T(8,128)(2,1)S(1)} %pad_maximum_fusion.refs_1_), channel_id=1, source_target_pairs={{0,16},{4,12},{8,24},{12,4},{16,0},{20,28},{24,8},{28,20},{1,17},{... | collective-permute-start | bytes 5898248 | tf_op jit(solution)/shard_map/ppermute | solution.py:642
  133.1 15.3 %collective-permute-start.13 = (bf16[2,3,32,5120]{3,2,1,0:T(8,128)(2,1)}, bf16[2,3,32,5120]{3,2,1,0:T(8,128)(2,1)}, u32[]{:S(2)}, u32[]{:S(2)}) collective-permute-start(bf16[2,3,32,5120]{3,2,1,0:T(8,128)(2,1)} %collective-permute-done.11.refs_2_), channel_id=1, source_target_pairs={{0,4},{4,0},{8,12},{12,8},{16,20},{20,16},{24,28},{28,24},{1,5},{5... | collective-permute-start | bytes 5898248 | tf_op jit(solution)/shard_map/ppermute | solution.py:642
  148.6 45.5 %collective-permute-start.15 = (bf16[2,3,128,1024]{3,2,1,0:T(8,128)(2,1)S(1)}, bf16[2,3,128,1024]{3,2,1,0:T(8,128)(2,1)S(1)}, u32[]{:S(2)}, u32[]{:S(2)}) collective-permute-start(bf16[2,3,128,1024]{3,2,1,0:T(8,128)(2,1)S(1)} %pad_maximum_fusion.1.refs_1_), channel_id=1, source_target_pairs={{0,16},{4,12},{8,24},{12,4},{16,0},{20,28},{24,8},{28,20},{1,17},{... | collective-permute-start | bytes 4718600 | tf_op jit(solution)/shard_map/ppermute | solution.py:642
  194.1 16.3 %collective-permute-start.16 = (bf16[2,3,128,1024]{3,2,1,0:T(8,128)(2,1)S(1)}, bf16[2,3,128,1024]{3,2,1,0:T(8,128)(2,1)}, u32[]{:S(2)}, u32[]{:S(2)}) collective-permute-start(bf16[2,3,128,1024]{3,2,1,0:T(8,128)(2,1)S(1)} %pad_maximum_fusion.1.refs_1_), channel_id=1, source_target_pairs={{0,4},{4,0},{8,12},{12,8},{16,20},{20,16},{24,28},{28,24},{1,5},{5... | collective-permute-start | bytes 4718600 | tf_op jit(solution)/shard_map/ppermute | solution.py:642
  194.2 16.2 %collective-permute-start.17 = (bf16[2,3,128,1024]{3,2,1,0:T(8,128)(2,1)S(1)}, bf16[2,3,128,1024]{3,2,1,0:T(8,128)(2,1)}, u32[]{:S(2)}, u32[]{:S(2)}) collective-permute-start(bf16[2,3,128,1024]{3,2,1,0:T(8,128)(2,1)S(1)} %collective-permute-done.15.refs_2_), channel_id=1, source_target_pairs={{0,4},{4,0},{8,12},{12,8},{16,20},{20,16},{24,28},{28,24},{1,5},{5... | collective-permute-start | bytes 4718600 | tf_op jit(solution)/shard_map/ppermute | solution.py:642
  210.4 24.8 %collective-permute-start.18 = (bf16[4096,512]{1,0:T(8,128)(2,1)}, bf16[4096,512]{1,0:T(8,128)(2,1)}, u32[]{:S(2)}, u32[]{:S(2)}) collective-permute-start(bf16[4096,512]{1,0:T(8,128)(2,1)} %grad_send.5), channel_id=1, source_target_pairs={{0,4},{4,0},{8,12},{12,8},{16,20},{20,16},{24,28},{28,24},{1,5},{5... | collective-permute-start | bytes 12582920 | tf_op jit(solution)/shard_map/ppermute | solution.py:642
  259.6 28.1 %collective-permute-start.19 = (bf16[1024,2048]{1,0:T(8,128)(2,1)}, bf16[1024,2048]{1,0:T(8,128)(2,1)}, u32[]{:S(2)}, u32[]{:S(2)}) collective-permute-start(bf16[1024,2048]{1,0:T(8,128)(2,1)} %grad_send.6), channel_id=1, source_target_pairs={{0,4},{4,0},{8,12},{12,8},{16,20},{20,16},{24,28},{28,24},{1,5},{5... | collective-permute-start | bytes 12582920 | tf_op jit(solution)/shard_map/ppermute | solution.py:642
  260.1 27.6 %collective-permute-start.20 = (bf16[2,4,256,512]{3,2,1,0:T(8,128)(2,1)}, bf16[2,4,256,512]{3,2,1,0:T(8,128)(2,1)}, u32[]{:S(2)}, u32[]{:S(2)}) collective-permute-start(bf16[2,4,256,512]{3,2,1,0:T(8,128)(2,1)} %get-tuple-element.179), channel_id=1, source_target_pairs={{0,8},{4,20},{8,0},{12,28},{16,24},{20,4},{24,16},{28,12},{1,9},{5... | collective-permute-start | bytes 6291464 | tf_op jit(solution)/shard_map/ppermute | solution.py:642
  305.8 30.0 %collective-permute-start.23 = (bf16[2,4,64,2048]{3,2,1,0:T(8,128)(2,1)}, bf16[2,4,64,2048]{3,2,1,0:T(8,128)(2,1)}, u32[]{:S(2)}, u32[]{:S(2)}) collective-permute-start(bf16[2,4,64,2048]{3,2,1,0:T(8,128)(2,1)} %get-tuple-element.195), channel_id=1, source_target_pairs={{0,8},{4,20},{8,0},{12,28},{16,24},{20,4},{24,16},{28,12},{1,9},{5... | collective-permute-start | bytes 6291464 | tf_op jit(solution)/shard_map/ppermute | solution.py:642
  307.6 85.4 %all-gather.17.cloned.1.call-start = ((), (), s32[]{:S(2)}) async-start(), calls=%async_computation.8 | async-start | bytes 2359296 | tf_op jit(solution)/shard_map/all_gather | solution.py:764
  313.4 22.4 %collective-permute-start.22 = (bf16[1024,512]{1,0:T(8,128)(2,1)}, bf16[1024,512]{1,0:T(8,128)(2,1)S(1)}, u32[]{:S(2)}, u32[]{:S(2)}) collective-permute-start(bf16[1024,512]{1,0:T(8,128)(2,1)} %grad_send.7), channel_id=1, source_target_pairs={{0,4},{4,0},{8,12},{12,8},{16,20},{20,16},{24,28},{28,24},{1,5},{5... | collective-permute-start | bytes 3145736 | tf_op jit(solution)/shard_map/ppermute | solution.py:642
  347.3 80.8 %reduce-scatter.8.cloned.1.call-start = ((), (), s32[]{:S(2)}) async-start(), calls=%async_computation.5 | async-start | bytes 1310720 | tf_op jit(solution)/shard_map/reduce_scatter | solution.py:787
  347.3 17.7 %collective-permute-start.25 = (bf16[4,64,2048]{2,1,0:T(8,128)(2,1)S(1)}, bf16[4,64,2048]{2,1,0:T(8,128)(2,1)S(1)}, u32[]{:S(2)}, u32[]{:S(2)}) collective-permute-start(bf16[4,64,2048]{2,1,0:T(8,128)(2,1)S(1)} %copy-done.13), channel_id=1, source_target_pairs={{0,16},{4,12},{8,24},{12,4},{16,0},{20,28},{24,8},{28,20},{1,17},{... | collective-permute-start | bytes 3145736 | tf_op jit(solution)/shard_map/ppermute | solution.py:642
  369.4 23.7 %collective-permute-start.26 = (bf16[2,4,64,1280]{3,2,1,0:T(8,128)(2,1)}, bf16[2,4,64,1280]{3,2,1,0:T(8,128)(2,1)}, u32[]{:S(2)}, u32[]{:S(2)}) collective-permute-start(bf16[2,4,64,1280]{3,2,1,0:T(8,128)(2,1)} %constant_dynamic-update-slice_fusion.10), channel_id=1, source_target_pairs={{0,8},{4,20},{8,0},{12,28},{16,24},{20,4},{24,16},{28,12},{1,9},{5... | collective-permute-start | bytes 3932168 | tf_op jit(solution)/shard_map/ppermute | solution.py:642
  403.6 72.4 %reduce-scatter.6.cloned.1.call-start = ((), (), s32[]{:S(2)}) async-start(), calls=%async_computation.4 | async-start | bytes 819200 | tf_op jit(solution)/shard_map/reduce_scatter | solution.py:787
  415.5 107.6 %all-gather.21.cloned.1.call-start = ((), (), s32[]{:S(2)}) async-start(), calls=%async_computation.10 | async-start | bytes 2359296 | tf_op jit(solution)/shard_map/all_gather | solution.py:764
  428.1 99.2 %all-gather.19.cloned.1.call-start = ((), (), s32[]{:S(2)}) async-start(), calls=%async_computation.9 | async-start | bytes 1474560 | tf_op jit(solution)/shard_map/all_gather | solution.py:764
  435.5 25.6 %collective-permute-start.29 = (bf16[2,4,64,768]{3,2,1,0:T(8,128)(2,1)}, bf16[2,4,64,768]{3,2,1,0:T(8,128)(2,1)S(1)}, u32[]{:S(2)}, u32[]{:S(2)}) collective-permute-start(bf16[2,4,64,768]{3,2,1,0:T(8,128)(2,1)} %get-tuple-element.221), channel_id=1, source_target_pairs={{0,8},{4,20},{8,0},{12,28},{16,24},{20,4},{24,16},{28,12},{1,9},{5... | collective-permute-start | bytes 2359304 | tf_op jit(solution)/shard_map/ppermute | solution.py:642
  469.2 25.7 %collective-permute-start.34 = (bf16[128,128]{1,0:T(8,128)(2,1)S(1)}, bf16[128,128]{1,0:T(8,128)(2,1)S(1)}, u32[]{:S(2)}, u32[]{:S(2)}) collective-permute-start(bf16[128,128]{1,0:T(8,128)(2,1)S(1)} %get-tuple-element.278), channel_id=1, source_target_pairs={{0,1},{1,2},{2,3},{3,0},{4,5},{5,6},{6,7},{7,4},{8,9},{9,10},{10,1... | collective-permute-start | bytes 98312 | tf_op jit(solution)/shard_map/ppermute | solution.py:799
  470.8 26.9 %collective-permute-start.35 = (bf16[128,128]{1,0:T(8,128)(2,1)S(1)}, bf16[128,128]{1,0:T(8,128)(2,1)S(1)}, u32[]{:S(2)}, u32[]{:S(2)}) collective-permute-start(bf16[128,128]{1,0:T(8,128)(2,1)S(1)} %get-tuple-element.280), channel_id=1, source_target_pairs={{0,2},{1,3},{2,0},{3,1},{4,6},{5,7},{6,4},{7,5},{8,10},{9,11},{10,... | collective-permute-start | bytes 98312 | tf_op jit(solution)/shard_map/ppermute | solution.py:799
  473.2 24.5 %collective-permute-start.36 = (bf16[128,128]{1,0:T(8,128)(2,1)S(1)}, bf16[128,128]{1,0:T(8,128)(2,1)S(1)}, u32[]{:S(2)}, u32[]{:S(2)}) collective-permute-start(bf16[128,128]{1,0:T(8,128)(2,1)S(1)} %get-tuple-element.279), channel_id=1, source_target_pairs={{0,3},{1,0},{2,1},{3,2},{4,7},{5,4},{6,5},{7,6},{8,11},{9,8},{10,9... | collective-permute-start | bytes 98312 | tf_op jit(solution)/shard_map/ppermute | solution.py:799
  474.8 22.9 %collective-permute-start.31 = (bf16[64,768]{1,0:T(8,128)(2,1)S(1)}, bf16[64,768]{1,0:T(8,128)(2,1)S(1)}, u32[]{:S(2)}, u32[]{:S(2)}) collective-permute-start(bf16[64,768]{1,0:T(8,128)(2,1)S(1)} %get-tuple-element.266), channel_id=1, source_target_pairs={{0,1},{1,2},{2,3},{3,0},{4,5},{5,6},{6,7},{7,4},{8,9},{9,10},{10,1... | collective-permute-start | bytes 294920 | tf_op jit(solution)/shard_map/ppermute | solution.py:799
  475.4 22.3 %collective-permute-start.32 = (bf16[64,768]{1,0:T(8,128)(2,1)S(1)}, bf16[64,768]{1,0:T(8,128)(2,1)S(1)}, u32[]{:S(2)}, u32[]{:S(2)}) collective-permute-start(bf16[64,768]{1,0:T(8,128)(2,1)S(1)} %get-tuple-element.268), channel_id=1, source_target_pairs={{0,2},{1,3},{2,0},{3,1},{4,6},{5,7},{6,4},{7,5},{8,10},{9,11},{10,... | collective-permute-start | bytes 294920 | tf_op jit(solution)/shard_map/ppermute | solution.py:799
  (48 other events, 599.5 us)
Sparse Core Ops, SparseCore 0:
  53.9 30.0 all-gather.12
  89.2 26.0 all-gather.14
  307.8 25.1 reduce-scatter.3
  347.4 28.5 all-gather.16
  403.7 24.4 reduce-scatter.7
  430.3 20.7 reduce-scatter.5
  453.0 28.2 all-gather.20
  483.1 24.9 all-gather.18

commit v4 on v3

v4 whole, which is shorter than its diff:
```python
from functools import partial

import jax
import jax.numpy as jnp
from jax import lax
from jax.experimental import pallas as pl
from jax.experimental.pallas import tpu as pltpu
from jax.sharding import PartitionSpec as P

D = 1024
HEADS = 16
HEAD_DIM = 64
SG = 7
LG = 12
SMALL_LEN = 50
LARGE_LEN = 145
ROWS = 1450
PAD = 1472
GROUP = 8
WINDOW = 176
WINDOWS = 10
ROW_TILE = 368
FAR = -1e30
LOW = jnp.bfloat16
ANYWHERE = pl.BlockSpec(memory_space=pl.ANY)


EPS = 1e-06


def grid_fraction(index):
    scaled = jnp.maximum((2 * index + 1) * SG - LG, 0)
    lower = scaled // (2 * LG)
    return (scaled - 2 * LG * lower).astype(jnp.float32) / (2.0 * LG)


def interp_table(position_source):
    position = jnp.arange(LARGE_LEN, dtype=jnp.int32)
    patch = jnp.maximum(position - 1, 0)
    frac_row = grid_fraction(patch // LG)
    frac_col = grid_fraction(patch % LG)
    weights = jnp.stack(
        [
            (1.0 - frac_row) * (1.0 - frac_col),
            (1.0 - frac_row) * frac_col,
            frac_row * (1.0 - frac_col),
            frac_row * frac_col,
        ],
        axis=1,
    )
    class_row = (jnp.arange(4, dtype=jnp.int32) == 0).astype(jnp.float32)
    weights = jnp.where((position == 0)[:, None], class_row[None, :], weights)
    onehot = (
        position_source[:, :, None] == jnp.arange(SMALL_LEN, dtype=jnp.int32)[None, None, :]
    ).astype(jnp.float32)
    return jnp.sum(weights[:, :, None] * onehot, axis=1)


def dot_nt(left, right):
    return lax.dot_general(
        left, right, (((1,), (1,)), ((), ())), preferred_element_type=jnp.float32
    )


def dot_nn(left, right):
    return lax.dot_general(
        left, right, (((1,), (0,)), ((), ())), preferred_element_type=jnp.float32
    )


def dot_tn(left, right):
    return lax.dot_general(
        left, right, (((0,), (0,)), ((), ())), preferred_element_type=jnp.float32
    )


def cost(flops, moved):
    return pl.CostEstimate(flops=int(flops), transcendentals=0, bytes_accessed=int(moved))


def after(value, *others):
    return lax.optimization_barrier((value, *others))[0]


def sync(*values):
    return lax.optimization_barrier(values)


def window_start(window, step):
    return pl.multiple_of(jnp.minimum(window * step // 16 * 16, PAD - WINDOW), 16)


def image_of(row, length, step):
    image = jnp.where(row >= length, 1, 0) + jnp.where(row >= 2 * length, 1, 0)
    return jnp.where(row < 0, -1, jnp.where(row >= step, 3, image))


def mask_kernel(s_ref, mask_ref):
    length, step = s_ref[0], s_ref[1]

    def one(window, carry):
        base = window_start(window, step) - window * step
        shape = (WINDOW, 2 * WINDOW)
        rows = image_of(lax.broadcasted_iota(jnp.int32, shape, 0) + base, length, step)
        cols = lax.broadcasted_iota(jnp.int32, shape, 1)
        cols = jnp.where(cols < WINDOW, cols, cols - WINDOW)
        cols = image_of(cols + base, length, step)
        mask_ref[window] = jnp.where(rows == cols, 0.0, FAR).astype(jnp.float32)
        return carry

    lax.fori_loop(0, WINDOWS, one, 0)


def image_masks(lengths):
    return pl.pallas_call(
        mask_kernel,
        out_shape=jax.ShapeDtypeStruct((WINDOWS, WINDOW, 2 * WINDOW), jnp.float32),
        in_specs=[pl.BlockSpec(memory_space=pltpu.SMEM)],
        name="image_masks",
    )(lengths)


MASKS = pl.BlockSpec((WINDOWS, WINDOW, 2 * WINDOW), lambda i, s: (0, 0, 0))


def split_heads(value):
    lane = lax.broadcasted_iota(jnp.int32, value.shape, 1)
    zero = jnp.zeros_like(value)
    even, odd = jnp.where(lane < HEAD_DIM, value, zero), jnp.where(lane < HEAD_DIM, zero, value)
    return jnp.concatenate([even, odd], axis=0)


def slabs(refs, at):
    return [ref[at, i : i + 128] for ref in refs for i in range(0, ref.shape[1], 128)]


def join_heads(value):
    even, odd = value[:WINDOW], value[WINDOW:]
    lane = lax.broadcasted_iota(jnp.int32, even.shape, 1)
    return jnp.where(lane < HEAD_DIM, even, odd)


def keep_rows(ref, start, first, value):
    row = lax.broadcasted_iota(jnp.int32, value.shape, 0) + start
    value = jnp.where(row < ROWS, value, 0.0)
    at = pl.ds(start, WINDOW)
    old = ref[at, :].astype(jnp.float32)
    ref[at, :] = jnp.where(row >= first, value, old).astype(ref.dtype)


def forward_kernel(s_ref, mask_ref, q_ref, k_ref, v_ref, o_ref):
    step = s_ref[1]

    def one(window, carry):
        start = window_start(window, step)
        at = pl.ds(start, WINDOW)
        query = [split_heads(v * LOW(0.125)) for v in slabs([q_ref], at)]
        keys, values = slabs([k_ref], at), slabs([v_ref], at)
        mask = mask_ref[window]
        each = range(len(keys))
        scores = [dot_nt(keys[i], query[i]) + mask for i in each]
        top = [jnp.max(v, axis=0, keepdims=True) for v in scores]
        raised = [jnp.exp(scores[i] - top[i]) for i in each]
        scale = [1.0 / jnp.sum(v, axis=0, keepdims=True) for v in raised]
        out = [dot_tn((raised[i] * scale[i]).astype(LOW), values[i]) for i in each]
        for j in each:
            cols = slice(128 * j, 128 * j + 128)
            keep_rows(o_ref.at[:, cols], start, window * step, join_heads(out[j]))
        return carry

    lax.fori_loop(0, WINDOWS, one, 0)


def backward_kernel(s_ref, mask_ref, *refs):
    q_refs, k_refs, v_refs, g_refs, out_refs = [refs[2 * i : 2 * i + 2] for i in range(5)]
    step = s_ref[1]

    def one(window, carry):
        start = window_start(window, step)
        at = pl.ds(start, WINDOW)
        query = [split_heads(v * LOW(0.125)) for v in slabs(q_refs, at)]
        grad = [split_heads(v) for v in slabs(g_refs, at)]
        keys, values = slabs(k_refs, at), slabs(v_refs, at)
        mask = mask_ref[window]
        each = range(len(keys))
        scores = [dot_nt(keys[i], query[i]) + mask for i in each]
        grad_probs = [dot_nt(values[i], grad[i]) for i in each]
        top = [jnp.max(v, axis=0, keepdims=True) for v in scores]
        raised = [jnp.exp(scores[i] - top[i]) for i in each]
        scale = [1.0 / jnp.sum(v, axis=0, keepdims=True) for v in raised]
        probs = [raised[i] * scale[i] for i in each]
        inner = [jnp.sum(grad_probs[i] * probs[i], axis=0, keepdims=True) for i in each]
        grad_scores = [(probs[i] * (grad_probs[i] - inner[i])).astype(LOW) for i in each]
        grad_v = [dot_nn(probs[i].astype(LOW), grad[i]) for i in each]
        grad_k = [dot_nn(grad_scores[i], query[i]) for i in each]
        grad_q = [dot_tn(grad_scores[i], keys[i]) for i in each]
        first = window * step
        for j in each:
            out = out_refs[j // 2]
            cols = slice(j % 2 * 128, j % 2 * 128 + 128)
            keep_rows(out.at[0, :, cols], start, first, join_heads(grad_q[j]) * 0.125)
            keep_rows(out.at[1, :, cols], start, first, grad_k[j])
            keep_rows(out.at[2, :, cols], start, first, grad_v[j])
        return carry

    lax.fori_loop(0, WINDOWS, one, 0)


def attend_forward(lengths, masks, projected):
    def part(base):
        return pl.BlockSpec((PAD, D), lambda i, s: (0, base))

    return pl.pallas_call(
        forward_kernel,
        out_shape=jax.ShapeDtypeStruct((PAD, D), LOW),
        grid_spec=pltpu.PrefetchScalarGridSpec(
            num_scalar_prefetch=1,
            grid=(1,),
            in_specs=[MASKS, part(0), part(1), part(2)],
            out_specs=part(0),
        ),
        cost_estimate=cost(2e10, 1e7),
        name="attend_forward",
    )(lengths, masks, projected, projected, projected)


def attend_backward(numbers, masks, projected, grad):
    width = D // 4

    def part(base, i):
        return pl.BlockSpec((PAD, width), lambda n, s: (0, s[2 + i] + base))

    return pl.pallas_call(
        backward_kernel,
        out_shape=[jax.ShapeDtypeStruct((3, PAD, width), LOW)] * 2,
        grid_spec=pltpu.PrefetchScalarGridSpec(
            num_scalar_prefetch=1,
            grid=(1,),
            in_specs=[MASKS] + [part(base, i) for base in (0, 4, 8, 0) for i in (0, 1)],
            out_specs=[pl.BlockSpec((3, PAD, width), lambda n, s: (0, 0, 0))] * 2,
        ),
        cost_estimate=cost(2e10, 1e7),
        name="attend_backward",
    )(numbers, masks, *([projected] * 6), grad, grad)


def hidden_kernel(shards, steps, rows, s_ref, x_ref, b_ref, *refs):
    parts, (activ_ref, slope_ref, full), (held, sem) = refs[:5], refs[5:8], refs[8:]
    step = pl.program_id(0)
    tile = activ_ref.shape[1]
    half = held.shape[1] // 2

    def columns(i):
        return fetch_copies(shards, s_ref, parts, held, sem.at[i], i * half, i * half, half)

    def keep():
        return pltpu.make_async_copy(held, full, sem.at[0, 0])

    @pl.when(step == 0)
    def _():
        start_wait(columns(0), wait=False)
        start_wait(columns(1), wait=False)
        start_wait(columns(0), start=False)

    @pl.when(step == steps // 2)
    def _():
        start_wait(columns(1), start=False)
        keep().start()

    weight = held[:, pl.ds(pl.multiple_of(step * tile, tile), tile)]
    for i in range(PAD // rows):
        at = slice(i * rows, (i + 1) * rows)
        hidden = dot_nn(x_ref[at, :], weight) + b_ref[...]
        cdf = 0.5 * lax.erf(hidden * 0.7071067811865476) + 0.5
        density = jnp.exp(-0.5 * hidden * hidden) * 0.3989422804014327
        activ_ref[at, :] = (hidden * cdf).astype(LOW)
        slope_ref[at, :] = (cdf + hidden * density).astype(LOW)

    @pl.when(step == steps - 1)
    def _():
        keep().wait()


def hidden_layer(second, bias, shard, sets):
    width = bias.shape[0]
    tile = 512
    steps = width // tile
    return pl.pallas_call(
        partial(hidden_kernel, lax.axis_size("fsdp"), steps, 736),
        out_shape=[jax.ShapeDtypeStruct((PAD, width), LOW)] * 2 + [fetch_shape(shard, width)],
        grid_spec=pltpu.PrefetchScalarGridSpec(
            num_scalar_prefetch=1,
            grid=(steps,),
            in_specs=[
                pl.BlockSpec((PAD, D), lambda n, s: (0, 0)),
                pl.BlockSpec((1, tile), lambda n, s: (0, n)),
            ]
            + [ANYWHERE] * 5,
            out_specs=[pl.BlockSpec((PAD, tile), lambda n, s: (0, n))] * 2 + [ANYWHERE],
            scratch_shapes=fetch_scratch(shard, width, 2),
        ),
        cost_estimate=cost(2.4e10, 4e7),
        name="hidden_layer",
    )(fetch_numbers(), second, bias.reshape(1, width), shard, *sets)


def hidden_back_kernel(shards, steps, rows, s_ref, g_ref, slope_ref, *refs):
    parts, (out_ref, sum_ref, full), (held, sem) = refs[:5], refs[5:8], refs[8:]
    step = pl.program_id(0)
    per = steps // shards
    tile = out_ref.shape[1]

    def copies():
        return fetch_copies(shards, s_ref, parts, held, sem)

    def keep():
        return pltpu.make_async_copy(held, full, sem.at[0])

    @pl.when(step == 0)
    def _():
        every = copies()
        start_wait(every, wait=False)
        start_wait(every[:1], start=False)

    for k in range(1, shards):

        @pl.when(step == k * per)
        def _(k=k):
            start_wait(copies()[k :: shards - 1], start=False)
            if k == shards - 1:
                keep().start()

    block = lax.rem(s_ref[1] + step // per, shards) * per + step % per
    weight = held[pl.ds(pl.multiple_of(block * tile, tile), tile), :]
    total = jnp.zeros_like(sum_ref)
    for i in range(PAD // rows):
        at = slice(i * rows, (i + 1) * rows)
        grad = dot_nt(g_ref[at, :], weight) * slope_ref[at, :].astype(jnp.float32)
        grad = grad.astype(LOW)
        out_ref[at, :] = grad
        total = total + column_sum(grad.astype(jnp.float32))
    sum_ref[...] = total

    @pl.when(step == steps - 1)
    def _():
        keep().wait()


def hidden_back(grad, slope, shard, sets):
    width = slope.shape[1]
    tile = 512
    steps = width // tile
    shards = lax.axis_size("fsdp")
    per = steps // shards

    def block(n, s):
        return lax.rem(s[1] + n // per, shards) * per + n % per

    cols = pl.BlockSpec((PAD, tile), lambda n, s: (0, block(n, s)))
    return pl.pallas_call(
        partial(hidden_back_kernel, shards, steps, 368),
        out_shape=[
            jax.ShapeDtypeStruct((PAD, width), LOW),
            jax.ShapeDtypeStruct((1, width), jnp.float32),
            fetch_shape(shard),
        ],
        grid_spec=pltpu.PrefetchScalarGridSpec(
            num_scalar_prefetch=1,
            grid=(steps,),
            in_specs=[pl.BlockSpec((PAD, D), lambda n, s: (0, 0)), cols] + [ANYWHERE] * 5,
            out_specs=[cols, pl.BlockSpec((1, tile), lambda n, s: (0, block(n, s))), ANYWHERE],
            scratch_shapes=fetch_scratch(shard),
        ),
        cost_estimate=cost(1.8e10, 4e7),
        name="hidden_back",
    )(fetch_numbers(), grad, slope, shard, *sets)


def normalise(value):
    average = jnp.mean(value, axis=-1, keepdims=True)
    centred = value - average
    inv_std = lax.rsqrt(jnp.mean(centred * centred, axis=-1, keepdims=True) + EPS)
    return centred * inv_std, inv_std


def back_through_norm(grad, normed, inv_std, gain):
    scaled = grad * gain
    inner = (
        scaled
        - jnp.mean(scaled, axis=-1, keepdims=True)
        - normed * jnp.mean(scaled * normed, axis=-1, keepdims=True)
    )
    return inv_std * inner


def column_sum(value):
    return jnp.sum(value, axis=0, keepdims=True)


VECTORS = pl.BlockSpec((8, D), lambda i, *s: (0, 0))
GAIN_ONE, SHIFT_ONE, QUERY, VALUE, OUTPUT, GAIN_TWO, SHIFT_TWO, RETURN = [
    slice(i, i + 1) for i in range(8)
]


def rows_of(width, stacked=0):
    if stacked:
        return pl.BlockSpec((stacked, ROW_TILE, width), lambda i, *s: (0, i, 0))
    return pl.BlockSpec((ROW_TILE, width), lambda i, *s: (i, 0))


def whole(*shape):
    return pl.BlockSpec(shape, lambda i, *s: (0,) * len(shape))


def embed_kernel(tokens_ref, spread_ref, table_ref, vec_ref, stream_ref, first_ref):
    row = lax.broadcasted_iota(jnp.int32, stream_ref.shape, 0) + pl.program_id(0) * ROW_TILE
    tokens = jnp.where(row < ROWS, tokens_ref[...].astype(jnp.float32), 0.0)
    stream = tokens + dot_nn(spread_ref[...], table_ref[...])
    stream_ref[...] = stream
    normed, _ = normalise(stream)
    first_ref[...] = (normed * vec_ref[GAIN_ONE, :] + vec_ref[SHIFT_ONE, :]).astype(LOW)


def embed(tokens, spread, table, vectors):
    slots = spread.shape[1]
    return pl.pallas_call(
        embed_kernel,
        out_shape=[
            jax.ShapeDtypeStruct((PAD, D), jnp.float32),
            jax.ShapeDtypeStruct((PAD, D), LOW),
        ],
        grid=(PAD // ROW_TILE,),
        in_specs=[rows_of(D), rows_of(slots), whole(slots, D), VECTORS],
        out_specs=[rows_of(D), rows_of(D)],
        cost_estimate=cost(1e9, 1.5e7),
        name="embed",
    )(tokens, spread, table, vectors)


def project_kernel(shards, steps, s_ref, a_ref, b_ref, *refs):
    parts, (out_ref, full), (held, sem) = refs[:5], refs[5:7], refs[7:]
    finish = fetch(shards, s_ref, parts, held, full, sem, steps)
    query, value = b_ref[QUERY, :], b_ref[VALUE, :]
    bias = jnp.concatenate([query, jnp.zeros_like(query), value], axis=1)
    out_ref[...] = (dot_nn(a_ref[...], held[...]) + bias).astype(LOW)
    finish()


def project(first, vectors, shard, sets):
    width = shard.shape[1]
    steps = PAD // ROW_TILE
    return pl.pallas_call(
        partial(project_kernel, lax.axis_size("fsdp"), steps),
        out_shape=[jax.ShapeDtypeStruct((PAD, width), LOW), fetch_shape(shard)],
        grid_spec=pltpu.PrefetchScalarGridSpec(
            num_scalar_prefetch=1,
            grid=(steps,),
            in_specs=[rows_of(D), VECTORS] + [ANYWHERE] * 5,
            out_specs=[rows_of(width), ANYWHERE],
            scratch_shapes=fetch_scratch(shard),
        ),
        cost_estimate=cost(2 * PAD * D * width, 2e7),
        name="project",
    )(fetch_numbers(), first, vectors, shard, *sets)


def branch_kernel(shards, steps, s_ref, a_ref, stream_ref, vec_ref, *refs):
    parts, (mid_ref, second_ref, full), (held, sem) = refs[:5], refs[5:8], refs[8:]
    first = parts[0].shape[1] - D
    finish = fetch(shards, s_ref, parts, held, full, sem, steps, first)
    mid = stream_ref[...] + dot_nn(a_ref[...], held[...]) + vec_ref[OUTPUT, :]
    mid_ref[...] = mid
    normed, _ = normalise(mid)
    second_ref[...] = (normed * vec_ref[GAIN_TWO, :] + vec_ref[SHIFT_TWO, :]).astype(LOW)
    finish()


def branch(attended, stream, vectors, shard, sets):
    steps = PAD // ROW_TILE
    return pl.pallas_call(
        partial(branch_kernel, lax.axis_size("fsdp"), steps),
        out_shape=[
            jax.ShapeDtypeStruct((PAD, D), jnp.float32),
            jax.ShapeDtypeStruct((PAD, D), LOW),
            fetch_shape(shard, D),
        ],
        grid_spec=pltpu.PrefetchScalarGridSpec(
            num_scalar_prefetch=1,
            grid=(steps,),
            in_specs=[rows_of(D), rows_of(D), VECTORS] + [ANYWHERE] * 5,
            out_specs=[rows_of(D), rows_of(D), ANYWHERE],
            scratch_shapes=fetch_scratch(shard, D),
        ),
        cost_estimate=cost(2 * PAD * D * D, 3e7),
        name="branch",
    )(fetch_numbers(), attended, stream, vectors, shard, *sets)


def return_kernel(a_ref, w_ref, mid_ref, vec_ref, out_ref):
    value = mid_ref[...] + dot_nn(a_ref[...], w_ref[...]) + vec_ref[RETURN, :]
    out_ref[...] = value.astype(LOW)


def return_layer(activ, weight, mid, vectors):
    width = weight.shape[0]
    return pl.pallas_call(
        return_kernel,
        out_shape=jax.ShapeDtypeStruct((ROWS, D), LOW),
        grid=(PAD // ROW_TILE,),
        in_specs=[rows_of(width), whole(width, D), rows_of(D), VECTORS],
        out_specs=rows_of(D),
        cost_estimate=cost(2 * PAD * D * width, 3e7),
        name="return_layer",
    )(activ, weight, mid, vectors)


def second_back_kernel(
    h_ref, w_ref, o_ref, mid_ref, g_ref, gain_ref, out_ref, low_ref, att_ref, sums_ref
):
    @pl.when(pl.program_id(0) == 0)
    def _():
        sums_ref[...] = jnp.zeros_like(sums_ref)

    grad = dot_nt(h_ref[...], w_ref[...])
    normed, inv_std = normalise(mid_ref[...])
    out = g_ref[...].astype(jnp.float32)
    sums_ref[3:4, :] += column_sum(out)
    out = out + back_through_norm(grad, normed, inv_std, gain_ref[GAIN_TWO, :])
    out_ref[...] = out
    low = out.astype(LOW)
    low_ref[...] = low
    att_ref[...] = dot_nt(low, o_ref[...]).astype(LOW)
    sums_ref[0:1, :] += column_sum(low.astype(jnp.float32))
    sums_ref[1:2, :] += column_sum(grad * normed)
    sums_ref[2:3, :] += column_sum(grad)


def second_back(grad_hidden, weight, output, mid, grad, vectors):
    width = grad_hidden.shape[1]
    return pl.pallas_call(
        second_back_kernel,
        out_shape=[
            jax.ShapeDtypeStruct((PAD, D), jnp.float32),
            jax.ShapeDtypeStruct((PAD, D), LOW),
            jax.ShapeDtypeStruct((PAD, D), LOW),
            jax.ShapeDtypeStruct((8, D), jnp.float32),
        ],
        grid=(PAD // ROW_TILE,),
        in_specs=[
            rows_of(width),
            whole(D, width),
            whole(D, D),
            rows_of(D),
            rows_of(D),
            VECTORS,
        ],
        out_specs=[rows_of(D), rows_of(D), rows_of(D), whole(8, D)],
        cost_estimate=cost(2 * PAD * D * width, 4e7),
        name="second_back",
    )(grad_hidden, weight, output, mid, grad, vectors)


def first_back_kernel(s_ref, *refs):
    heads, w_refs, (stream_ref, mid_ref, spread_ref, gain_ref) = refs[:4], refs[4:16], refs[16:20]
    out_ref, table_ref, sums_ref = refs[20:]

    @pl.when(pl.program_id(0) == 0)
    def _():
        sums_ref[...] = jnp.zeros_like(sums_ref)
        table_ref[...] = jnp.zeros_like(table_ref)

    grad = 0.0
    for j, ref in enumerate(heads):
        for t in range(3):
            grad = grad + dot_nt(ref[t], w_refs[3 * j + t][...])
    normed, inv_std = normalise(stream_ref[...])
    out = mid_ref[...] + back_through_norm(grad, normed, inv_std, gain_ref[GAIN_ONE, :])
    low = out.astype(LOW)
    out_ref[...] = low
    rest = (out - low.astype(jnp.float32)).astype(LOW)
    table_ref[...] += dot_tn(spread_ref[...], low) + dot_tn(spread_ref[...], rest)
    sums_ref[0:1, :] += column_sum(grad * normed)
    sums_ref[1:2, :] += column_sum(grad)
    for j, ref in enumerate(heads):
        width = ref.shape[2]
        at = pl.ds(pl.multiple_of(s_ref[j] * width, width), width)
        sums_ref[2:3, at] += column_sum(ref[0].astype(jnp.float32))
        sums_ref[3:4, at] += column_sum(ref[2].astype(jnp.float32))


def first_back(quarters, heads, joined, stream, grad_mid, spread, vectors):
    width = D // 4
    w_specs = [
        pl.BlockSpec((D, width), lambda i, s, j=j, t=t: (0, 4 * t + s[j]))
        for j in range(4)
        for t in range(3)
    ]
    slots = spread.shape[1]
    return pl.pallas_call(
        first_back_kernel,
        out_shape=[
            jax.ShapeDtypeStruct((ROWS, D), LOW),
            jax.ShapeDtypeStruct((slots, D), jnp.float32),
            jax.ShapeDtypeStruct((8, D), jnp.float32),
        ],
        grid_spec=pltpu.PrefetchScalarGridSpec(
            num_scalar_prefetch=1,
            grid=(PAD // ROW_TILE,),
            in_specs=[rows_of(width, 3)] * 4
            + w_specs
            + [rows_of(D), rows_of(D), rows_of(slots), VECTORS],
            out_specs=[rows_of(D), whole(slots, D), whole(8, D)],
        ),
        cost_estimate=cost(2 * PAD * D * 3 * D, 4e7),
        name="first_back",
    )(quarters, *heads, *([joined] * 12), stream, grad_mid, spread, vectors)


def widen_kernel(moves, count, *refs):
    for source, at, target, block, to, width in moves:
        rows = refs[source].shape[2]
        down = slice(block * rows, (block + 1) * rows)
        for core in (0, 1):
            value = refs[source][0, core, :, at : at + width].astype(jnp.float32)
            refs[count + target][down, to[core] : to[core] + width] = value


def widen(sources, shapes, moves):
    rows = sources[0].shape[1]
    return pl.pallas_call(
        partial(widen_kernel, moves, len(sources)),
        out_shape=[jax.ShapeDtypeStruct((4 * n * rows, w), jnp.float32) for n, w in shapes],
        grid=(4,),
        in_specs=[
            pl.BlockSpec((1, 2, rows, v.shape[2]), lambda i: (i, 0, 0, 0)) for v in sources
        ],
        out_specs=[pl.BlockSpec((n * rows, w), lambda i: (i, 0)) for n, w in shapes],
        cost_estimate=cost(1, 6e6),
        name="widen",
    )(*[v.reshape(4, 2, rows, v.shape[2]) for v in sources])


def grad_value(f_ref, a_ref, b_ref):
    if len(b_ref.shape) == 2:
        return dot_tn(a_ref[...], b_ref[...]) * f_ref[0]
    return jnp.concatenate([dot_tn(a_ref[...], b_ref[i]) for i in range(3)], axis=1) * f_ref[0]


def grad_send_kernel(c_ref, f_ref, a_ref, b_ref, out_ref):
    out_ref[...] = grad_value(f_ref, a_ref, b_ref).astype(LOW)


def grad_keep_kernel(planes, c_ref, f_ref, a_ref, b_ref, got_ref, *refs):
    keep_ref, send_ref = refs[-2:]
    value = (grad_value(f_ref, a_ref, b_ref) + got_ref[...].astype(jnp.float32)).astype(LOW)
    core, place = c_ref[0], c_ref[1]
    rows = value.shape[0] // planes // 4
    for quarter in range(4):
        bits = place ^ quarter
        role = jnp.where(core == 0, bits, (bits >> 1) | ((bits & 1) << 1))
        for ref, near in ((keep_ref, 0), (send_ref, 1)):

            @pl.when(role % 2 == near)
            def _(ref=ref, quarter=quarter, role=role):
                for plane in range(planes):
                    at = (plane * 4 + quarter) * rows
                    ref[role // 2, plane] = value[at : at + rows]


def grad_half(
    numbers, factor, left, right, got=None, tile_m=1024, tile_n=512, width=None, first=0, into=()
):
    rows = left.shape[1]
    shards = lax.axis_size("fsdp")
    stacked = right.ndim == 3
    cols = 3 * right.shape[2] if stacked else right.shape[1] // 2
    tile_n = cols if stacked else tile_n
    steps = cols // tile_n
    in_specs = [
        pl.BlockSpec(memory_space=pltpu.SMEM),
        pl.BlockSpec((PAD, tile_m), lambda m, n, c: (0, m)),
    ]
    if stacked:
        in_specs.append(pl.BlockSpec((3, PAD, cols // 3), lambda m, n, c: (0, 0, 0)))
    else:
        in_specs.append(pl.BlockSpec((PAD, tile_n), lambda m, n, c: (0, n + c[0] * steps)))
    flat_spec = pl.BlockSpec((tile_m, tile_n), lambda m, n, c: (m, n))
    operands = [numbers, factor, left, right]
    if got is None:
        kernel, name = grad_send_kernel, "grad_send"
        out_shape, out_specs = jax.ShapeDtypeStruct((rows, cols), LOW), flat_spec
    else:
        planes = tile_m * shards // rows
        part = rows // shards // 4
        kernel, name = partial(grad_keep_kernel, planes), "grad_keep"
        in_specs.append(flat_spec)
        operands.append(got)
        out_shape = [jax.ShapeDtypeStruct((2, shards, part, width or cols), LOW)] * 2
        out_specs = [
            pl.BlockSpec((2, planes, part, tile_n), lambda m, n, c: (0, m, 0, n + first // tile_n))
        ] * 2
        in_specs += [ANYWHERE] * len(into)
        operands += into
    return pl.pallas_call(
        kernel,
        out_shape=out_shape,
        grid_spec=pltpu.PrefetchScalarGridSpec(
            num_scalar_prefetch=1,
            grid=(rows // tile_m, steps),
            in_specs=in_specs,
            out_specs=out_specs,
        ),
        input_output_aliases={5 + i: i for i in range(len(into))},
        cost_estimate=cost(2 * PAD * rows * cols, 1e7),
        name=name,
    )(*operands)


def swap(value, even, odd):
    size = lax.axis_size("dp")
    return lax.ppermute(value, "dp", [(i, i ^ (odd if i % 2 else even)) for i in range(size)])


def swap_core(value):
    return swap(value, 1, 1)


def swap_first(value):
    return swap(value, 2, 4)


def swap_second(value):
    return swap(value, 4, 2)


def own_piece(shard):
    part = shard.shape[0] // GROUP
    place = lax.axis_index("dp") % GROUP
    return lax.dynamic_slice_in_dim(shard, place * part, part, 0)


def from_above(piece):
    shards = lax.axis_size("fsdp")
    return [
        lax.ppermute(piece, "fsdp", [((i + k) % shards, i) for i in range(shards)])
        for k in range(1, shards)
    ]


def gather_z_native(piece):
    return lax.all_gather(piece, "fsdp", axis=0, tiled=False)


def others(every):
    shards = every.shape[0]
    twice = jnp.concatenate([every, every[:-1]], axis=0)
    return lax.dynamic_slice_in_dim(twice, lax.axis_index("fsdp") + 1, shards - 1, 0)


def gather_first(own):
    return own, swap_first(own)


def gather_second(own, got):
    both = jnp.stack([own, got])
    return both, swap_second(both)


def gather_core(both, far):
    return both, far, swap_core(both), swap_core(far)


def fetch_copies(shards, s_ref, refs, held, sem, first=0, at_col=0, cols=None):
    own, sets = refs[0], refs[1:]
    place, row = s_ref[0], s_ref[1]
    rows = own.shape[0]
    cols = cols or own.shape[1]
    part = rows // GROUP
    source_cols, held_cols = pl.ds(first, cols), pl.ds(at_col, cols)
    copies = [
        pltpu.make_async_copy(
            own.at[:, source_cols],
            held.at[pl.ds(pl.multiple_of(row * rows, rows), rows), held_cols],
            sem.at[0],
        )
    ]
    for flip in range(2):
        base = place ^ flip
        first_bits = jnp.where(base % 2 == 0, 2, 4)
        for source, bits in (
            (sets[2 * flip].at[0], 0),
            (sets[2 * flip].at[1], first_bits),
            (sets[2 * flip + 1].at[0], 6 - first_bits),
            (sets[2 * flip + 1].at[1], 6),
        ):
            for k in range(1, shards):
                at = lax.rem(row + k, shards) * rows + (base ^ bits) * part
                target = held.at[pl.ds(pl.multiple_of(at, part), part), held_cols]
                copies.append(
                    pltpu.make_async_copy(
                        source.at[k - 1, :, source_cols], target, sem.at[len(copies)]
                    )
                )
    return copies


def start_wait(copies, start=True, wait=True):
    for copy in copies if start else ():
        copy.start()
    for copy in copies if wait else ():
        copy.wait()


def fetch(shards, s_ref, refs, held, full, sem, steps, first=0):
    def keep():
        return pltpu.make_async_copy(held, full, sem.at[0])

    @pl.when(pl.program_id(0) == 0)
    def _():
        start_wait(fetch_copies(shards, s_ref, refs, held, sem, first, 0, held.shape[1]))
        keep().start()

    def finish():
        @pl.when(pl.program_id(0) == steps - 1)
        def _():
            keep().wait()

    return finish


def fetch_numbers():
    place = lax.axis_index("dp") % GROUP
    return jnp.stack([place, lax.axis_index("fsdp")]).astype(jnp.int32)


def fetch_scratch(shard, cols=None, sets=1):
    shards = lax.axis_size("fsdp")
    count = 1 + 8 * (shards - 1)
    return [
        pltpu.VMEM((shards * shard.shape[0], cols or shard.shape[1]), shard.dtype),
        pltpu.SemaphoreType.DMA((count,) if sets == 1 else (sets, count)),
    ]


def fetch_shape(shard, cols=None):
    shards = lax.axis_size("fsdp")
    return jax.ShapeDtypeStruct((shards * shard.shape[0], cols or shard.shape[1]), shard.dtype)


def plane_gather(value, axis):
    size = lax.axis_size("dp")
    groups = None
    if size > GROUP:
        groups = [[g * GROUP + i for i in range(GROUP)] for g in range(size // GROUP)]
    return lax.all_gather(value, "dp", axis=axis, tiled=False, axis_index_groups=groups)


def rest_sum(value):
    size = lax.axis_size("dp")
    if size == GROUP:
        return value
    groups = [[g * GROUP + i for g in range(size // GROUP)] for i in range(GROUP)]
    return lax.psum(value, "dp", axis_index_groups=groups)


def add_low(left, right):
    return (left.astype(jnp.float32) + right.astype(jnp.float32)).astype(LOW)


def sum_first(got, keep):
    return add_low(keep[0], got[0]), swap_second(add_low(keep[1], got[1]))


def sum_z(both):
    shards, part, cols = both.shape
    piece = lax.psum_scatter(
        both.reshape(shards * part, cols), "fsdp", scatter_dimension=0, tiled=True
    )
    return rest_sum(piece)


def sum_z_direct(value):
    shards = lax.axis_size("fsdp")
    me = lax.axis_index("fsdp")
    total = lax.dynamic_index_in_dim(value, me, 0, keepdims=False).astype(jnp.float32)
    for step in range(1, shards):
        send = lax.dynamic_index_in_dim(value, (me + step) % shards, 0, keepdims=False)
        got = lax.ppermute(send, "fsdp", [(i, (i + step) % shards) for i in range(shards)])
        total = total + got.astype(jnp.float32)
    return total


def pack_kernel(s_ref, piece_ref, *refs):
    out_ref, rows_ref = refs[-2:]
    width, first = rows_ref.shape[1], piece_ref.shape[1]
    out_ref[:, :first] = piece_ref[...]
    rows_ref[...] = jnp.zeros_like(rows_ref)
    row = 0
    for ref in refs[:-2]:
        if len(ref.shape) == 2:
            rows_ref[row : row + ref.shape[0], :] = ref[...]
            row += ref.shape[0]
            continue
        for i in range(0, ref.shape[0], width):
            rows_ref[row : row + 1, :] = ref[i : i + width].reshape(1, width)
            row += 1
    tall = out_ref.shape[0]
    for i in range(rows_ref.shape[0] // tall):
        at = first + i * width
        out_ref[:, at : at + width] = rows_ref[i * tall : (i + 1) * tall, :]


def pack(shard, vectors, table):
    rows, cols = shard.shape
    tall, width = rows // GROUP, vectors[0].shape[0]
    wide = cols + 64 // tall * width
    place = (lax.axis_index("dp") % GROUP).astype(jnp.int32).reshape(1)
    return pl.pallas_call(
        pack_kernel,
        out_shape=jax.ShapeDtypeStruct((tall, wide), LOW),
        grid_spec=pltpu.PrefetchScalarGridSpec(
            num_scalar_prefetch=1,
            grid=(1,),
            in_specs=[pl.BlockSpec((tall, cols), lambda i, s: (s[0], 0))]
            + [pl.BlockSpec(v.shape, lambda i, s: (0,)) for v in vectors]
            + [pl.BlockSpec(table.shape, lambda i, s: (0, 0))],
            out_specs=pl.BlockSpec((tall, wide), lambda i, s: (0, 0)),
            scratch_shapes=[pltpu.VMEM((64, width), LOW)],
        ),
        cost_estimate=cost(1, 1e5),
        name="pack",
    )(place, shard, *vectors, table)


def unpack_kernel(s_ref, *refs):
    parts, (out_ref, table_ref, rows_ref) = refs[:-3], refs[-3:]
    width = rows_ref.shape[1]
    tall = parts[0].shape[0]
    table_ref[...] = jnp.zeros_like(table_ref)
    for k, ref in enumerate(parts):
        at = lax.rem(s_ref[0] + k, len(parts)) * width
        at = pl.ds(pl.multiple_of(at, width), width)
        for i in range(64 // tall):
            rows_ref[i * tall : (i + 1) * tall, :] = ref[:, i * width : (i + 1) * width]
        out_ref[:, at] = rows_ref[...].astype(jnp.float32)
        table = rows_ref[12 : 12 + SMALL_LEN, :]
        table_ref[0:SMALL_LEN, at] = table
        table_ref[64 : 64 + SMALL_LEN, at] = table


def unpack(parts, first, width):
    shards = len(parts)
    tall = parts[0].shape[0]
    wide = parts[0].shape[1] - first
    return pl.pallas_call(
        unpack_kernel,
        out_shape=[
            jax.ShapeDtypeStruct((64, shards * width), jnp.float32),
            jax.ShapeDtypeStruct((128, shards * width), LOW),
        ],
        grid=(1,),
        in_specs=[pl.BlockSpec(memory_space=pltpu.SMEM)]
        + [pl.BlockSpec((tall, wide), lambda i: (0, first // wide))] * shards,
        out_specs=[
            pl.BlockSpec((64, shards * width), lambda i: (0, 0)),
            pl.BlockSpec((128, shards * width), lambda i: (0, 0)),
        ],
        scratch_shapes=[pltpu.VMEM((64, width), LOW)],
        cost_estimate=cost(1, 1e6),
        name="unpack",
    )(lax.axis_index("fsdp").astype(jnp.int32).reshape(1), *parts)


def per_device(
    tokens,
    output_grad,
    group_member,
    image_counts,
    position_source,
    position_table,
    first_gain,
    first_shift,
    input_proj,
    query_bias,
    value_bias,
    output_proj,
    output_bias,
    second_gain,
    second_shift,
    hidden_weight,
    hidden_bias,
    return_weight,
    return_bias,
):
    dp_size = lax.axis_size("dp")
    fsdp_size = lax.axis_size("fsdp")
    core = (lax.axis_index("dp") & 1).astype(jnp.int32)
    quarter = ((lax.axis_index("dp") % GROUP) >> 1).astype(jnp.int32)
    mine, other = jnp.stack([core, quarter]), jnp.stack([1 - core, quarter])
    vectors = (
        first_gain,
        first_shift,
        query_bias,
        value_bias,
        output_bias,
        second_gain,
        second_shift,
        return_bias,
        hidden_bias,
    )
    packed_own = pack(input_proj, vectors, position_table)
    parts = from_above(packed_own)
    hidden_shard = jnp.concatenate([hidden_weight, output_proj], axis=1)
    hidden_own = own_piece(hidden_weight)
    output_own = own_piece(output_proj)
    return_z = own_piece(return_weight)
    member = group_member[0]
    is_large = member == 1
    length = jnp.where(is_large, LARGE_LEN, SMALL_LEN)
    step = jnp.where(is_large, LARGE_LEN, 3 * SMALL_LEN)
    group_high = dp_size * 7 // 16
    group_low = dp_size - group_high
    counts = image_counts.astype(jnp.float32)
    share = jnp.where(is_large, counts[1], counts[0]) / (counts[0] + counts[1])
    images = jnp.where(
        is_large,
        group_high * fsdp_size * (ROWS // LARGE_LEN),
        group_low * fsdp_size * (ROWS // SMALL_LEN),
    ).astype(jnp.float32)
    factor = share / images
    scale = factor.reshape(1)

    row_index = jnp.arange(PAD, dtype=jnp.int32)
    place = jnp.where(row_index < ROWS, row_index % length, -1)
    inter = interp_table(position_source)
    identity = (
        jnp.arange(LARGE_LEN, dtype=jnp.int32)[:, None]
        == jnp.arange(SMALL_LEN, dtype=jnp.int32)[None, :]
    ).astype(jnp.float32)
    mixing = jnp.where(is_large, inter, identity)
    picker = (place[:, None] == jnp.arange(LARGE_LEN, dtype=jnp.int32)[None, :]).astype(jnp.float32)
    spread = jnp.dot(picker, mixing, precision=lax.Precision.HIGHEST)
    lengths = jnp.stack([length, step])
    upper = spread.astype(LOW)
    lower = (spread - upper.astype(jnp.float32)).astype(LOW)
    spread_low = jnp.concatenate(
        [jnp.pad(v, ((0, 0), (0, 64 - SMALL_LEN))) for v in (upper, lower)], axis=1
    )

    quarters = jnp.stack([2 * core, 2 - 2 * core, 2 * core + 1, 3 - 2 * core])
    numbers_one = jnp.concatenate([lengths, quarters[:2]])
    numbers_two = jnp.concatenate([lengths, quarters[2:]])
    spread_low, scale, mine, other, lengths, numbers_one, numbers_two, hidden_own, *parts = sync(
        spread_low, scale, mine, other, lengths, numbers_one, numbers_two, hidden_own, *parts
    )
    joint_z = jnp.stack([v[:, : 3 * D] for v in parts])
    smalls, table_pair = unpack([packed_own] + parts, 3 * D, first_gain.shape[0])
    hidden_add = smalls[8:12].reshape(4, fsdp_size, -1).transpose(1, 0, 2).reshape(-1)
    joint_one = gather_first(joint_z)
    hidden_z = gather_z_native(after(hidden_own, joint_z))
    output_z = from_above(after(output_own, joint_z))
    stream, first_low = embed(tokens, spread_low, table_pair, smalls)
    first_low, *joint_one = sync(first_low, *joint_one)
    joint_two = gather_second(*joint_one)
    output_grad, lengths, _ = sync(output_grad, lengths, joint_two[0])
    masks = image_masks(lengths)
    grad_pad = jnp.pad(output_grad, ((0, PAD - ROWS), (0, 0)))
    output_z = jnp.stack(output_z)
    *joint_two, hidden_z, output_z, hidden_add, return_z, grad_pad, masks = sync(
        *joint_two, hidden_z, output_z, hidden_add, return_z, grad_pad, masks
    )
    joint_sets = gather_core(*joint_two)
    first_low, *joint_sets = sync(first_low, *joint_sets)
    hidden_one = gather_first(jnp.concatenate([others(hidden_z), output_z], axis=-1))
    return_early, *return_late = from_above(return_z)
    projected, joint_full = project(
        after(first_low, hidden_one[0]), smalls, input_proj, joint_sets
    )
    projected, return_early, *hidden_one = sync(projected, return_early, *hidden_one)
    hidden_two = gather_second(*hidden_one)
    projected = after(projected, hidden_two[0])
    attended = attend_forward(lengths, masks, projected)
    attended, *rest = sync(attended, *hidden_two, *return_late)
    hidden_two, return_late = rest[:2], rest[2:]
    hidden_sets = gather_core(*hidden_two)
    return_one = gather_first(jnp.stack([return_early, *return_late]))
    attended, *hidden_sets = sync(attended, *hidden_sets)
    mid, second, outproj_full = branch(
        after(attended, return_one[0]),
        stream,
        smalls,
        hidden_shard,
        hidden_sets,
    )
    second, *return_one = sync(second, *return_one)
    return_two = gather_second(*return_one)
    activ, slope, hidden_full = hidden_layer(
        after(second, return_two[0]), hidden_add, hidden_shard, hidden_sets
    )
    activ, slope, *return_two = sync(activ, slope, *return_two)
    return_sets = gather_core(*return_two)
    return_send = grad_half(other, scale, activ, grad_pad)
    return_send, *return_sets = sync(return_send, *return_sets)
    return_got = swap_core(return_send)
    grad_hidden, grad_hidden_add, return_full = hidden_back(
        after(grad_pad, return_send), slope, return_weight, return_sets
    )
    grad_hidden, return_got = sync(grad_hidden, return_got)
    return_keep, return_out = grad_half(mine, scale, activ, grad_pad, return_got)
    return_in = swap_first(return_out)
    hidden_send = grad_half(other, scale, after(second, return_out), grad_hidden)
    hidden_got = swap_core(hidden_send)
    grad_mid, grad_branch, grad_att, sums_two = second_back(
        after(grad_hidden, hidden_send), hidden_full, outproj_full, mid, grad_pad, smalls
    )
    grad_branch, hidden_got, return_in = sync(grad_branch, hidden_got, return_in)
    return_kept, return_in = sum_first(return_in, return_keep)
    hidden_keep, hidden_out = grad_half(
        mine, scale, after(second, return_kept), grad_hidden, hidden_got
    )
    hidden_out, grad_branch, return_in = sync(hidden_out, grad_branch, return_in)
    hidden_in = swap_first(hidden_out)
    output_send = grad_half(other, scale, attended, grad_branch)
    output_got = swap_core(output_send)
    return_piece = sum_z(add_low(return_kept, return_in))
    mine_one, other_one = attend_backward(
        numbers_one, masks, projected, after(grad_att, output_send)
    )
    mine_one, other_one, output_got, hidden_in, return_piece = sync(
        mine_one, other_one, output_got, hidden_in, return_piece
    )
    hidden_kept, hidden_in = sum_first(hidden_in, hidden_keep)
    joint_send = grad_half(other, scale, after(first_low, hidden_kept), other_one, tile_m=512)
    joint_got = swap_core(joint_send)
    wide = dict(width=5 * D // 4)
    output_pair = grad_half(
        mine,
        scale,
        attended,
        after(grad_branch, joint_send),
        output_got,
        tile_n=256,
        first=3 * D // 4,
        **wide,
    )
    *output_pair, joint_got = sync(*output_pair, joint_got)
    joint_keep, joint_out = grad_half(
        mine, scale, first_low, mine_one, joint_got, tile_m=512, into=output_pair, **wide
    )
    joint_out, hidden_in = sync(joint_out, hidden_in)
    joint_in = swap_first(joint_out)
    hidden_piece = sum_z(add_low(hidden_kept, hidden_in))
    mine_two, other_two = attend_backward(
        numbers_two, masks, projected, after(grad_att, joint_out)
    )
    mine_two, other_two, joint_in, hidden_piece = sync(mine_two, other_two, joint_in, hidden_piece)
    joint_kept, joint_in = sum_first(joint_in, joint_keep)
    last_send = grad_half(other, scale, after(first_low, joint_kept), other_two, tile_m=512)
    last_got = swap_core(last_send)
    last_keep, last_out = grad_half(mine, scale, first_low, mine_two, last_got, tile_m=512)
    last_out, joint_in = sync(last_out, joint_in)
    joint_piece = sum_z(add_low(joint_kept, joint_in))
    last_in = swap_first(last_out)
    heads = sync(mine_one, other_one, mine_two, other_two, last_out)[:4]
    tokens_grad, grad_table, sums_one = first_back(
        quarters, heads, joint_full, stream, grad_mid, spread_low, smalls
    )
    tokens_grad, grad_table, sums_one, last_in, joint_piece = sync(
        tokens_grad, grad_table, sums_one, last_in, joint_piece
    )
    last_kept, last_in = sum_first(last_in, last_keep)
    rows = joint_piece.shape[0]
    blocks = return_piece.shape[0] // rows
    pieces = [return_piece[i * rows : (i + 1) * rows] for i in range(blocks)]
    pieces += [hidden_piece, joint_piece]
    return_cols, hidden_cols = blocks * return_piece.shape[1], hidden_piece.shape[1]
    every = plane_gather(jnp.concatenate(pieces, axis=1), axis=0)

    grad_table = grad_table[:SMALL_LEN] + grad_table[64 : 64 + SMALL_LEN]
    hidden_rows = grad_hidden_add.reshape(fsdp_size, 4, -1).transpose(1, 0, 2).reshape(4, D)
    packed = jnp.concatenate([sums_one[:4], sums_two[:4], hidden_rows, grad_table], axis=0) * scale[0]
    packed = jnp.pad(packed, ((0, smalls.shape[0] - packed.shape[0]), (0, 0))).astype(LOW)
    packed = packed.reshape(packed.shape[0], fsdp_size, -1).transpose(1, 0, 2)
    packed, last_in = sync(packed, last_in)
    last_both = add_low(last_kept, last_in)
    last_cols = last_both.shape[-1]
    packed = packed.reshape(fsdp_size, rows, -1)
    last_both = jnp.concatenate([last_both, packed], axis=-1)
    last_piece = sum_z_direct(last_both).astype(LOW)
    block_out = return_layer(after(activ, last_both), return_full, mid, smalls)
    block_out, last_piece = sync(block_out, last_piece)
    small_rows = 12 + SMALL_LEN
    wide = first_gain.shape[0]
    small_piece = last_piece[:, last_cols:].reshape(-1, wide)[:small_rows].reshape(rows, -1)
    last_piece = jnp.concatenate([last_piece[:, :last_cols], small_piece], axis=1)
    last_every = plane_gather(rest_sum(last_piece), axis=0)
    summed = jnp.sum(last_every[:, :, last_cols:].astype(jnp.float32), axis=0)
    summed = summed.reshape(small_rows, -1)
    half, part = D // 2, D // 4
    moves = [(0, i * half, 0, i, (0, half), half) for i in range(blocks)]
    moves.append((0, return_cols, 1, 0, (0, 2 * D), 2 * D))
    for t in range(3):
        to = (t * D, t * D + half)
        moves.append((0, return_cols + hidden_cols + t * part, 2, 0, to, part))
        moves.append((1, t * part, 2, 0, (to[0] + part, to[1] + part), part))
    moves.append((0, return_cols + hidden_cols + 3 * part, 3, 0, (0, half), half))
    return_w_out, hidden_w_out, joint_out, outproj_out = widen(
        [every, last_every], [(blocks, D), (1, 4 * D), (1, 3 * D), (1, D)], moves
    )
    return (
        block_out,
        tokens_grad,
        summed[12 : 12 + SMALL_LEN],
        summed[0],
        summed[1],
        joint_out,
        summed[2],
        summed[3],
        outproj_out,
        summed[4],
        summed[5],
        summed[6],
        hidden_w_out,
        summed[8:12].reshape(-1),
        return_w_out,
        summed[7],
    )


def solution(mesh):
    in_specs = (
        P(("dp", "fsdp"), None),
        P(("dp", "fsdp"), None),
        P("dp"),
        P(),
        P(),
        P(None, "fsdp"),
        P("fsdp"),
        P("fsdp"),
        P("fsdp", None),
        P("fsdp"),
        P("fsdp"),
        P("fsdp", None),
        P("fsdp"),
        P("fsdp"),
        P("fsdp"),
        P("fsdp", None),
        P("fsdp"),
        P("fsdp", None),
        P("fsdp"),
    )
    out_specs = (
        P(("dp", "fsdp"), None),
        P(("dp", "fsdp"), None),
        P(None, "fsdp"),
        P("fsdp"),
        P("fsdp"),
        P("fsdp", None),
        P("fsdp"),
        P("fsdp"),
        P("fsdp", None),
        P("fsdp"),
        P("fsdp"),
        P("fsdp"),
        P("fsdp", None),
        P("fsdp"),
        P("fsdp", None),
        P("fsdp"),
    )
    return jax.shard_map(
        per_device, mesh=mesh, in_specs=in_specs, out_specs=out_specs, check_vma=False
    )
```

time: 547 us -> 475 us (0.87)
  local copies, waits for them, and re-layouts: 45.1 us -> 17.8 us
  waiting for transfers between devices: 58.9 us -> 33.4 us
  blocking collectives: 20.4 us -> 13.2 us
    ppermute x25, waiting for transfers between devices: 31.7 us -> 14.2 us  [swap(): lax.ppermute(value, 'dp', [(i, i ^ (odd if i % 2 else even)) for i in ran...]
    pallas_call x2 -> x6, Pallas kernels: 51.2 us -> 64.5 us  [the longest x1 29.3 us: hidden_layer(): pl.pallas_call(partial(hidden_kernel, lax.axis_size('fsdp'), steps, 736),...]
    reshape x15 -> x5, local copies, waits for them, and re-layouts: 9.94 us -> 0.29 us  [the longest x1 0.14 us: per_device(): last_piece[:, last_cols:].reshape(-1, wide)[:small_rows].reshape(rows, -1)]
    all_gather x1 -> x0, blocking collectives: 9.58 us -> none  [small_sum(): every = lax.all_gather(value.astype(LOW), 'dp', axis=0, tiled=False)]
    unnamed x107 -> x56, local copies, waits for them, and re-layouts: 15.2 us -> 6.04 us
    ppermute x6 -> x9, starting transfers between devices: 10 us -> 17.4 us  [from_above(): lax.ppermute(piece, 'fsdp', [((i + k) % shards, i) for i in range(shards)])]
    all_gather x2 -> x1, waiting for transfers between devices: 14.2 us -> 7.08 us  [gather_z_native(): return lax.all_gather(piece, 'fsdp', axis=0, tiled=False)]
    pallas_call x3 -> x1, Pallas kernels: 12.5 us -> 7.75 us  [widen(): pl.pallas_call(partial(widen_kernel, moves, len(sources)), out_shape=[jax...]
  transfers between devices with their start and end apart: 45 -> 42, of which waited for: 12 -> 14; matrix products, arithmetic and copies ran while one was open for 12% -> 5% of each run, Pallas kernels for 53% -> 58%
where the time goes in v4:
time: 475 us; the launch traced here: 468 us
  Pallas kernels  318 us (67%)
  starting transfers between devices  42.8 us (9%)
  waiting for transfers between devices  33.4 us (7%)
  other arithmetic  23.7 us (5%)
  between operations  18.1 us (4%)
  local copies, waits for them, and re-layouts  17.8 us (4%)
  blocking collectives  13.2 us (3%)
    pallas_call x10, Pallas kernels, grad_half(): pl.pallas_call(kernel, out_shape=out_shape, grid_spec=pltpu.PrefetchScala...  88.2 us
    pallas_call x2, Pallas kernels, attend_backward(): pl.pallas_call(backward_kernel, out_shape=[jax.ShapeDtypeStruct((3, PAD,...  40.3 us
    pallas_call x1, Pallas kernels, hidden_layer(): pl.pallas_call(partial(hidden_kernel, lax.axis_size('fsdp'), steps, 736),...  29.3 us
    pallas_call x1, Pallas kernels, second_back(): pl.pallas_call(second_back_kernel, out_shape=[jax.ShapeDtypeStruct((PAD,...  26.2 us
    pallas_call x1, Pallas kernels, first_back(): pl.pallas_call(first_back_kernel, out_shape=[jax.ShapeDtypeStruct((ROWS,...  23 us
    pallas_call x1, Pallas kernels, hidden_back(): pl.pallas_call(partial(hidden_back_kernel, shards, steps, 368), out_shape...  22.6 us
    ppermute x25, starting transfers between devices, swap(): lax.ppermute(value, 'dp', [(i, i ^ (odd if i % 2 else even)) for i in ran...  21.3 us
    pallas_call x1, Pallas kernels, attend_forward(): pl.pallas_call(forward_kernel, out_shape=jax.ShapeDtypeStruct((PAD, D), L...  20.1 us
  transfers between devices with their start and end apart: 42, of which 14 were waited for; matrix products, arithmetic and copies ran while one was open for 5% of the time, Pallas kernels for 58%

profile of v4, /device:TPU:0, one launch (start us, length us, event | category | flops | bytes accessed | tf_op | source)
XLA Modules:
  0.0 467.5 jit_solution(4499533420469029266)
XLA Ops:
  9.0 3.0 collective-permute-start.2
  33.3 6.4 %embed.1 = (f32[1472,1024]{1,0:T(8,128)}, bf16[1472,1024]{1,0:T(8,128)(2,1)}) custom-call(bf16[1450,1024]{1,0:T(8,128)(2,1)} %tokens_ref.1, bf16[1472,128]{1,0:T(8,128)(2,1)} %fusion.14.spread_ref.refs_18_, bf16[128,1024]{1,0:T(8,128)(2,1)} %get-tuple-element.169.table_ref, f32[64,1024]{1,0:T(8,128)} %get-tuple-element.170.vec_ref.b_ref.gain_ref.refs_19_), custom_call_target="tpu_custom_call" | custom-call | flops 1000000000 | bytes 15000000 | tf_op jit(solution)/shard_map/embed/pallas_call | solution.py:427
  43.4 5.4 %collective-permute-start.7 = (bf16[32,1024]{1,0:T(8,128)(2,1)S(1)}, bf16[32,1024]{1,0:T(8,128)(2,1)S(1)}, u32[]{:S(2)}, u32[]{:S(2)}) collective-permute-start(bf16[32,1024]{1,0:T(8,128)(2,1)S(1)} %constant_dynamic-slice_fusion.1), channel_id=1, source_target_pairs={{3,0},{0,1},{1,2},{2,3},{7,4},{4,5},{5,6},{6,7},{11,8},{8,9},{9,10... | collective-permute-start | bytes 196616 | tf_op jit(solution)/shard_map/ppermute | solution.py:746
  54.1 4.6 collective-permute-done.6
  58.7 2.8 image_masks.1.mask_ref
  63.5 7.1 %all-gather.6.cloned.1.call-done = bf16[128,4096]{1,0:T(8,128)(2,1)} async-done(((bf16[32,4096]{1,0:T(8,128)(2,1)}), bf16[128,4096]{1,0:T(8,128)(2,1)}) %all-gather.6.cloned.1.call-update) | async-done | bytes 1048592 | tf_op jit(solution)/shard_map/all_gather | solution.py:752
  75.5 16.3 %project.1 = (bf16[1472,3072]{1,0:T(8,128)(2,1)}, bf16[1024,3072]{1,0:T(8,128)(2,1)}) custom-call(s32[2]{0:T(128)} %get-tuple-element.337.s_ref, bf16[1472,1024]{1,0:T(8,128)(2,1)} %get-tuple-element.278.a_ref, f32[64,1024]{1,0:T(8,128)} %get-tuple-element.170.vec_ref.b_ref.gain_ref.refs_19_, bf16[256,3072]{1,0:T(8,128)(2,1)} %refs_0_.4, ...), custom_call_target="tpu_custom_call" | custom-call | flops 9261023232 | bytes 20000000 | tf_op jit(solution)/shard_map/project/pallas_call | solution.py:453
  96.6 20.1 %attend_forward.1.a_ref = bf16[1472,1024]{1,0:T(8,128)(2,1)} custom-call(s32[2]{0:T(128)} %get-tuple-element.174.s_ref, f32[10,176,352]{2,1,0:T(8,128)} %image_masks.1.mask_ref, bf16[1472,3072]{1,0:T(8,128)(2,1)} %get-tuple-element.196.q_ref.k_ref.v_ref.refs_0_.refs_1_.refs_2_.refs_3_.refs_4_.refs_5_, ...), custom_call_target="tpu_custom_call" | custom-call | flops 20000000000 | bytes 10000000 | tf_op jit(solution)/shard_map/attend_forward/pallas_call | solution.py:213
  125.4 12.4 %branch.1 = (f32[1472,1024]{1,0:T(8,128)}, bf16[1472,1024]{1,0:T(8,128)(2,1)}, bf16[1024,1024]{1,0:T(8,128)(2,1)}) custom-call(s32[2]{0:T(128)} %get-tuple-element.337.s_ref, bf16[1472,1024]{1,0:T(8,128)(2,1)} %attend_forward.1.a_ref, f32[1472,1024]{1,0:T(8,128)} %get-tuple-element.205.stream_ref.refs_16_, ...), custom_call_target="tpu_custom_call" | custom-call | flops 3087007744 | bytes 30000000 | tf_op jit(solution)/shard_map/branch/pallas_call | solution.py:481
  140.6 29.3 %hidden_layer.1 = (bf16[1472,4096]{1,0:T(8,128)(2,1)}, bf16[1472,4096]{1,0:T(8,128)(2,1)}, bf16[1024,4096]{1,0:T(8,128)(2,1)}) custom-call(s32[2]{0:T(128)} %get-tuple-element.337.s_ref, bf16[1472,1024]{1,0:T(8,128)(2,1)} %get-tuple-element.247.x_ref.a_ref, f32[1,4096]{1,0:T(1,128)} %bitcast.125, bf16[256,5120]{1,0:T(8,128)(2,1)} %copy-done, ...), custom_call_target="tpu_custom_call" | custom-call | flops 24000000000 | bytes 40000000 | tf_op jit(solution)/shard_map/hidden_layer/pallas_call | solution.py:288
  170.5 11.8 %grad_send.5 = bf16[4096,512]{1,0:T(8,128)(2,1)} custom-call(s32[2]{0:T(128)} %get-tuple-element.223.c_ref, f32[1]{0:T(128)} %bitcast.5.f_ref, bf16[1472,4096]{1,0:T(8,128)(2,1)} %get-tuple-element.300.a_ref, bf16[1472,1024]{1,0:T(8,128)(2,1)} %pad.18.b_ref.g_ref), custom_call_target="tpu_custom_call" | custom-call | flops 6174015488 | bytes 10000000 | tf_op jit(solution)/shard_map/grad_send/pallas_call | solution.py:705
  182.4 22.6 %hidden_back.1 = (bf16[1472,4096]{1,0:T(8,128)(2,1)}, f32[1,4096]{1,0:T(1,128)}, bf16[4096,1024]{1,0:T(8,128)(2,1)}) custom-call(s32[2]{0:T(128)} %get-tuple-element.337.s_ref, bf16[1472,1024]{1,0:T(8,128)(2,1)} %pad.18.b_ref.g_ref, bf16[1472,4096]{1,0:T(8,128)(2,1)} %get-tuple-element.228.slope_ref, bf16[1024,1024]{1,0:T(8,128)(2,1)} %refs_0_.5, ...), custom_call_target="tpu_custom_call" | custom-call | flops 17999998976 | bytes 40000000 | tf_op jit(solution)/shard_map/hidden_back/pallas_call | solution.py:360
  205.1 12.9 %grad_keep.5 = (bf16[2,4,256,512]{3,2,1,0:T(8,128)(2,1)}, bf16[2,4,256,512]{3,2,1,0:T(8,128)(2,1)}) custom-call(s32[2]{0:T(128)} %get-tuple-element.219.c_ref, f32[1]{0:T(128)} %bitcast.5.f_ref, bf16[1472,4096]{1,0:T(8,128)(2,1)} %get-tuple-element.300.a_ref, bf16[1472,1024]{1,0:T(8,128)(2,1)} %pad.18.b_ref.g_ref, ...), custom_call_target="tpu_custom_call" | custom-call | flops 6174015488 | bytes 10000000 | tf_op jit(solution)/shard_map/grad_keep/pallas_call | solution.py:705
  218.0 11.5 %grad_send.6 = bf16[1024,2048]{1,0:T(8,128)(2,1)} custom-call(s32[2]{0:T(128)} %get-tuple-element.223.c_ref, f32[1]{0:T(128)} %bitcast.5.f_ref, bf16[1472,1024]{1,0:T(8,128)(2,1)} %get-tuple-element.247.x_ref.a_ref, bf16[1472,4096]{1,0:T(8,128)(2,1)} %get-tuple-element.238.b_ref.h_ref), custom_call_target="tpu_custom_call" | custom-call | flops 6174015488 | bytes 10000000 | tf_op jit(solution)/shard_map/grad_send/pallas_call | solution.py:705
  231.4 26.2 %second_back.1 = (f32[1472,1024]{1,0:T(8,128)}, bf16[1472,1024]{1,0:T(8,128)(2,1)}, bf16[1472,1024]{1,0:T(8,128)(2,1)}, f32[8,1024]{1,0:T(8,128)}) custom-call(bf16[1472,4096]{1,0:T(8,128)(2,1)} %get-tuple-element.238.b_ref.h_ref, bf16[1024,4096]{1,0:T(8,128)(2,1)} %get-tuple-element.239.w_ref, bf16[1024,1024]{1,0:T(8,128)(2,1)} %get-tuple-element.240.o_ref, ...), custom_call_target="tpu_custom_call" | custom-call | flops 12348030976 | bytes 40000000 | tf_op jit(solution)/shard_map/second_back/pallas_call | solution.py:541
  257.6 3.1 fusion.2
  261.3 12.4 %grad_keep.6 = (bf16[2,4,64,2048]{3,2,1,0:T(8,128)(2,1)}, bf16[2,4,64,2048]{3,2,1,0:T(8,128)(2,1)}) custom-call(s32[2]{0:T(128)} %get-tuple-element.219.c_ref, f32[1]{0:T(128)} %bitcast.5.f_ref, bf16[1472,1024]{1,0:T(8,128)(2,1)} %get-tuple-element.247.x_ref.a_ref, bf16[1472,4096]{1,0:T(8,128)(2,1)} %get-tuple-element.238.b_ref.h_ref, ...), custom_call_target="tpu_custom_call" | custom-call | flops 6174015488 | bytes 10000000 | tf_op jit(solution)/shard_map/grad_keep/pallas_call | solution.py:705
  277.7 5.9 %grad_send.7 = bf16[1024,512]{1,0:T(8,128)(2,1)} custom-call(s32[2]{0:T(128)} %get-tuple-element.223.c_ref, f32[1]{0:T(128)} %bitcast.5.f_ref, bf16[1472,1024]{1,0:T(8,128)(2,1)} %attend_forward.1.a_ref, bf16[1472,1024]{1,0:T(8,128)(2,1)} %get-tuple-element.262.b_ref), custom_call_target="tpu_custom_call" | custom-call | flops 1543503872 | bytes 10000000 | tf_op jit(solution)/shard_map/grad_send/pallas_call | solution.py:705
  283.6 20.2 %attend_backward.2 = (bf16[3,1472,256]{2,1,0:T(8,128)(2,1)}, bf16[3,1472,256]{2,1,0:T(8,128)(2,1)}) custom-call(s32[4]{0:T(128)} %get-tuple-element.243.s_ref, f32[10,176,352]{2,1,0:T(8,128)} %image_masks.1.mask_ref, bf16[1472,3072]{1,0:T(8,128)(2,1)} %get-tuple-element.196.q_ref.k_ref.v_ref.refs_0_.refs_1_.refs_2_.refs_3_.refs_4_.refs_5_, ...), custom_call_target="tpu_custom_call" | custom-call | flops 20000000000 | bytes 10000000 | tf_op jit(solution)/shard_map/attend_backward/pallas_call | solution.py:233
  304.8 3.3 fusion.4
  308.1 6.6 %grad_send.8 = bf16[1024,768]{1,0:T(8,128)(2,1)} custom-call(s32[2]{0:T(128)} %get-tuple-element.223.c_ref, f32[1]{0:T(128)} %bitcast.5.f_ref, bf16[1472,1024]{1,0:T(8,128)(2,1)} %get-tuple-element.278.a_ref, bf16[3,1472,256]{2,1,0:T(8,128)(2,1)} %get-tuple-element.284.b_ref.refs_1_), custom_call_target="tpu_custom_call" | custom-call | flops 2315255808 | bytes 10000000 | tf_op jit(solution)/shard_map/grad_send/pallas_call | solution.py:705
  315.9 6.2 %grad_keep.7 = (bf16[2,4,64,1280]{3,2,1,0:T(8,128)(2,1)}, bf16[2,4,64,1280]{3,2,1,0:T(8,128)(2,1)}) custom-call(s32[2]{0:T(128)} %get-tuple-element.219.c_ref, f32[1]{0:T(128)} %bitcast.5.f_ref, bf16[1472,1024]{1,0:T(8,128)(2,1)} %attend_forward.1.a_ref, bf16[1472,1024]{1,0:T(8,128)(2,1)} %get-tuple-element.262.b_ref, bf16[1024,512]{1,0:T(8,128)(2,1)} %copy-done.10), custom_call_target="tpu_custom_call" | custom-call | flops 1543503872 | bytes 10000000 | tf_op jit(solution)/shard_map/grad_keep/pallas_call | solution.py:705
  323.3 7.1 %grad_keep.8 = (bf16[2,4,64,1280]{3,2,1,0:T(8,128)(2,1)}, bf16[2,4,64,1280]{3,2,1,0:T(8,128)(2,1)}) custom-call(s32[2]{0:T(128)} %get-tuple-element.219.c_ref, f32[1]{0:T(128)} %bitcast.5.f_ref, bf16[1472,1024]{1,0:T(8,128)(2,1)} %get-tuple-element.278.a_ref, ...), custom_call_target="tpu_custom_call", output_to_operand_aliasing={{0}: (5, {}), {1}: (6, {})} | custom-call | flops 2315255808 | bytes 10000000 | tf_op jit(solution)/shard_map/grad_keep/pallas_call | solution.py:705
  334.4 20.0 %attend_backward.3 = (bf16[3,1472,256]{2,1,0:T(8,128)(2,1)}, bf16[3,1472,256]{2,1,0:T(8,128)(2,1)}) custom-call(s32[4]{0:T(128)} %get-tuple-element.221.s_ref, f32[10,176,352]{2,1,0:T(8,128)} %image_masks.1.mask_ref, bf16[1472,3072]{1,0:T(8,128)(2,1)} %get-tuple-element.196.q_ref.k_ref.v_ref.refs_0_.refs_1_.refs_2_.refs_3_.refs_4_.refs_5_, ...), custom_call_target="tpu_custom_call" | custom-call | flops 20000000000 | bytes 10000000 | tf_op jit(solution)/shard_map/attend_backward/pallas_call | solution.py:233
  354.5 4.5 reduce-scatter.6.cloned.1.call-done
  360.6 6.7 %grad_send.9 = bf16[1024,768]{1,0:T(8,128)(2,1)} custom-call(s32[2]{0:T(128)} %get-tuple-element.223.c_ref, f32[1]{0:T(128)} %bitcast.5.f_ref, bf16[1472,1024]{1,0:T(8,128)(2,1)} %get-tuple-element.278.a_ref, bf16[3,1472,256]{2,1,0:T(8,128)(2,1)} %get-tuple-element.286.b_ref.refs_3_), custom_call_target="tpu_custom_call" | custom-call | flops 2315255808 | bytes 10000000 | tf_op jit(solution)/shard_map/grad_send/pallas_call | solution.py:705
  371.0 7.1 %grad_keep.9 = (bf16[2,4,64,768]{3,2,1,0:T(8,128)(2,1)}, bf16[2,4,64,768]{3,2,1,0:T(8,128)(2,1)}) custom-call(s32[2]{0:T(128)} %get-tuple-element.219.c_ref, f32[1]{0:T(128)} %bitcast.5.f_ref, bf16[1472,1024]{1,0:T(8,128)(2,1)} %get-tuple-element.278.a_ref, bf16[3,1472,256]{2,1,0:T(8,128)(2,1)} %get-tuple-element.285.b_ref.refs_2_, ...), custom_call_target="tpu_custom_call" | custom-call | flops 2315255808 | bytes 10000000 | tf_op jit(solution)/shard_map/grad_keep/pallas_call | solution.py:705
  381.2 23.0 %first_back.1 = (bf16[1450,1024]{1,0:T(8,128)(2,1)}, f32[128,1024]{1,0:T(8,128)}, f32[8,1024]{1,0:T(8,128)}) custom-call(s32[4]{0:T(128)} %add_add_fusion.1.s_ref, bf16[3,1472,256]{2,1,0:T(8,128)(2,1)} %get-tuple-element.283.b_ref.refs_0_, bf16[3,1472,256]{2,1,0:T(8,128)(2,1)} %get-tuple-element.284.b_ref.refs_1_, ...), custom_call_target="tpu_custom_call" | custom-call | flops 9261023232 | bytes 40000000 | tf_op jit(solution)/shard_map/first_back/pallas_call | solution.py:600
  409.3 5.0 %collective-permute-done.33 = bf16[4,64,768]{2,1,0:T(8,128)(2,1)S(1)} collective-permute-done((bf16[4,64,768]{2,1,0:T(8,128)(2,1)S(1)}, bf16[4,64,768]{2,1,0:T(8,128)(2,1)S(1)}, u32[]{:S(2)}, u32[]{:S(2)}) %collective-permute-start.33) | collective-permute-done | bytes 393248 | tf_op jit(solution)/shard_map/ppermute | solution.py:722
  418.4 19.0 %return_layer.1 = bf16[1450,1024]{1,0:T(8,128)(2,1)} custom-call(bf16[1472,4096]{1,0:T(8,128)(2,1)} %get-tuple-element.300.a_ref, bf16[4096,1024]{1,0:T(8,128)(2,1)} %get-tuple-element.301.w_ref, f32[1472,1024]{1,0:T(8,128)} %get-tuple-element.241.mid_ref, f32[64,1024]{1,0:T(8,128)} %get-tuple-element.170.vec_ref.b_ref.gain_ref.refs_19_), custom_call_target="tpu_custom_call" | custom-call | flops 12348030976 | bytes 30000000 | tf_op jit(solution)/shard_map/return_layer/pallas_call | solution.py:507
  437.7 13.2 %all-gather.1 = bf16[512,1016]{1,0:T(8,128)(2,1)S(1)} all-gather(bf16[64,1016]{1,0:T(8,128)(2,1)S(1)} %pad_maximum_fusion.8), channel_id=3, replica_groups=mesh['dp'=8,'fsdp'=4] {'dp'}, dimensions={0}, use_global_device_ids=true | all-gather | bytes 1170432 | tf_op jit(solution)/shard_map/all_gather | solution.py:856
  453.0 7.8 %widen.1 = (f32[1024,1024]{1,0:T(8,128)}, f32[256,4096]{1,0:T(8,128)}, f32[256,3072]{1,0:T(8,128)}, f32[256,1024]{1,0:T(8,128)}) custom-call(bf16[4,2,64,5376]{3,2,1,0:T(8,128)(2,1)} %bitcast.100, bf16[4,2,64,1016]{3,2,1,0:T(8,128)(2,1)} %bitcast.102), custom_call_target="tpu_custom_call" | custom-call | flops 1 | bytes 6000000 | tf_op jit(solution)/shard_map/widen/pallas_call | solution.py:631
  (204 shorter events, 86.0 us)
Async XLA Ops:
  7.2 63.4 %all-gather.6.cloned.1.call-start = ((), (), s32[]{:S(2)}) async-start(), calls=%async_computation.6 | async-start | bytes 1310720 | tf_op jit(solution)/shard_map/all_gather | solution.py:752
  9.0 18.7 %collective-permute-start.2 = (bf16[32,3584]{1,0:T(8,128)(2,1)}, bf16[32,3584]{1,0:T(8,128)(2,1)S(1)}, u32[]{:S(2)}, u32[]{:S(2)}) collective-permute-start(bf16[32,3584]{1,0:T(8,128)(2,1)} %pack.1.refs_0_), channel_id=1, source_target_pairs={{3,0},{0,1},{1,2},{2,3},{7,4},{4,5},{5,6},{6,7},{11,8},{8,9},{9,10... | collective-permute-start | bytes 688136 | tf_op jit(solution)/shard_map/ppermute | solution.py:746
  12.0 17.8 %collective-permute-start.1 = (bf16[32,3584]{1,0:T(8,128)(2,1)}, bf16[32,3584]{1,0:T(8,128)(2,1)S(1)}, u32[]{:S(2)}, u32[]{:S(2)}) collective-permute-start(bf16[32,3584]{1,0:T(8,128)(2,1)} %pack.1.refs_0_), channel_id=1, source_target_pairs={{2,0},{3,1},{0,2},{1,3},{6,4},{7,5},{4,6},{5,7},{10,8},{11,9},{8,1... | collective-permute-start | bytes 688136 | tf_op jit(solution)/shard_map/ppermute | solution.py:746
  14.6 15.2 %collective-permute-start = (bf16[32,3584]{1,0:T(8,128)(2,1)}, bf16[32,3584]{1,0:T(8,128)(2,1)S(1)}, u32[]{:S(2)}, u32[]{:S(2)}) collective-permute-start(bf16[32,3584]{1,0:T(8,128)(2,1)} %pack.1.refs_0_), channel_id=1, source_target_pairs={{1,0},{2,1},{3,2},{0,3},{5,4},{6,5},{7,6},{4,7},{9,8},{10,9},{11,1... | collective-permute-start | bytes 688136 | tf_op jit(solution)/shard_map/ppermute | solution.py:746
  33.2 270.6 %reduce-scatter.4.cloned.1.call-start = ((), (), s32[]{:S(2)}) async-start(), calls=%async_computation.3 | async-start | bytes 1310720 | tf_op jit(solution)/shard_map/reduce_scatter | solution.py:877
  41.0 29.6 %collective-permute-start.4 = (bf16[2,3,32,3072]{3,2,1,0:T(8,128)(2,1)}, bf16[2,3,32,3072]{3,2,1,0:T(8,128)(2,1)}, u32[]{:S(2)}, u32[]{:S(2)}) collective-permute-start(bf16[2,3,32,3072]{3,2,1,0:T(8,128)(2,1)} %pad_maximum_fusion.2.refs_1_), channel_id=1, source_target_pairs={{0,16},{4,12},{8,24},{12,4},{16,0},{20,28},{24,8},{28,20},{1,17},{... | collective-permute-start | bytes 3538952 | tf_op jit(solution)/shard_map/ppermute | solution.py:722
  43.4 10.7 %collective-permute-start.7 = (bf16[32,1024]{1,0:T(8,128)(2,1)S(1)}, bf16[32,1024]{1,0:T(8,128)(2,1)S(1)}, u32[]{:S(2)}, u32[]{:S(2)}) collective-permute-start(bf16[32,1024]{1,0:T(8,128)(2,1)S(1)} %constant_dynamic-slice_fusion.1), channel_id=1, source_target_pairs={{3,0},{0,1},{1,2},{2,3},{7,4},{4,5},{5,6},{6,7},{11,8},{8,9},{9,10... | collective-permute-start | bytes 196616 | tf_op jit(solution)/shard_map/ppermute | solution.py:746
  72.7 19.1 %collective-permute-start.11 = (bf16[3,32,5120]{2,1,0:T(8,128)(2,1)S(1)}, bf16[3,32,5120]{2,1,0:T(8,128)(2,1)S(1)}, u32[]{:S(2)}, u32[]{:S(2)}) collective-permute-start(bf16[3,32,5120]{2,1,0:T(8,128)(2,1)S(1)} %pad_maximum_fusion.4), channel_id=1, source_target_pairs={{0,8},{4,20},{8,0},{12,28},{16,24},{20,4},{24,16},{28,12},{1,9},{5... | collective-permute-start | bytes 2949128 | tf_op jit(solution)/shard_map/ppermute | solution.py:722
  74.2 17.6 %collective-permute-start.10 = (bf16[128,1024]{1,0:T(8,128)(2,1)S(1)}, bf16[128,1024]{1,0:T(8,128)(2,1)S(1)}, u32[]{:S(2)}, u32[]{:S(2)}) collective-permute-start(bf16[128,1024]{1,0:T(8,128)(2,1)S(1)} %constant_dynamic-slice_fusion), channel_id=1, source_target_pairs={{1,0},{2,1},{3,2},{0,3},{5,4},{6,5},{7,6},{4,7},{9,8},{10,9},{11,1... | collective-permute-start | bytes 786440 | tf_op jit(solution)/shard_map/ppermute | solution.py:746
  93.3 24.9 %collective-permute-start.12 = (bf16[2,3,32,5120]{3,2,1,0:T(8,128)(2,1)}, bf16[2,3,32,5120]{3,2,1,0:T(8,128)(2,1)}, u32[]{:S(2)}, u32[]{:S(2)}) collective-permute-start(bf16[2,3,32,5120]{3,2,1,0:T(8,128)(2,1)} %pad_maximum_fusion.refs_1_), channel_id=1, source_target_pairs={{0,16},{4,12},{8,24},{12,4},{16,0},{20,28},{24,8},{28,20},{1,17},{... | collective-permute-start | bytes 5898248 | tf_op jit(solution)/shard_map/ppermute | solution.py:722
  94.8 22.0 %collective-permute-start.14 = (bf16[128,1024]{1,0:T(8,128)(2,1)S(1)}, bf16[128,1024]{1,0:T(8,128)(2,1)S(1)}, u32[]{:S(2)}, u32[]{:S(2)}) collective-permute-start(bf16[128,1024]{1,0:T(8,128)(2,1)S(1)} %constant_dynamic-slice_fusion), channel_id=1, source_target_pairs={{3,0},{0,1},{1,2},{2,3},{7,4},{4,5},{5,6},{6,7},{11,8},{8,9},{9,10... | collective-permute-start | bytes 786440 | tf_op jit(solution)/shard_map/ppermute | solution.py:746
  95.5 21.2 %collective-permute-start.13 = (bf16[128,1024]{1,0:T(8,128)(2,1)S(1)}, bf16[128,1024]{1,0:T(8,128)(2,1)S(1)}, u32[]{:S(2)}, u32[]{:S(2)}) collective-permute-start(bf16[128,1024]{1,0:T(8,128)(2,1)S(1)} %constant_dynamic-slice_fusion), channel_id=1, source_target_pairs={{2,0},{3,1},{0,2},{1,3},{6,4},{7,5},{4,6},{5,7},{10,8},{11,9},{8,1... | collective-permute-start | bytes 786440 | tf_op jit(solution)/shard_map/ppermute | solution.py:746
  118.9 18.9 %collective-permute-start.17 = (bf16[3,128,1024]{2,1,0:T(8,128)(2,1)S(1)}, bf16[3,128,1024]{2,1,0:T(8,128)(2,1)}, u32[]{:S(2)}, u32[]{:S(2)}) collective-permute-start(bf16[3,128,1024]{2,1,0:T(8,128)(2,1)S(1)} %pad_maximum_fusion.5), channel_id=1, source_target_pairs={{0,8},{4,20},{8,0},{12,28},{16,24},{20,4},{24,16},{28,12},{1,9},{5... | collective-permute-start | bytes 2359304 | tf_op jit(solution)/shard_map/ppermute | solution.py:722
  139.1 30.8 %collective-permute-start.18 = (bf16[2,3,128,1024]{3,2,1,0:T(8,128)(2,1)S(1)}, bf16[2,3,128,1024]{3,2,1,0:T(8,128)(2,1)}, u32[]{:S(2)}, u32[]{:S(2)}) collective-permute-start(bf16[2,3,128,1024]{3,2,1,0:T(8,128)(2,1)S(1)} %pad_maximum_fusion.1.refs_1_), channel_id=1, source_target_pairs={{0,16},{4,12},{8,24},{12,4},{16,0},{20,28},{24,8},{28,20},{1,17},{... | collective-permute-start | bytes 4718600 | tf_op jit(solution)/shard_map/ppermute | solution.py:722
  169.9 12.4 %collective-permute-start.19 = (bf16[2,3,128,1024]{3,2,1,0:T(8,128)(2,1)S(1)}, bf16[2,3,128,1024]{3,2,1,0:T(8,128)(2,1)}, u32[]{:S(2)}, u32[]{:S(2)}) collective-permute-start(bf16[2,3,128,1024]{3,2,1,0:T(8,128)(2,1)S(1)} %pad_maximum_fusion.1.refs_1_), channel_id=1, source_target_pairs={{0,4},{4,0},{8,12},{12,8},{16,20},{20,16},{24,28},{28,24},{1,5},{5... | collective-permute-start | bytes 4718600 | tf_op jit(solution)/shard_map/ppermute | solution.py:722
  170.0 12.3 %collective-permute-start.20 = (bf16[2,3,128,1024]{3,2,1,0:T(8,128)(2,1)}, bf16[2,3,128,1024]{3,2,1,0:T(8,128)(2,1)}, u32[]{:S(2)}, u32[]{:S(2)}) collective-permute-start(bf16[2,3,128,1024]{3,2,1,0:T(8,128)(2,1)} %collective-permute-done.18.refs_2_), channel_id=1, source_target_pairs={{0,4},{4,0},{8,12},{12,8},{16,20},{20,16},{24,28},{28,24},{1,5},{5... | collective-permute-start | bytes 4718600 | tf_op jit(solution)/shard_map/ppermute | solution.py:722
  182.3 22.8 %collective-permute-start.21 = (bf16[4096,512]{1,0:T(8,128)(2,1)}, bf16[4096,512]{1,0:T(8,128)(2,1)}, u32[]{:S(2)}, u32[]{:S(2)}) collective-permute-start(bf16[4096,512]{1,0:T(8,128)(2,1)} %grad_send.5), channel_id=1, source_target_pairs={{0,4},{4,0},{8,12},{12,8},{16,20},{20,16},{24,28},{28,24},{1,5},{5... | collective-permute-start | bytes 12582920 | tf_op jit(solution)/shard_map/ppermute | solution.py:722
  229.5 28.0 %collective-permute-start.22 = (bf16[1024,2048]{1,0:T(8,128)(2,1)}, bf16[1024,2048]{1,0:T(8,128)(2,1)}, u32[]{:S(2)}, u32[]{:S(2)}) collective-permute-start(bf16[1024,2048]{1,0:T(8,128)(2,1)} %grad_send.6), channel_id=1, source_target_pairs={{0,4},{4,0},{8,12},{12,8},{16,20},{20,16},{24,28},{28,24},{1,5},{5... | collective-permute-start | bytes 12582920 | tf_op jit(solution)/shard_map/ppermute | solution.py:722
  230.0 27.6 %collective-permute-start.23 = (bf16[2,4,256,512]{3,2,1,0:T(8,128)(2,1)}, bf16[2,4,256,512]{3,2,1,0:T(8,128)(2,1)}, u32[]{:S(2)}, u32[]{:S(2)}) collective-permute-start(bf16[2,4,256,512]{3,2,1,0:T(8,128)(2,1)} %get-tuple-element.236), channel_id=1, source_target_pairs={{0,8},{4,20},{8,0},{12,28},{16,24},{20,4},{24,16},{28,12},{1,9},{5... | collective-permute-start | bytes 6291464 | tf_op jit(solution)/shard_map/ppermute | solution.py:722
  260.7 15.0 %collective-permute-start.24 = (bf16[4,256,512]{2,1,0:T(8,128)(2,1)}, bf16[4,256,512]{2,1,0:T(8,128)(2,1)S(1)}, u32[]{:S(2)}, u32[]{:S(2)}) collective-permute-start(bf16[4,256,512]{2,1,0:T(8,128)(2,1)} %get-tuple-element.314), channel_id=1, source_target_pairs={{0,16},{4,12},{8,24},{12,4},{16,0},{20,28},{24,8},{28,20},{1,17},{... | collective-permute-start | bytes 3145736 | tf_op jit(solution)/shard_map/ppermute | solution.py:722
  277.0 82.0 %reduce-scatter.6.cloned.1.call-start = ((), (), s32[]{:S(2)}) async-start(), calls=%async_computation.4 | async-start | bytes 1310720 | tf_op jit(solution)/shard_map/reduce_scatter | solution.py:877
  277.0 26.8 %collective-permute-start.26 = (bf16[2,4,64,2048]{3,2,1,0:T(8,128)(2,1)}, bf16[2,4,64,2048]{3,2,1,0:T(8,128)(2,1)}, u32[]{:S(2)}, u32[]{:S(2)}) collective-permute-start(bf16[2,4,64,2048]{3,2,1,0:T(8,128)(2,1)} %get-tuple-element.255), channel_id=1, source_target_pairs={{0,8},{4,20},{8,0},{12,28},{16,24},{20,4},{24,16},{28,12},{1,9},{5... | collective-permute-start | bytes 6291464 | tf_op jit(solution)/shard_map/ppermute | solution.py:722
  283.6 20.2 %collective-permute-start.25 = (bf16[1024,512]{1,0:T(8,128)(2,1)}, bf16[1024,512]{1,0:T(8,128)(2,1)S(1)}, u32[]{:S(2)}, u32[]{:S(2)}) collective-permute-start(bf16[1024,512]{1,0:T(8,128)(2,1)} %grad_send.7), channel_id=1, source_target_pairs={{0,4},{4,0},{8,12},{12,8},{16,20},{20,16},{24,28},{28,24},{1,5},{5... | collective-permute-start | bytes 3145736 | tf_op jit(solution)/shard_map/ppermute | solution.py:722
  315.2 15.2 %collective-permute-start.28 = (bf16[4,64,2048]{2,1,0:T(8,128)(2,1)}, bf16[4,64,2048]{2,1,0:T(8,128)(2,1)}, u32[]{:S(2)}, u32[]{:S(2)}) collective-permute-start(bf16[4,64,2048]{2,1,0:T(8,128)(2,1)} %get-tuple-element.312), channel_id=1, source_target_pairs={{0,16},{4,12},{8,24},{12,4},{16,0},{20,28},{24,8},{28,20},{1,17},{... | collective-permute-start | bytes 3145736 | tf_op jit(solution)/shard_map/ppermute | solution.py:722
  333.1 71.2 %reduce-scatter.8.cloned.1.call-start = ((), (), s32[]{:S(2)}) async-start(), calls=%async_computation.5 | async-start | bytes 819200 | tf_op jit(solution)/shard_map/reduce_scatter | solution.py:877
  333.2 21.3 %collective-permute-start.29 = (bf16[2,4,64,1280]{3,2,1,0:T(8,128)(2,1)S(1)}, bf16[2,4,64,1280]{3,2,1,0:T(8,128)(2,1)}, u32[]{:S(2)}, u32[]{:S(2)}) collective-permute-start(bf16[2,4,64,1280]{3,2,1,0:T(8,128)(2,1)S(1)} %copy-done.9), channel_id=1, source_target_pairs={{0,8},{4,20},{8,0},{12,28},{16,24},{20,4},{24,16},{28,12},{1,9},{5... | collective-permute-start | bytes 3932168 | tf_op jit(solution)/shard_map/ppermute | solution.py:722
  367.9 10.7 %collective-permute-start.31 = (bf16[4,64,1280]{2,1,0:T(8,128)(2,1)S(1)}, bf16[4,64,1280]{2,1,0:T(8,128)(2,1)S(1)}, u32[]{:S(2)}, u32[]{:S(2)}) collective-permute-start(bf16[4,64,1280]{2,1,0:T(8,128)(2,1)S(1)} %get-tuple-element.316), channel_id=1, source_target_pairs={{0,16},{4,12},{8,24},{12,4},{16,0},{20,28},{24,8},{28,20},{1,17},{... | collective-permute-start | bytes 1966088 | tf_op jit(solution)/shard_map/ppermute | solution.py:722
  379.5 73.4 %all-gather.8.cloned.1.call-start = ((), (), s32[]{:S(2)}) async-start(), calls=%async_computation.7 | async-start | bytes 6193152 | tf_op jit(solution)/shard_map/all_gather | solution.py:856
  379.6 24.7 %collective-permute-start.32 = (bf16[2,4,64,768]{3,2,1,0:T(8,128)(2,1)}, bf16[2,4,64,768]{3,2,1,0:T(8,128)(2,1)S(1)}, u32[]{:S(2)}, u32[]{:S(2)}) collective-permute-start(bf16[2,4,64,768]{3,2,1,0:T(8,128)(2,1)} %get-tuple-element.282), channel_id=1, source_target_pairs={{0,8},{4,20},{8,0},{12,28},{16,24},{20,4},{24,16},{28,12},{1,9},{5... | collective-permute-start | bytes 2359304 | tf_op jit(solution)/shard_map/ppermute | solution.py:722
  414.5 22.9 %collective-permute-start.34 = (bf16[64,1024]{1,0:T(8,128)(2,1)S(1)}, bf16[64,1024]{1,0:T(8,128)(2,1)S(1)}, u32[]{:S(2)}, u32[]{:S(2)}) collective-permute-start(bf16[64,1024]{1,0:T(8,128)(2,1)S(1)} %get-tuple-element.318), channel_id=1, source_target_pairs={{0,1},{1,2},{2,3},{3,0},{4,5},{5,6},{6,7},{7,4},{8,9},{9,10},{10,1... | collective-permute-start | bytes 393224 | tf_op jit(solution)/shard_map/ppermute | solution.py:889
  414.6 22.8 %collective-permute-start.35 = (bf16[64,1024]{1,0:T(8,128)(2,1)S(1)}, bf16[64,1024]{1,0:T(8,128)(2,1)S(1)}, u32[]{:S(2)}, u32[]{:S(2)}) collective-permute-start(bf16[64,1024]{1,0:T(8,128)(2,1)S(1)} %get-tuple-element.319), channel_id=1, source_target_pairs={{0,2},{1,3},{2,0},{3,1},{4,6},{5,7},{6,4},{7,5},{8,10},{9,11},{10,... | collective-permute-start | bytes 393224 | tf_op jit(solution)/shard_map/ppermute | solution.py:889
  415.9 21.5 %collective-permute-start.36 = (bf16[64,1024]{1,0:T(8,128)(2,1)S(1)}, bf16[64,1024]{1,0:T(8,128)(2,1)S(1)}, u32[]{:S(2)}, u32[]{:S(2)}) collective-permute-start(bf16[64,1024]{1,0:T(8,128)(2,1)S(1)} %get-tuple-element.320), channel_id=1, source_target_pairs={{0,3},{1,0},{2,1},{3,2},{4,7},{5,4},{6,5},{7,6},{8,11},{9,8},{10,9... | collective-permute-start | bytes 393224 | tf_op jit(solution)/shard_map/ppermute | solution.py:889
  (33 other events, 268.8 us)
Sparse Core Ops, SparseCore 0:
  33.3 37.2 all-gather.5
  277.1 24.5 reduce-scatter.3
  333.2 25.6 reduce-scatter.5
  379.7 20.8 reduce-scatter.7
  406.3 41.5 all-gather.7

commit v5 on v4

--- a/solution.py
+++ b/solution.py
@@ -934,15 +934,18 @@
 
 
 def unpack_kernel(s_ref, *refs):
-    parts, (out_ref, table_ref, rows_ref) = refs[:-3], refs[-3:]
-    width = rows_ref.shape[1]
+    parts, (out_ref, table_ref, rest_ref, rows_ref) = refs[:-4], refs[-4:]
+    width, first = rows_ref.shape[1], rest_ref.shape[2]
     tall = parts[0].shape[0]
     table_ref[...] = jnp.zeros_like(table_ref)
     for k, ref in enumerate(parts):
         at = lax.rem(s_ref[0] + k, len(parts)) * width
         at = pl.ds(pl.multiple_of(at, width), width)
         for i in range(64 // tall):
-            rows_ref[i * tall : (i + 1) * tall, :] = ref[:, i * width : (i + 1) * width]
+            source = first + i * width
+            rows_ref[i * tall : (i + 1) * tall, :] = ref[:, source : source + width]
+        if k:
+            rest_ref[k - 1] = ref[:, :first]
         out_ref[:, at] = rows_ref[...].astype(jnp.float32)
         table = rows_ref[12 : 12 + SMALL_LEN, :]
         table_ref[0:SMALL_LEN, at] = table
@@ -951,20 +954,21 @@
 
 def unpack(parts, first, width):
     shards = len(parts)
-    tall = parts[0].shape[0]
-    wide = parts[0].shape[1] - first
+    tall, wide = parts[0].shape
     return pl.pallas_call(
         unpack_kernel,
         out_shape=[
             jax.ShapeDtypeStruct((64, shards * width), jnp.float32),
             jax.ShapeDtypeStruct((128, shards * width), LOW),
+            jax.ShapeDtypeStruct((shards - 1, tall, first), LOW),
         ],
         grid=(1,),
         in_specs=[pl.BlockSpec(memory_space=pltpu.SMEM)]
-        + [pl.BlockSpec((tall, wide), lambda i: (0, first // wide))] * shards,
+        + [pl.BlockSpec((tall, wide), lambda i: (0, 0))] * shards,
         out_specs=[
             pl.BlockSpec((64, shards * width), lambda i: (0, 0)),
             pl.BlockSpec((128, shards * width), lambda i: (0, 0)),
+            pl.BlockSpec((shards - 1, tall, first), lambda i: (0, 0, 0)),
         ],
         scratch_shapes=[pltpu.VMEM((64, width), LOW)],
         cost_estimate=cost(1, 1e6),
@@ -1054,8 +1058,7 @@
     spread_low, scale, mine, other, lengths, numbers_one, numbers_two, hidden_own, *parts = sync(
         spread_low, scale, mine, other, lengths, numbers_one, numbers_two, hidden_own, *parts
     )
-    joint_z = jnp.stack([v[:, : 3 * D] for v in parts])
-    smalls, table_pair = unpack([packed_own] + parts, 3 * D, first_gain.shape[0])
+    smalls, table_pair, joint_z = unpack([packed_own] + parts, 3 * D, first_gain.shape[0])
     hidden_add = smalls[8:12].reshape(4, fsdp_size, -1).transpose(1, 0, 2).reshape(-1)
     joint_one = gather_first(joint_z)
     hidden_z = gather_z_native(after(hidden_own, joint_z))
@@ -1067,10 +1070,10 @@
     masks = image_masks(lengths)
     grad_pad = jnp.pad(output_grad, ((0, PAD - ROWS), (0, 0)))
     output_z = jnp.stack(output_z)
-    *joint_two, hidden_z, output_z, hidden_add, return_z, grad_pad, masks = sync(
-        *joint_two, hidden_z, output_z, hidden_add, return_z, grad_pad, masks
-    )
     joint_sets = gather_core(*joint_two)
+    hidden_z, output_z, hidden_add, return_z, grad_pad, masks, _ = sync(
+        hidden_z, output_z, hidden_add, return_z, grad_pad, masks, joint_two[1]
+    )
     first_low, *joint_sets = sync(first_low, *joint_sets)
     hidden_one = gather_first(jnp.concatenate([others(hidden_z), output_z], axis=-1))
     return_early, *return_late = from_above(return_z)

time: 475 us -> 475 us (level)
    ppermute x25, waiting for transfers between devices: 14.2 us -> 21.8 us  [swap(): lax.ppermute(value, 'dp', [(i, i ^ (odd if i % 2 else even)) for i in ran...]
where the time goes in v5:
time: 475 us; the launch traced here: 468 us
  Pallas kernels  319 us (67%)
  starting transfers between devices  39.9 us (8%)
  waiting for transfers between devices  34 us (7%)
  other arithmetic  24.3 us (5%)
  local copies, waits for them, and re-layouts  18.8 us (4%)
  between operations  18 us (4%)
  blocking collectives  13.1 us (3%)
    pallas_call x10, Pallas kernels, grad_half(): pl.pallas_call(kernel, out_shape=out_shape, grid_spec=pltpu.PrefetchScala...  88.3 us
    pallas_call x2, Pallas kernels, attend_backward(): pl.pallas_call(backward_kernel, out_shape=[jax.ShapeDtypeStruct((3, PAD,...  40.3 us
    pallas_call x1, Pallas kernels, hidden_layer(): pl.pallas_call(partial(hidden_kernel, lax.axis_size('fsdp'), steps, 736),...  29.3 us
    pallas_call x1, Pallas kernels, second_back(): pl.pallas_call(second_back_kernel, out_shape=[jax.ShapeDtypeStruct((PAD,...  26.2 us
    pallas_call x1, Pallas kernels, first_back(): pl.pallas_call(first_back_kernel, out_shape=[jax.ShapeDtypeStruct((ROWS,...  23 us
    pallas_call x1, Pallas kernels, hidden_back(): pl.pallas_call(partial(hidden_back_kernel, shards, steps, 368), out_shape...  22.6 us
    ppermute x25, waiting for transfers between devices, swap(): lax.ppermute(value, 'dp', [(i, i ^ (odd if i % 2 else even)) for i in ran...  21.8 us
    pallas_call x1, Pallas kernels, attend_forward(): pl.pallas_call(forward_kernel, out_shape=jax.ShapeDtypeStruct((PAD, D), L...  20.1 us
  transfers between devices with their start and end apart: 42, of which 14 were waited for; matrix products, arithmetic and copies ran while one was open for 5% of the time, Pallas kernels for 58%

profile of v5, /device:TPU:0, one launch (start us, length us, event | category | flops | bytes accessed | tf_op | source)
XLA Modules:
  0.0 467.6 jit_solution(2966398981776973128)
XLA Ops:
  9.0 3.0 collective-permute-start.2
  34.5 6.4 %embed.1 = (f32[1472,1024]{1,0:T(8,128)}, bf16[1472,1024]{1,0:T(8,128)(2,1)}) custom-call(bf16[1450,1024]{1,0:T(8,128)(2,1)} %tokens_ref.1, bf16[1472,128]{1,0:T(8,128)(2,1)} %fusion.14.spread_ref.refs_18_, bf16[128,1024]{1,0:T(8,128)(2,1)} %get-tuple-element.168.table_ref, f32[64,1024]{1,0:T(8,128)} %get-tuple-element.169.vec_ref.b_ref.gain_ref.refs_19_), custom_call_target="tpu_custom_call" | custom-call | flops 1000000000 | bytes 15000000 | tf_op jit(solution)/shard_map/embed/pallas_call | solution.py:427
  46.5 5.3 %collective-permute-start.6 = (bf16[32,1024]{1,0:T(8,128)(2,1)S(1)}, bf16[32,1024]{1,0:T(8,128)(2,1)S(1)}, u32[]{:S(2)}, u32[]{:S(2)}) collective-permute-start(bf16[32,1024]{1,0:T(8,128)(2,1)S(1)} %constant_dynamic-slice_fusion.1), channel_id=1, source_target_pairs={{3,0},{0,1},{1,2},{2,3},{7,4},{4,5},{5,6},{6,7},{11,8},{8,9},{9,10... | collective-permute-start | bytes 196616 | tf_op jit(solution)/shard_map/ppermute | solution.py:746
  56.5 4.1 collective-permute-done.7.refs_2_
  61.6 2.8 image_masks.1.mask_ref
  66.4 5.4 %all-gather.6.cloned.1.call-done = bf16[128,4096]{1,0:T(8,128)(2,1)} async-done(((bf16[32,4096]{1,0:T(8,128)(2,1)}), bf16[128,4096]{1,0:T(8,128)(2,1)}) %all-gather.6.cloned.1.call-update) | async-done | bytes 1048592 | tf_op jit(solution)/shard_map/all_gather | solution.py:752
  77.1 16.3 %project.1 = (bf16[1472,3072]{1,0:T(8,128)(2,1)}, bf16[1024,3072]{1,0:T(8,128)(2,1)}) custom-call(s32[2]{0:T(128)} %pad_add_fusion.s_ref, bf16[1472,1024]{1,0:T(8,128)(2,1)} %get-tuple-element.276.a_ref, f32[64,1024]{1,0:T(8,128)} %get-tuple-element.169.vec_ref.b_ref.gain_ref.refs_19_, bf16[256,3072]{1,0:T(8,128)(2,1)} %refs_0_.4, ...), custom_call_target="tpu_custom_call" | custom-call | flops 9261023232 | bytes 20000000 | tf_op jit(solution)/shard_map/project/pallas_call | solution.py:453
  97.3 20.1 %attend_forward.1.a_ref = bf16[1472,1024]{1,0:T(8,128)(2,1)} custom-call(s32[2]{0:T(128)} %pad_add_fusion.3.s_ref, f32[10,176,352]{2,1,0:T(8,128)} %image_masks.1.mask_ref, bf16[1472,3072]{1,0:T(8,128)(2,1)} %get-tuple-element.194.q_ref.k_ref.v_ref.refs_0_.refs_1_.refs_2_.refs_3_.refs_4_.refs_5_, ...), custom_call_target="tpu_custom_call" | custom-call | flops 20000000000 | bytes 10000000 | tf_op jit(solution)/shard_map/attend_forward/pallas_call | solution.py:213
  126.9 12.4 %branch.1 = (f32[1472,1024]{1,0:T(8,128)}, bf16[1472,1024]{1,0:T(8,128)(2,1)}, bf16[1024,1024]{1,0:T(8,128)(2,1)}) custom-call(s32[2]{0:T(128)} %pad_add_fusion.s_ref, bf16[1472,1024]{1,0:T(8,128)(2,1)} %attend_forward.1.a_ref, f32[1472,1024]{1,0:T(8,128)} %get-tuple-element.203.stream_ref.refs_16_, ...), custom_call_target="tpu_custom_call" | custom-call | flops 3087007744 | bytes 30000000 | tf_op jit(solution)/shard_map/branch/pallas_call | solution.py:481
  142.2 29.3 %hidden_layer.1 = (bf16[1472,4096]{1,0:T(8,128)(2,1)}, bf16[1472,4096]{1,0:T(8,128)(2,1)}, bf16[1024,4096]{1,0:T(8,128)(2,1)}) custom-call(s32[2]{0:T(128)} %pad_add_fusion.s_ref, bf16[1472,1024]{1,0:T(8,128)(2,1)} %get-tuple-element.245.x_ref.a_ref, f32[1,4096]{1,0:T(1,128)} %bitcast.119, bf16[256,5120]{1,0:T(8,128)(2,1)} %copy-done, ...), custom_call_target="tpu_custom_call" | custom-call | flops 24000000000 | bytes 40000000 | tf_op jit(solution)/shard_map/hidden_layer/pallas_call | solution.py:288
  172.0 11.8 %grad_send.5 = bf16[4096,512]{1,0:T(8,128)(2,1)} custom-call(s32[2]{0:T(128)} %get-tuple-element.221.c_ref, f32[1]{0:T(128)} %bitcast.5.f_ref, bf16[1472,4096]{1,0:T(8,128)(2,1)} %get-tuple-element.298.a_ref, bf16[1472,1024]{1,0:T(8,128)(2,1)} %pad.18.b_ref.g_ref), custom_call_target="tpu_custom_call" | custom-call | flops 6174015488 | bytes 10000000 | tf_op jit(solution)/shard_map/grad_send/pallas_call | solution.py:705
  184.0 22.6 %hidden_back.1 = (bf16[1472,4096]{1,0:T(8,128)(2,1)}, f32[1,4096]{1,0:T(1,128)}, bf16[4096,1024]{1,0:T(8,128)(2,1)}) custom-call(s32[2]{0:T(128)} %pad_add_fusion.s_ref, bf16[1472,1024]{1,0:T(8,128)(2,1)} %pad.18.b_ref.g_ref, bf16[1472,4096]{1,0:T(8,128)(2,1)} %get-tuple-element.226.slope_ref, bf16[1024,1024]{1,0:T(8,128)(2,1)} %refs_0_.5, ...), custom_call_target="tpu_custom_call" | custom-call | flops 17999998976 | bytes 40000000 | tf_op jit(solution)/shard_map/hidden_back/pallas_call | solution.py:360
  206.6 12.9 %grad_keep.5 = (bf16[2,4,256,512]{3,2,1,0:T(8,128)(2,1)}, bf16[2,4,256,512]{3,2,1,0:T(8,128)(2,1)}) custom-call(s32[2]{0:T(128)} %get-tuple-element.217.c_ref, f32[1]{0:T(128)} %bitcast.5.f_ref, bf16[1472,4096]{1,0:T(8,128)(2,1)} %get-tuple-element.298.a_ref, bf16[1472,1024]{1,0:T(8,128)(2,1)} %pad.18.b_ref.g_ref, ...), custom_call_target="tpu_custom_call" | custom-call | flops 6174015488 | bytes 10000000 | tf_op jit(solution)/shard_map/grad_keep/pallas_call | solution.py:705
  219.5 11.5 %grad_send.6 = bf16[1024,2048]{1,0:T(8,128)(2,1)} custom-call(s32[2]{0:T(128)} %get-tuple-element.221.c_ref, f32[1]{0:T(128)} %bitcast.5.f_ref, bf16[1472,1024]{1,0:T(8,128)(2,1)} %get-tuple-element.245.x_ref.a_ref, bf16[1472,4096]{1,0:T(8,128)(2,1)} %get-tuple-element.236.b_ref.h_ref), custom_call_target="tpu_custom_call" | custom-call | flops 6174015488 | bytes 10000000 | tf_op jit(solution)/shard_map/grad_send/pallas_call | solution.py:705
  232.1 26.2 %second_back.1 = (f32[1472,1024]{1,0:T(8,128)}, bf16[1472,1024]{1,0:T(8,128)(2,1)}, bf16[1472,1024]{1,0:T(8,128)(2,1)}, f32[8,1024]{1,0:T(8,128)}) custom-call(bf16[1472,4096]{1,0:T(8,128)(2,1)} %get-tuple-element.236.b_ref.h_ref, bf16[1024,4096]{1,0:T(8,128)(2,1)} %get-tuple-element.237.w_ref, bf16[1024,1024]{1,0:T(8,128)(2,1)} %get-tuple-element.238.o_ref, ...), custom_call_target="tpu_custom_call" | custom-call | flops 12348030976 | bytes 40000000 | tf_op jit(solution)/shard_map/second_back/pallas_call | solution.py:541
  258.3 3.1 fusion.2
  262.3 12.4 %grad_keep.6 = (bf16[2,4,64,2048]{3,2,1,0:T(8,128)(2,1)}, bf16[2,4,64,2048]{3,2,1,0:T(8,128)(2,1)}) custom-call(s32[2]{0:T(128)} %get-tuple-element.217.c_ref, f32[1]{0:T(128)} %bitcast.5.f_ref, bf16[1472,1024]{1,0:T(8,128)(2,1)} %get-tuple-element.245.x_ref.a_ref, bf16[1472,4096]{1,0:T(8,128)(2,1)} %get-tuple-element.236.b_ref.h_ref, ...), custom_call_target="tpu_custom_call" | custom-call | flops 6174015488 | bytes 10000000 | tf_op jit(solution)/shard_map/grad_keep/pallas_call | solution.py:705
  279.3 6.0 %grad_send.7 = bf16[1024,512]{1,0:T(8,128)(2,1)} custom-call(s32[2]{0:T(128)} %get-tuple-element.221.c_ref, f32[1]{0:T(128)} %bitcast.5.f_ref, bf16[1472,1024]{1,0:T(8,128)(2,1)} %attend_forward.1.a_ref, bf16[1472,1024]{1,0:T(8,128)(2,1)} %get-tuple-element.260.b_ref), custom_call_target="tpu_custom_call" | custom-call | flops 1543503872 | bytes 10000000 | tf_op jit(solution)/shard_map/grad_send/pallas_call | solution.py:705
  285.3 20.2 %attend_backward.2 = (bf16[3,1472,256]{2,1,0:T(8,128)(2,1)}, bf16[3,1472,256]{2,1,0:T(8,128)(2,1)}) custom-call(s32[4]{0:T(128)} %get-tuple-element.241.s_ref, f32[10,176,352]{2,1,0:T(8,128)} %image_masks.1.mask_ref, bf16[1472,3072]{1,0:T(8,128)(2,1)} %get-tuple-element.194.q_ref.k_ref.v_ref.refs_0_.refs_1_.refs_2_.refs_3_.refs_4_.refs_5_, ...), custom_call_target="tpu_custom_call" | custom-call | flops 20000000000 | bytes 10000000 | tf_op jit(solution)/shard_map/attend_backward/pallas_call | solution.py:233
  306.5 3.3 fusion.4
  309.8 6.6 %grad_send.8 = bf16[1024,768]{1,0:T(8,128)(2,1)} custom-call(s32[2]{0:T(128)} %get-tuple-element.221.c_ref, f32[1]{0:T(128)} %bitcast.5.f_ref, bf16[1472,1024]{1,0:T(8,128)(2,1)} %get-tuple-element.276.a_ref, bf16[3,1472,256]{2,1,0:T(8,128)(2,1)} %get-tuple-element.282.b_ref.refs_1_), custom_call_target="tpu_custom_call" | custom-call | flops 2315255808 | bytes 10000000 | tf_op jit(solution)/shard_map/grad_send/pallas_call | solution.py:705
  317.2 6.2 %grad_keep.7 = (bf16[2,4,64,1280]{3,2,1,0:T(8,128)(2,1)}, bf16[2,4,64,1280]{3,2,1,0:T(8,128)(2,1)}) custom-call(s32[2]{0:T(128)} %get-tuple-element.217.c_ref, f32[1]{0:T(128)} %bitcast.5.f_ref, bf16[1472,1024]{1,0:T(8,128)(2,1)} %attend_forward.1.a_ref, bf16[1472,1024]{1,0:T(8,128)(2,1)} %get-tuple-element.260.b_ref, bf16[1024,512]{1,0:T(8,128)(2,1)} %copy-done.10), custom_call_target="tpu_custom_call" | custom-call | flops 1543503872 | bytes 10000000 | tf_op jit(solution)/shard_map/grad_keep/pallas_call | solution.py:705
  324.5 7.1 %grad_keep.8 = (bf16[2,4,64,1280]{3,2,1,0:T(8,128)(2,1)}, bf16[2,4,64,1280]{3,2,1,0:T(8,128)(2,1)}) custom-call(s32[2]{0:T(128)} %get-tuple-element.217.c_ref, f32[1]{0:T(128)} %bitcast.5.f_ref, bf16[1472,1024]{1,0:T(8,128)(2,1)} %get-tuple-element.276.a_ref, ...), custom_call_target="tpu_custom_call", output_to_operand_aliasing={{0}: (5, {}), {1}: (6, {})} | custom-call | flops 2315255808 | bytes 10000000 | tf_op jit(solution)/shard_map/grad_keep/pallas_call | solution.py:705
  335.4 20.0 %attend_backward.3 = (bf16[3,1472,256]{2,1,0:T(8,128)(2,1)}, bf16[3,1472,256]{2,1,0:T(8,128)(2,1)}) custom-call(s32[4]{0:T(128)} %get-tuple-element.219.s_ref, f32[10,176,352]{2,1,0:T(8,128)} %image_masks.1.mask_ref, bf16[1472,3072]{1,0:T(8,128)(2,1)} %get-tuple-element.194.q_ref.k_ref.v_ref.refs_0_.refs_1_.refs_2_.refs_3_.refs_4_.refs_5_, ...), custom_call_target="tpu_custom_call" | custom-call | flops 20000000000 | bytes 10000000 | tf_op jit(solution)/shard_map/attend_backward/pallas_call | solution.py:233
  355.5 3.7 reduce-scatter.6.cloned.1.call-done
  360.8 6.7 %grad_send.9 = bf16[1024,768]{1,0:T(8,128)(2,1)} custom-call(s32[2]{0:T(128)} %get-tuple-element.221.c_ref, f32[1]{0:T(128)} %bitcast.5.f_ref, bf16[1472,1024]{1,0:T(8,128)(2,1)} %get-tuple-element.276.a_ref, bf16[3,1472,256]{2,1,0:T(8,128)(2,1)} %get-tuple-element.284.b_ref.refs_3_), custom_call_target="tpu_custom_call" | custom-call | flops 2315255808 | bytes 10000000 | tf_op jit(solution)/shard_map/grad_send/pallas_call | solution.py:705
  371.2 7.1 %grad_keep.9 = (bf16[2,4,64,768]{3,2,1,0:T(8,128)(2,1)}, bf16[2,4,64,768]{3,2,1,0:T(8,128)(2,1)}) custom-call(s32[2]{0:T(128)} %get-tuple-element.217.c_ref, f32[1]{0:T(128)} %bitcast.5.f_ref, bf16[1472,1024]{1,0:T(8,128)(2,1)} %get-tuple-element.276.a_ref, bf16[3,1472,256]{2,1,0:T(8,128)(2,1)} %get-tuple-element.283.b_ref.refs_2_, ...), custom_call_target="tpu_custom_call" | custom-call | flops 2315255808 | bytes 10000000 | tf_op jit(solution)/shard_map/grad_keep/pallas_call | solution.py:705
  381.4 23.0 %first_back.1 = (bf16[1450,1024]{1,0:T(8,128)(2,1)}, f32[128,1024]{1,0:T(8,128)}, f32[8,1024]{1,0:T(8,128)}) custom-call(s32[4]{0:T(128)} %add_add_fusion.1.s_ref, bf16[3,1472,256]{2,1,0:T(8,128)(2,1)} %get-tuple-element.281.b_ref.refs_0_, bf16[3,1472,256]{2,1,0:T(8,128)(2,1)} %get-tuple-element.282.b_ref.refs_1_, ...), custom_call_target="tpu_custom_call" | custom-call | flops 9261023232 | bytes 40000000 | tf_op jit(solution)/shard_map/first_back/pallas_call | solution.py:600
  409.4 5.0 %collective-permute-done.33 = bf16[4,64,768]{2,1,0:T(8,128)(2,1)S(1)} collective-permute-done((bf16[4,64,768]{2,1,0:T(8,128)(2,1)S(1)}, bf16[4,64,768]{2,1,0:T(8,128)(2,1)S(1)}, u32[]{:S(2)}, u32[]{:S(2)}) %collective-permute-start.33) | collective-permute-done | bytes 393248 | tf_op jit(solution)/shard_map/ppermute | solution.py:722
  418.5 19.0 %return_layer.1 = bf16[1450,1024]{1,0:T(8,128)(2,1)} custom-call(bf16[1472,4096]{1,0:T(8,128)(2,1)} %get-tuple-element.298.a_ref, bf16[4096,1024]{1,0:T(8,128)(2,1)} %get-tuple-element.299.w_ref, f32[1472,1024]{1,0:T(8,128)} %get-tuple-element.239.mid_ref, f32[64,1024]{1,0:T(8,128)} %get-tuple-element.169.vec_ref.b_ref.gain_ref.refs_19_), custom_call_target="tpu_custom_call" | custom-call | flops 12348030976 | bytes 30000000 | tf_op jit(solution)/shard_map/return_layer/pallas_call | solution.py:507
  437.8 13.1 %all-gather.1 = bf16[512,1016]{1,0:T(8,128)(2,1)S(1)} all-gather(bf16[64,1016]{1,0:T(8,128)(2,1)S(1)} %pad_maximum_fusion.7), channel_id=3, replica_groups=mesh['dp'=8,'fsdp'=4] {'dp'}, dimensions={0}, use_global_device_ids=true | all-gather | bytes 1170432 | tf_op jit(solution)/shard_map/all_gather | solution.py:856
  453.0 7.8 %widen.1 = (f32[1024,1024]{1,0:T(8,128)}, f32[256,4096]{1,0:T(8,128)}, f32[256,3072]{1,0:T(8,128)}, f32[256,1024]{1,0:T(8,128)}) custom-call(bf16[4,2,64,5376]{3,2,1,0:T(8,128)(2,1)} %bitcast.94, bf16[4,2,64,1016]{3,2,1,0:T(8,128)(2,1)} %bitcast.96), custom_call_target="tpu_custom_call" | custom-call | flops 1 | bytes 6000000 | tf_op jit(solution)/shard_map/widen/pallas_call | solution.py:631
  (203 shorter events, 89.1 us)
Async XLA Ops:
  7.2 64.7 %all-gather.6.cloned.1.call-start = ((), (), s32[]{:S(2)}) async-start(), calls=%async_computation.6 | async-start | bytes 1310720 | tf_op jit(solution)/shard_map/all_gather | solution.py:752
  9.0 18.8 %collective-permute-start.2 = (bf16[32,3584]{1,0:T(8,128)(2,1)}, bf16[32,3584]{1,0:T(8,128)(2,1)S(1)}, u32[]{:S(2)}, u32[]{:S(2)}) collective-permute-start(bf16[32,3584]{1,0:T(8,128)(2,1)} %pack.1.refs_0_), channel_id=1, source_target_pairs={{3,0},{0,1},{1,2},{2,3},{7,4},{4,5},{5,6},{6,7},{11,8},{8,9},{9,10... | collective-permute-start | bytes 688136 | tf_op jit(solution)/shard_map/ppermute | solution.py:746
  12.0 17.8 %collective-permute-start.1 = (bf16[32,3584]{1,0:T(8,128)(2,1)}, bf16[32,3584]{1,0:T(8,128)(2,1)S(1)}, u32[]{:S(2)}, u32[]{:S(2)}) collective-permute-start(bf16[32,3584]{1,0:T(8,128)(2,1)} %pack.1.refs_0_), channel_id=1, source_target_pairs={{2,0},{3,1},{0,2},{1,3},{6,4},{7,5},{4,6},{5,7},{10,8},{11,9},{8,1... | collective-permute-start | bytes 688136 | tf_op jit(solution)/shard_map/ppermute | solution.py:746
  14.6 15.2 %collective-permute-start = (bf16[32,3584]{1,0:T(8,128)(2,1)}, bf16[32,3584]{1,0:T(8,128)(2,1)S(1)}, u32[]{:S(2)}, u32[]{:S(2)}) collective-permute-start(bf16[32,3584]{1,0:T(8,128)(2,1)} %pack.1.refs_0_), channel_id=1, source_target_pairs={{1,0},{2,1},{3,2},{0,3},{5,4},{6,5},{7,6},{4,7},{9,8},{10,9},{11,1... | collective-permute-start | bytes 688136 | tf_op jit(solution)/shard_map/ppermute | solution.py:746
  34.4 271.1 %reduce-scatter.4.cloned.1.call-start = ((), (), s32[]{:S(2)}) async-start(), calls=%async_computation.3 | async-start | bytes 1310720 | tf_op jit(solution)/shard_map/reduce_scatter | solution.py:877
  44.1 16.5 %collective-permute-start.7 = (bf16[2,3,32,3072]{3,2,1,0:T(8,128)(2,1)}, bf16[2,3,32,3072]{3,2,1,0:T(8,128)(2,1)}, u32[]{:S(2)}, u32[]{:S(2)}) collective-permute-start(bf16[2,3,32,3072]{3,2,1,0:T(8,128)(2,1)} %pad_maximum_fusion.2.refs_1_), channel_id=1, source_target_pairs={{0,16},{4,12},{8,24},{12,4},{16,0},{20,28},{24,8},{28,20},{1,17},{... | collective-permute-start | bytes 3538952 | tf_op jit(solution)/shard_map/ppermute | solution.py:722
  46.5 14.2 %collective-permute-start.6 = (bf16[32,1024]{1,0:T(8,128)(2,1)S(1)}, bf16[32,1024]{1,0:T(8,128)(2,1)S(1)}, u32[]{:S(2)}, u32[]{:S(2)}) collective-permute-start(bf16[32,1024]{1,0:T(8,128)(2,1)S(1)} %constant_dynamic-slice_fusion.1), channel_id=1, source_target_pairs={{3,0},{0,1},{1,2},{2,3},{7,4},{4,5},{5,6},{6,7},{11,8},{8,9},{9,10... | collective-permute-start | bytes 196616 | tf_op jit(solution)/shard_map/ppermute | solution.py:746
  56.5 20.5 %collective-permute-start.8 = (bf16[2,3,32,3072]{3,2,1,0:T(8,128)(2,1)}, bf16[2,3,32,3072]{3,2,1,0:T(8,128)(2,1)}, u32[]{:S(2)}, u32[]{:S(2)}) collective-permute-start(bf16[2,3,32,3072]{3,2,1,0:T(8,128)(2,1)} %pad_maximum_fusion.2.refs_1_), channel_id=1, source_target_pairs={{0,4},{4,0},{8,12},{12,8},{16,20},{20,16},{24,28},{28,24},{1,5},{5... | collective-permute-start | bytes 3538952 | tf_op jit(solution)/shard_map/ppermute | solution.py:722
  60.7 16.4 %collective-permute-start.9 = (bf16[2,3,32,3072]{3,2,1,0:T(8,128)(2,1)}, bf16[2,3,32,3072]{3,2,1,0:T(8,128)(2,1)}, u32[]{:S(2)}, u32[]{:S(2)}) collective-permute-start(bf16[2,3,32,3072]{3,2,1,0:T(8,128)(2,1)} %collective-permute-done.7.refs_2_), channel_id=1, source_target_pairs={{0,4},{4,0},{8,12},{12,8},{16,20},{20,16},{24,28},{28,24},{1,5},{5... | collective-permute-start | bytes 3538952 | tf_op jit(solution)/shard_map/ppermute | solution.py:722
  73.7 19.7 %collective-permute-start.11 = (bf16[3,32,5120]{2,1,0:T(8,128)(2,1)S(1)}, bf16[3,32,5120]{2,1,0:T(8,128)(2,1)S(1)}, u32[]{:S(2)}, u32[]{:S(2)}) collective-permute-start(bf16[3,32,5120]{2,1,0:T(8,128)(2,1)S(1)} %pad_maximum_fusion.4), channel_id=1, source_target_pairs={{0,8},{4,20},{8,0},{12,28},{16,24},{20,4},{24,16},{28,12},{1,9},{5... | collective-permute-start | bytes 2949128 | tf_op jit(solution)/shard_map/ppermute | solution.py:722
  75.8 17.6 %collective-permute-start.10 = (bf16[128,1024]{1,0:T(8,128)(2,1)S(1)}, bf16[128,1024]{1,0:T(8,128)(2,1)S(1)}, u32[]{:S(2)}, u32[]{:S(2)}) collective-permute-start(bf16[128,1024]{1,0:T(8,128)(2,1)S(1)} %constant_dynamic-slice_fusion), channel_id=1, source_target_pairs={{1,0},{2,1},{3,2},{0,3},{5,4},{6,5},{7,6},{4,7},{9,8},{10,9},{11,1... | collective-permute-start | bytes 786440 | tf_op jit(solution)/shard_map/ppermute | solution.py:746
  94.9 24.9 %collective-permute-start.12 = (bf16[2,3,32,5120]{3,2,1,0:T(8,128)(2,1)}, bf16[2,3,32,5120]{3,2,1,0:T(8,128)(2,1)}, u32[]{:S(2)}, u32[]{:S(2)}) collective-permute-start(bf16[2,3,32,5120]{3,2,1,0:T(8,128)(2,1)} %pad_maximum_fusion.refs_1_), channel_id=1, source_target_pairs={{0,16},{4,12},{8,24},{12,4},{16,0},{20,28},{24,8},{28,20},{1,17},{... | collective-permute-start | bytes 5898248 | tf_op jit(solution)/shard_map/ppermute | solution.py:722
  96.3 21.1 %collective-permute-start.14 = (bf16[128,1024]{1,0:T(8,128)(2,1)S(1)}, bf16[128,1024]{1,0:T(8,128)(2,1)S(1)}, u32[]{:S(2)}, u32[]{:S(2)}) collective-permute-start(bf16[128,1024]{1,0:T(8,128)(2,1)S(1)} %constant_dynamic-slice_fusion), channel_id=1, source_target_pairs={{3,0},{0,1},{1,2},{2,3},{7,4},{4,5},{5,6},{6,7},{11,8},{8,9},{9,10... | collective-permute-start | bytes 786440 | tf_op jit(solution)/shard_map/ppermute | solution.py:746
  97.1 20.4 %collective-permute-start.13 = (bf16[128,1024]{1,0:T(8,128)(2,1)S(1)}, bf16[128,1024]{1,0:T(8,128)(2,1)S(1)}, u32[]{:S(2)}, u32[]{:S(2)}) collective-permute-start(bf16[128,1024]{1,0:T(8,128)(2,1)S(1)} %constant_dynamic-slice_fusion), channel_id=1, source_target_pairs={{2,0},{3,1},{0,2},{1,3},{6,4},{7,5},{4,6},{5,7},{10,8},{11,9},{8,1... | collective-permute-start | bytes 786440 | tf_op jit(solution)/shard_map/ppermute | solution.py:746
  120.4 18.9 %collective-permute-start.17 = (bf16[3,128,1024]{2,1,0:T(8,128)(2,1)S(1)}, bf16[3,128,1024]{2,1,0:T(8,128)(2,1)}, u32[]{:S(2)}, u32[]{:S(2)}) collective-permute-start(bf16[3,128,1024]{2,1,0:T(8,128)(2,1)S(1)} %pad_maximum_fusion.5), channel_id=1, source_target_pairs={{0,8},{4,20},{8,0},{12,28},{16,24},{20,4},{24,16},{28,12},{1,9},{5... | collective-permute-start | bytes 2359304 | tf_op jit(solution)/shard_map/ppermute | solution.py:722
  140.6 30.8 %collective-permute-start.18 = (bf16[2,3,128,1024]{3,2,1,0:T(8,128)(2,1)S(1)}, bf16[2,3,128,1024]{3,2,1,0:T(8,128)(2,1)}, u32[]{:S(2)}, u32[]{:S(2)}) collective-permute-start(bf16[2,3,128,1024]{3,2,1,0:T(8,128)(2,1)S(1)} %pad_maximum_fusion.1.refs_1_), channel_id=1, source_target_pairs={{0,16},{4,12},{8,24},{12,4},{16,0},{20,28},{24,8},{28,20},{1,17},{... | collective-permute-start | bytes 4718600 | tf_op jit(solution)/shard_map/ppermute | solution.py:722
  171.5 12.4 %collective-permute-start.19 = (bf16[2,3,128,1024]{3,2,1,0:T(8,128)(2,1)S(1)}, bf16[2,3,128,1024]{3,2,1,0:T(8,128)(2,1)}, u32[]{:S(2)}, u32[]{:S(2)}) collective-permute-start(bf16[2,3,128,1024]{3,2,1,0:T(8,128)(2,1)S(1)} %pad_maximum_fusion.1.refs_1_), channel_id=1, source_target_pairs={{0,4},{4,0},{8,12},{12,8},{16,20},{20,16},{24,28},{28,24},{1,5},{5... | collective-permute-start | bytes 4718600 | tf_op jit(solution)/shard_map/ppermute | solution.py:722
  183.8 22.8 %collective-permute-start.21 = (bf16[4096,512]{1,0:T(8,128)(2,1)}, bf16[4096,512]{1,0:T(8,128)(2,1)}, u32[]{:S(2)}, u32[]{:S(2)}) collective-permute-start(bf16[4096,512]{1,0:T(8,128)(2,1)} %grad_send.5), channel_id=1, source_target_pairs={{0,4},{4,0},{8,12},{12,8},{16,20},{20,16},{24,28},{28,24},{1,5},{5... | collective-permute-start | bytes 12582920 | tf_op jit(solution)/shard_map/ppermute | solution.py:722
  231.1 27.2 %collective-permute-start.22 = (bf16[1024,2048]{1,0:T(8,128)(2,1)}, bf16[1024,2048]{1,0:T(8,128)(2,1)}, u32[]{:S(2)}, u32[]{:S(2)}) collective-permute-start(bf16[1024,2048]{1,0:T(8,128)(2,1)} %grad_send.6), channel_id=1, source_target_pairs={{0,4},{4,0},{8,12},{12,8},{16,20},{20,16},{24,28},{28,24},{1,5},{5... | collective-permute-start | bytes 12582920 | tf_op jit(solution)/shard_map/ppermute | solution.py:722
  231.6 26.7 %collective-permute-start.23 = (bf16[2,4,256,512]{3,2,1,0:T(8,128)(2,1)}, bf16[2,4,256,512]{3,2,1,0:T(8,128)(2,1)}, u32[]{:S(2)}, u32[]{:S(2)}) collective-permute-start(bf16[2,4,256,512]{3,2,1,0:T(8,128)(2,1)} %get-tuple-element.234), channel_id=1, source_target_pairs={{0,8},{4,20},{8,0},{12,28},{16,24},{20,4},{24,16},{28,12},{1,9},{5... | collective-permute-start | bytes 6291464 | tf_op jit(solution)/shard_map/ppermute | solution.py:722
  261.4 15.0 %collective-permute-start.24 = (bf16[4,256,512]{2,1,0:T(8,128)(2,1)}, bf16[4,256,512]{2,1,0:T(8,128)(2,1)S(1)}, u32[]{:S(2)}, u32[]{:S(2)}) collective-permute-start(bf16[4,256,512]{2,1,0:T(8,128)(2,1)} %get-tuple-element.312), channel_id=1, source_target_pairs={{0,16},{4,12},{8,24},{12,4},{16,0},{20,28},{24,8},{28,20},{1,17},{... | collective-permute-start | bytes 3145736 | tf_op jit(solution)/shard_map/ppermute | solution.py:722
  277.7 81.4 %reduce-scatter.6.cloned.1.call-start = ((), (), s32[]{:S(2)}) async-start(), calls=%async_computation.4 | async-start | bytes 1310720 | tf_op jit(solution)/shard_map/reduce_scatter | solution.py:877
  277.8 27.8 %collective-permute-start.26 = (bf16[2,4,64,2048]{3,2,1,0:T(8,128)(2,1)}, bf16[2,4,64,2048]{3,2,1,0:T(8,128)(2,1)}, u32[]{:S(2)}, u32[]{:S(2)}) collective-permute-start(bf16[2,4,64,2048]{3,2,1,0:T(8,128)(2,1)} %get-tuple-element.253), channel_id=1, source_target_pairs={{0,8},{4,20},{8,0},{12,28},{16,24},{20,4},{24,16},{28,12},{1,9},{5... | collective-permute-start | bytes 6291464 | tf_op jit(solution)/shard_map/ppermute | solution.py:722
  285.3 20.3 %collective-permute-start.25 = (bf16[1024,512]{1,0:T(8,128)(2,1)}, bf16[1024,512]{1,0:T(8,128)(2,1)S(1)}, u32[]{:S(2)}, u32[]{:S(2)}) collective-permute-start(bf16[1024,512]{1,0:T(8,128)(2,1)} %grad_send.7), channel_id=1, source_target_pairs={{0,4},{4,0},{8,12},{12,8},{16,20},{20,16},{24,28},{28,24},{1,5},{5... | collective-permute-start | bytes 3145736 | tf_op jit(solution)/shard_map/ppermute | solution.py:722
  316.8 15.1 %collective-permute-start.28 = (bf16[4,64,2048]{2,1,0:T(8,128)(2,1)}, bf16[4,64,2048]{2,1,0:T(8,128)(2,1)}, u32[]{:S(2)}, u32[]{:S(2)}) collective-permute-start(bf16[4,64,2048]{2,1,0:T(8,128)(2,1)} %get-tuple-element.310), channel_id=1, source_target_pairs={{0,16},{4,12},{8,24},{12,4},{16,0},{20,28},{24,8},{28,20},{1,17},{... | collective-permute-start | bytes 3145736 | tf_op jit(solution)/shard_map/ppermute | solution.py:722
  334.7 69.8 %reduce-scatter.8.cloned.1.call-start = ((), (), s32[]{:S(2)}) async-start(), calls=%async_computation.5 | async-start | bytes 819200 | tf_op jit(solution)/shard_map/reduce_scatter | solution.py:877
  334.7 20.8 %collective-permute-start.29 = (bf16[2,4,64,1280]{3,2,1,0:T(8,128)(2,1)S(1)}, bf16[2,4,64,1280]{3,2,1,0:T(8,128)(2,1)}, u32[]{:S(2)}, u32[]{:S(2)}) collective-permute-start(bf16[2,4,64,1280]{3,2,1,0:T(8,128)(2,1)S(1)} %copy-done.9), channel_id=1, source_target_pairs={{0,8},{4,20},{8,0},{12,28},{16,24},{20,4},{24,16},{28,12},{1,9},{5... | collective-permute-start | bytes 3932168 | tf_op jit(solution)/shard_map/ppermute | solution.py:722
  379.7 73.3 %all-gather.8.cloned.1.call-start = ((), (), s32[]{:S(2)}) async-start(), calls=%async_computation.7 | async-start | bytes 6193152 | tf_op jit(solution)/shard_map/all_gather | solution.py:856
  379.8 24.6 %collective-permute-start.32 = (bf16[2,4,64,768]{3,2,1,0:T(8,128)(2,1)}, bf16[2,4,64,768]{3,2,1,0:T(8,128)(2,1)S(1)}, u32[]{:S(2)}, u32[]{:S(2)}) collective-permute-start(bf16[2,4,64,768]{3,2,1,0:T(8,128)(2,1)} %get-tuple-element.280), channel_id=1, source_target_pairs={{0,8},{4,20},{8,0},{12,28},{16,24},{20,4},{24,16},{28,12},{1,9},{5... | collective-permute-start | bytes 2359304 | tf_op jit(solution)/shard_map/ppermute | solution.py:722
  414.6 22.9 %collective-permute-start.34 = (bf16[64,1024]{1,0:T(8,128)(2,1)S(1)}, bf16[64,1024]{1,0:T(8,128)(2,1)S(1)}, u32[]{:S(2)}, u32[]{:S(2)}) collective-permute-start(bf16[64,1024]{1,0:T(8,128)(2,1)S(1)} %get-tuple-element.316), channel_id=1, source_target_pairs={{0,1},{1,2},{2,3},{3,0},{4,5},{5,6},{6,7},{7,4},{8,9},{9,10},{10,1... | collective-permute-start | bytes 393224 | tf_op jit(solution)/shard_map/ppermute | solution.py:889
  414.6 22.9 %collective-permute-start.35 = (bf16[64,1024]{1,0:T(8,128)(2,1)S(1)}, bf16[64,1024]{1,0:T(8,128)(2,1)S(1)}, u32[]{:S(2)}, u32[]{:S(2)}) collective-permute-start(bf16[64,1024]{1,0:T(8,128)(2,1)S(1)} %get-tuple-element.317), channel_id=1, source_target_pairs={{0,2},{1,3},{2,0},{3,1},{4,6},{5,7},{6,4},{7,5},{8,10},{9,11},{10,... | collective-permute-start | bytes 393224 | tf_op jit(solution)/shard_map/ppermute | solution.py:889
  416.0 21.5 %collective-permute-start.36 = (bf16[64,1024]{1,0:T(8,128)(2,1)S(1)}, bf16[64,1024]{1,0:T(8,128)(2,1)S(1)}, u32[]{:S(2)}, u32[]{:S(2)}) collective-permute-start(bf16[64,1024]{1,0:T(8,128)(2,1)S(1)} %get-tuple-element.318), channel_id=1, source_target_pairs={{0,3},{1,0},{2,1},{3,2},{4,7},{5,4},{6,5},{7,6},{8,11},{9,8},{10,9... | collective-permute-start | bytes 393224 | tf_op jit(solution)/shard_map/ppermute | solution.py:889
  (34 other events, 285.9 us)
Sparse Core Ops, SparseCore 0:
  34.6 37.2 all-gather.5
  277.8 24.9 reduce-scatter.3
  334.8 24.3 reduce-scatter.5
  379.8 20.8 reduce-scatter.7
  406.5 41.6 all-gather.7
